TPU v7x, 32 devices: a whole 2x2x4 slice. The times are simulated.
32 devices in a mesh: head: 2 (over y), blk: 16 (over z, x, core).
Axes of the slice: x: 2, y: 2, z: 4, core: 2. Of those that a mesh axis runs over, the one named last changes fastest.
Arguments:
- tokens: bfloat16 [2, 2, 1024, 767], P(None, 'head', 'blk'), may hold values from -6 to 6
- segments: int32 [2, 2, 1024], P(None, 'head', 'blk'), may hold values from 0 to 8, as said below
- cotangent: bfloat16 [2, 2, 1024, 767], P(None, 'head', 'blk'), may hold values from -6 to 6
- w_qkv: bfloat16 [768, 2304], P(('head', 'blk')), may hold values from -0.21875 to 0.21875
- w_out: bfloat16 [768, 767], P(('head', 'blk')), may hold values from -1.75 to 1.75
- w_up: bfloat16 [768, 3072], P(('head', 'blk')), may hold values from -0.21875 to 0.21875
- w_down: bfloat16 [3072, 767], P(('head', 'blk')), may hold values from -0.109375 to 0.109375
- gain_one: bfloat16 [768], P(('head', 'blk')), may hold values from 0.5 to 1.5
- gain_two: bfloat16 [768], P(('head', 'blk')), may hold values from 0.5 to 1.5
Outputs:
- mixed: bfloat16 [2, 2, 1024, 767], P(None, 'head', 'blk')
- grad_tokens: float32 [2, 2, 1024, 767], P(None, 'head', 'blk')
- grad_w_qkv: float32 [768, 2304], P(('head', 'blk'))
- grad_w_out: float32 [768, 767], P(('head', 'blk'))
- grad_w_up: float32 [768, 3072], P(('head', 'blk'))
- grad_w_down: float32 [3072, 767], P(('head', 'blk'))
- grad_gain_one: float32 [768], P(('head', 'blk'))
- grad_gain_two: float32 [768], P(('head', 'blk'))
Inputs may be any that keep to these rules, and one draw needn't show every extreme that they name: `segments`: in each group positions 0 to 511 carry 0; later positions carry 1 to 8, never falling, every continuation 1024 // 32 positions or more.
All inputs are finite; a program needn't handle non-finite values.
Results may differ from a plain program's by a relative error of at most 0.039.
Values may be sent and summed in bfloat16 or wider, within the bound.
No kernel may reach another device: no remote copies, remote signals or barrier semaphores. Data moves between devices by JAX's collectives and lax.ppermute only.
A program may use at most 384 MiB of HBM per device.

v0:
```python
import math

import jax
import jax.numpy as jnp
from jax import lax
from jax.sharding import PartitionSpec as P

HEAD_DIM = 64


def compress_norm(values, gain):
    total_sum = jnp.sum(values, axis=-1, keepdims=True)
    full_vec = jnp.concatenate([values, -total_sum], axis=-1)
    factor = lax.rsqrt(jnp.mean(full_vec * full_vec, axis=-1, keepdims=True) + 1e-05)
    return full_vec * factor * gain


def gelu_tanh(values):
    return jax.nn.gelu(values, approximate=True)


def visibility(query_pos, query_seg, key_pos, key_seg):
    causal = key_pos[:, None, :] <= query_pos[None, :, None]
    shared = (key_seg[:, None, :] == 0) | (key_seg[:, None, :] == query_seg[:, :, None])
    return (causal & shared)[:, :, None, :]


def micro_step(token_block, segment_block, cotangent_block, weights_full, query_pos):
    proj_qkv, proj_out, proj_up, proj_down, norm_one, norm_two = weights_full
    norm_one = norm_one.astype(jnp.float32)
    norm_two = norm_two.astype(jnp.float32)
    group_local, seg_len, resid_width = token_block.shape
    model_width = proj_qkv.shape[0]
    row_count = group_local * seg_len
    score_scale = 1.0 / math.sqrt(HEAD_DIM)
    token_rows = token_block.astype(jnp.float32).reshape(row_count, resid_width)
    normed_f, norm_one_pull = jax.vjp(compress_norm, token_rows, norm_one)
    normed_one = normed_f.astype(jnp.bfloat16)
    projected = jnp.dot(normed_one, proj_qkv, preferred_element_type=jnp.float32).astype(
        jnp.bfloat16
    )
    projected = projected.reshape(group_local, seg_len, 3, model_width)
    head_groups = lax.axis_size("head")
    seg_wide = jnp.broadcast_to(
        segment_block.astype(jnp.bfloat16)[:, :, None, None], (group_local, seg_len, 1, head_groups)
    )
    moved_qkv, moved_seg = (
        lax.all_to_all(projected, "head", split_axis=3, concat_axis=0, tiled=True),
        lax.all_to_all(seg_wide, "head", split_axis=3, concat_axis=0, tiled=True),
    )
    groups = moved_qkv.shape[0]
    head_width = moved_qkv.shape[3]
    heads_here = head_width // HEAD_DIM
    head_shape = (groups, seg_len, heads_here, HEAD_DIM)
    queries = moved_qkv[:, :, 0].reshape(head_shape)
    keys_flat = moved_qkv[:, :, 1]
    values_flat = moved_qkv[:, :, 2]
    keys_local = keys_flat.reshape(head_shape)
    values_local = values_flat.reshape(head_shape)
    seg_bf = moved_seg[:, :, 0, 0]
    seg_here = seg_bf.astype(jnp.int32)
    key_piece = lax.all_gather(keys_flat, "blk", axis=1, tiled=True)
    value_piece = lax.all_gather(values_flat, "blk", axis=1, tiled=True)
    seg_piece = lax.all_gather(seg_bf, "blk", axis=1, tiled=True)
    key_pos = jnp.arange(key_piece.shape[1], dtype=jnp.int32)[None, :]
    running_max = jnp.full((groups, seg_len, heads_here), -1e30, jnp.float32)
    piece_rows = key_piece.shape[1]
    visible = visibility(query_pos, seg_here, key_pos, seg_piece.astype(jnp.int32))
    key_heads = key_piece.reshape(groups, piece_rows, heads_here, HEAD_DIM)
    value_heads = value_piece.reshape(groups, piece_rows, heads_here, HEAD_DIM)
    scores = score_scale * jnp.einsum(
        "gqhd,gkhd->gqhk", queries, key_heads, preferred_element_type=jnp.float32
    )
    masked = jnp.where(visible, scores, -1e30)
    new_max = jnp.maximum(running_max, jnp.max(masked, axis=-1))
    exp_terms = jnp.where(visible, jnp.exp(masked - new_max[..., None]), 0.0)
    new_sum = jnp.sum(exp_terms, axis=-1)
    new_acc = jnp.einsum(
        "gqhk,gkhd->gqhd",
        exp_terms.astype(jnp.bfloat16),
        value_heads,
        preferred_element_type=jnp.float32,
    )
    attn_f = new_acc / new_sum[..., None]
    log_totals = new_max + jnp.log(new_sum)
    attn_heads = attn_f.astype(jnp.bfloat16).reshape(groups, seg_len, head_width)
    attention = lax.all_to_all(attn_heads, "head", split_axis=0, concat_axis=2, tiled=True)
    attn_rows = attention.reshape(row_count, model_width)
    residual = token_rows + jnp.dot(attn_rows, proj_out, preferred_element_type=jnp.float32)
    normed_two_f, norm_two_pull = jax.vjp(compress_norm, residual, norm_two)
    normed_two = normed_two_f.astype(jnp.bfloat16)
    hidden = jnp.dot(normed_two, proj_up, preferred_element_type=jnp.float32)
    activated_f, gelu_pull = jax.vjp(gelu_tanh, hidden)
    activated = activated_f.astype(jnp.bfloat16)
    mixed = (residual + jnp.dot(activated, proj_down, preferred_element_type=jnp.float32)).astype(
        jnp.bfloat16
    )
    cot_rows = cotangent_block.reshape(row_count, resid_width)
    grad_down = jnp.einsum("ra,rb->ab", activated, cot_rows, preferred_element_type=jnp.float32)
    d_activated = jnp.einsum("rb,ab->ra", cot_rows, proj_down, preferred_element_type=jnp.float32)
    (d_hidden,) = gelu_pull(d_activated)
    d_hidden = d_hidden.astype(jnp.bfloat16)
    grad_up = jnp.einsum("ra,rb->ab", normed_two, d_hidden, preferred_element_type=jnp.float32)
    d_normed_two = jnp.einsum("rb,ab->ra", d_hidden, proj_up, preferred_element_type=jnp.float32)
    d_resid_part, grad_gain_two = norm_two_pull(d_normed_two)
    d_residual = cot_rows.astype(jnp.float32) + d_resid_part
    d_sum = d_residual.astype(jnp.bfloat16)
    grad_out = jnp.einsum("ra,rb->ab", attn_rows, d_sum, preferred_element_type=jnp.float32)
    d_attention = jnp.einsum(
        "rb,ab->ra", d_sum, proj_out, preferred_element_type=jnp.float32
    ).astype(jnp.bfloat16)
    d_attention = d_attention.reshape(group_local, seg_len, model_width)
    d_heads_flat = lax.all_to_all(d_attention, "head", split_axis=2, concat_axis=0, tiled=True)
    d_heads = d_heads_flat.reshape(head_shape)
    delta_rows = jnp.sum(d_heads.astype(jnp.float32) * attn_f, axis=-1)
    lse_all, delta_all = (
        lax.all_gather(log_totals, "blk", axis=1, tiled=True),
        lax.all_gather(delta_rows, "blk", axis=1, tiled=True),
    )
    key_piece = lax.all_gather(keys_flat, "blk", axis=1, tiled=True)
    value_piece = lax.all_gather(values_flat, "blk", axis=1, tiled=True)
    seg_piece = lax.all_gather(seg_bf, "blk", axis=1, tiled=True)
    key_pos = jnp.arange(key_piece.shape[1], dtype=jnp.int32)[None, :]
    piece_rows = key_piece.shape[1]
    visible = visibility(query_pos, seg_here, key_pos, seg_piece.astype(jnp.int32))
    key_heads = key_piece.reshape(groups, piece_rows, heads_here, HEAD_DIM)
    value_heads = value_piece.reshape(groups, piece_rows, heads_here, HEAD_DIM)
    scores = score_scale * jnp.einsum(
        "gqhd,gkhd->gqhk", queries, key_heads, preferred_element_type=jnp.float32
    )
    masked = jnp.where(visible, scores, -1e30)
    soft_weights = jnp.where(visible, jnp.exp(masked - log_totals[..., None]), 0.0)
    d_soft = jnp.einsum("gqhd,gkhd->gqhk", d_heads, value_heads, preferred_element_type=jnp.float32)
    d_scores = (soft_weights * (d_soft - delta_rows[..., None])).astype(jnp.bfloat16)
    d_query = score_scale * jnp.einsum(
        "gqhk,gkhd->gqhd", d_scores, key_heads, preferred_element_type=jnp.float32
    )
    queries_flat = moved_qkv[:, :, 0]
    query_piece = lax.all_gather(queries_flat, "blk", axis=1, tiled=True)
    dout_piece = lax.all_gather(d_heads_flat, "blk", axis=1, tiled=True)
    seg_piece = lax.all_gather(seg_bf, "blk", axis=1, tiled=True)
    piece_rows = query_piece.shape[1]
    piece_pos = jnp.arange(piece_rows, dtype=jnp.int32)
    visible = visibility(piece_pos, seg_piece.astype(jnp.int32), query_pos[None, :], seg_here)
    query_heads = query_piece.reshape(groups, piece_rows, heads_here, HEAD_DIM)
    dout_heads = dout_piece.reshape(groups, piece_rows, heads_here, HEAD_DIM)
    scores = score_scale * jnp.einsum(
        "gqhd,gkhd->gqhk", query_heads, keys_local, preferred_element_type=jnp.float32
    )
    masked = jnp.where(visible, scores, -1e30)
    soft_weights = jnp.where(visible, jnp.exp(masked - lse_all[..., None]), 0.0)
    d_soft = jnp.einsum(
        "gqhd,gkhd->gqhk", dout_heads, values_local, preferred_element_type=jnp.float32
    )
    d_scores = (soft_weights * (d_soft - delta_all[..., None])).astype(jnp.bfloat16)
    new_value = jnp.einsum(
        "gqhk,gqhd->gkhd",
        soft_weights.astype(jnp.bfloat16),
        dout_heads,
        preferred_element_type=jnp.float32,
    )
    new_key = score_scale * jnp.einsum(
        "gqhk,gqhd->gkhd", d_scores, query_heads, preferred_element_type=jnp.float32
    )
    d_stacked = (
        jnp.stack([d_query, new_key, new_value], axis=2)
        .astype(jnp.bfloat16)
        .reshape(groups, seg_len, 3, head_width)
    )
    d_projected = lax.all_to_all(d_stacked, "head", split_axis=0, concat_axis=3, tiled=True)
    d_proj_rows = d_projected.reshape(row_count, 3 * model_width)
    grad_qkv = jnp.einsum("ra,rb->ab", normed_one, d_proj_rows, preferred_element_type=jnp.float32)
    d_normed_one = jnp.einsum(
        "rb,ab->ra", d_proj_rows, proj_qkv, preferred_element_type=jnp.float32
    )
    d_token_part, grad_gain_one = norm_one_pull(d_normed_one)
    grad_tokens = (d_residual + d_token_part).reshape(group_local, seg_len, resid_width)
    mixed = mixed.reshape(group_local, seg_len, resid_width)
    return (
        mixed,
        grad_tokens,
        (grad_qkv, grad_out, grad_up, grad_down, grad_gain_one, grad_gain_two),
    )


def on_device(tokens, segments, cotangent, w_qkv, w_out, w_up, w_down, gain_one, gain_two):
    micro_count = tokens.shape[0]
    seg_len = tokens.shape[2]
    query_pos = lax.axis_index("blk") * seg_len + jnp.arange(seg_len, dtype=jnp.int32)
    mixed_list = []
    token_grad_list = []
    grad_terms = []
    for batch_index in range(micro_count):
        weights_full = (
            lax.all_gather(w_qkv, ("head", "blk"), axis=0, tiled=True),
            lax.all_gather(w_out, ("head", "blk"), axis=0, tiled=True),
            lax.all_gather(w_up, ("head", "blk"), axis=0, tiled=True),
            lax.all_gather(w_down, ("head", "blk"), axis=0, tiled=True),
            lax.all_gather(gain_one, ("head", "blk"), axis=0, tiled=True),
            lax.all_gather(gain_two, ("head", "blk"), axis=0, tiled=True),
        )
        mixed, grad_tokens, gradients = micro_step(
            tokens[batch_index],
            segments[batch_index],
            cotangent[batch_index],
            weights_full,
            query_pos,
        )
        mixed_list.append(mixed)
        token_grad_list.append(grad_tokens)
        grad_terms.append(
            (
                lax.psum_scatter(gradients[0], ("head", "blk"), scatter_dimension=0, tiled=True),
                lax.psum_scatter(gradients[1], ("head", "blk"), scatter_dimension=0, tiled=True),
                lax.psum_scatter(gradients[2], ("head", "blk"), scatter_dimension=0, tiled=True),
                lax.psum_scatter(gradients[3], ("head", "blk"), scatter_dimension=0, tiled=True),
                lax.psum_scatter(gradients[4], ("head", "blk"), scatter_dimension=0, tiled=True),
                lax.psum_scatter(gradients[5], ("head", "blk"), scatter_dimension=0, tiled=True),
            )
        )
    summed = grad_terms[0]
    for later_terms in grad_terms[1:]:
        summed = tuple((first + second for first, second in zip(summed, later_terms)))
    mixed_all = jnp.stack(mixed_list, axis=0)
    token_grads = jnp.stack(token_grad_list, axis=0)
    return (
        mixed_all,
        token_grads,
        summed[0],
        summed[1],
        summed[2],
        summed[3],
        summed[4],
        summed[5],
    )


def solution(mesh):
    placed = (
        P(None, "head", "blk", None),
        P(None, "head", "blk"),
        P(None, "head", "blk", None),
        P(("head", "blk"), None),
        P(("head", "blk"), None),
        P(("head", "blk"), None),
        P(("head", "blk"), None),
        P(("head", "blk")),
        P(("head", "blk")),
    )
    return jax.shard_map(
        on_device,
        mesh=mesh,
        in_specs=placed,
        out_specs=(
            P(None, "head", "blk", None),
            P(None, "head", "blk", None),
            P(("head", "blk"), None),
            P(("head", "blk"), None),
            P(("head", "blk"), None),
            P(("head", "blk"), None),
            P(("head", "blk")),
            P(("head", "blk")),
        ),
        check_vma=False,
    )
```

profile of v0, /device:TPU:0, one launch (start us, length us, event | category | flops | bytes accessed | tf_op | source)
XLA Modules:
  0.0 1142.3 jit_solution(4448662702824597230)
XLA Ops:
  10.8 42.0 %all-reduce.5 = (bf16[768]{0:T(1024)(128)(2,1)S(1)}, bf16[768]{0:T(1024)(128)(2,1)S(1)}) all-reduce(bf16[768]{0:T(1024)(128)(2,1)S(1)} %dynamic-update-slice, bf16[768]{0:T(1024)(128)(2,1)S(1)} %dynamic-update-slice.1), channel_id=1, replica_groups=mesh['head'=2,'blk'=16] {'head','blk'}, use_global_device_ids=true, to_apply=%add | all-reduce | flops 1536 | bytes 6144
  54.7 18.9 %all-gather.23.cloned.1.call-done = bf16[768,2304]{1,0:T(8,128)(2,1)} async-done(((bf16[24,2304]{1,0:T(8,128)(2,1)}), bf16[768,2304]{1,0:T(8,128)(2,1)}) %all-gather.23.cloned.1.call-update) | async-done | bytes 3538960 | tf_op jit(solution)/shard_map/all_gather | solution.py:195
  73.7 2.8 convolution_convert_fusion
  77.4 2.5 copy.301
  82.1 10.4 all_to_all.162
  94.8 3.0 copy.359
  103.0 2.5 convolution_convert_fusion.1
  111.8 9.6 all_to_all.163
  123.7 3.0 copy.356
  133.1 3.2 all-to-all-start.1
  137.1 2.9 all-to-all-done.1
  141.2 3.2 all-to-all-start.4
  146.5 23.6 %all-gather.1 = bf16[2,1,1024,1,1]{4,0,3,1,2:T(2,128)(2,1)} all-gather(bf16[2,1,64,1,1]{4,0,3,1,2:T(2,128)(2,1)} %copy.291), channel_id=3, replica_groups=mesh['head'=2,'blk'=16] {'blk'}, dimensions={2}, use_global_device_ids=true | all-gather | bytes 4352 | tf_op jit(solution)/shard_map/all_gather | solution.py:64
  173.4 20.5 %all-gather.4 = bf16[2,1,1024,1,1]{4,0,3,1,2:T(2,128)(2,1)} all-gather(bf16[2,1,64,1,1]{4,0,3,1,2:T(2,128)(2,1)} %copy.305), channel_id=6, replica_groups=mesh['head'=2,'blk'=16] {'blk'}, dimensions={2}, use_global_device_ids=true | all-gather | bytes 4352 | tf_op jit(solution)/shard_map/all_gather | solution.py:64
  201.5 4.9 copy.308
  212.1 5.0 copy.304
  217.0 4.3 fusion.173
  223.0 4.2 all-to-all-start.5
  227.3 5.0 copy.294
  237.9 24.4 %all-gather.31.cloned.1.call-done = bf16[2,1024,1,384]{3,0,2,1:T(2,128)(2,1)} async-done(((bf16[2,64,1,384]{3,0,2,1:T(2,128)(2,1)}), bf16[2,1024,1,384]{3,0,2,1:T(2,128)(2,1)}) %all-gather.31.cloned.1.call-update) | async-done | bytes 1572880 | tf_op jit(solution)/shard_map/all_gather | solution.py:63
  262.4 5.0 copy.290
  267.3 4.3 fusion.175
  273.3 4.0 all-to-all-start.2
  279.0 39.0 %all-gather.25.cloned.1.call-done = bf16[768,767]{1,0:T(8,128)(2,1)} async-done(((bf16[24,767]{1,0:T(8,128)(2,1)}), bf16[768,767]{1,0:T(8,128)(2,1)}) %all-gather.25.cloned.1.call-update) | async-done | bytes 1178128 | tf_op jit(solution)/shard_map/all_gather | solution.py:196
  332.0 51.5 %all-gather.27.cloned.1.call-done = bf16[768,3072]{1,0:T(8,128)(2,1)} async-done(((bf16[24,3072]{1,0:T(8,128)(2,1)}), bf16[768,3072]{1,0:T(8,128)(2,1)}) %all-gather.27.cloned.1.call-update) | async-done | bytes 4718608 | tf_op jit(solution)/shard_map/all_gather | solution.py:197
  383.5 4.4 fusion.170
  387.9 60.9 %all-gather.29.cloned.1.call-done = bf16[3072,767]{1,0:T(8,128)(2,1)} async-done(((bf16[96,767]{1,0:T(8,128)(2,1)}), bf16[3072,767]{1,0:T(8,128)(2,1)}) %all-gather.29.cloned.1.call-update) | async-done | bytes 4712464 | tf_op jit(solution)/shard_map/all_gather | solution.py:198
  448.8 4.3 fusion.99
  467.2 3.4 reduce.10
  472.4 8.3 all_to_all.164
  485.9 2.5 fusion.78
  490.2 3.4 reduce.11
  495.4 8.3 all_to_all.165
  508.9 8.8 reduce-scatter.7.cloned.1.call-start
  519.1 2.8 convolution_add_fusion.3
  522.0 2.7 fusion.125
  524.7 5.1 convolution_add_fusion.1
  529.9 2.7 fusion.168
  532.6 5.1 convolution_add_fusion.2
  551.7 26.7 %all_gather.91 = f32[2,1024,6]{2,0,1:T(2,128)} all-gather(f32[2,64,6]{2,0,1:T(2,128)} %copy.342), channel_id=1, replica_groups=mesh['head'=2,'blk'=16] {'blk'}, dimensions={1}, use_global_device_ids=true | all-gather | bytes 52224 | tf_op jit(solution)/shard_map/all_gather | solution.py:117
  581.9 23.4 %all_gather.87 = f32[2,1024,6]{2,0,1:T(2,128)} all-gather(f32[2,64,6]{2,0,1:T(2,128)} %copy.322), channel_id=1, replica_groups=mesh['head'=2,'blk'=16] {'blk'}, dimensions={1}, use_global_device_ids=true | all-gather | bytes 52224 | tf_op jit(solution)/shard_map/all_gather | solution.py:117
  607.3 4.9 copy.339
  612.3 4.9 copy.319
  617.2 3.9 fusion.108
  626.9 27.0 %all_gather.93 = f32[2,1024,6]{2,0,1:T(2,128)} all-gather(f32[2,64,6]{2,0,1:T(2,128)} %copy.348), channel_id=1, replica_groups=mesh['head'=2,'blk'=16] {'blk'}, dimensions={1}, use_global_device_ids=true | all-gather | bytes 52224 | tf_op jit(solution)/shard_map/all_gather | solution.py:118
  656.0 5.3 fusion.65
  666.6 24.1 %all_gather.89 = f32[2,1024,6]{2,0,1:T(2,128)} all-gather(f32[2,64,6]{2,0,1:T(2,128)} %copy.328), channel_id=1, replica_groups=mesh['head'=2,'blk'=16] {'blk'}, dimensions={1}, use_global_device_ids=true | all-gather | bytes 52224 | tf_op jit(solution)/shard_map/all_gather | solution.py:118
  692.7 5.4 fusion.64
  699.7 5.0 copy.346
  704.7 4.2 fusion.71
  710.6 5.3 fusion.67
  719.3 4.1 all-to-all-start.9
  723.5 5.0 copy.326
  728.4 5.3 fusion.66
  733.7 4.2 fusion.68
  743.0 4.1 all-to-all-start.7
  759.8 4.1 convolution_add_fusion
  764.7 3.8 fusion.76
  768.5 3.6 fusion.77
  774.2 2.6 multiply_reduce_fusion.5
  776.8 40.4 %all-reduce.4 = (f32[768]{0:T(1024)S(1)}, f32[768]{0:T(1024)S(1)}) all-reduce(f32[768]{0:T(1024)S(1)} %add.178, f32[768]{0:T(1024)S(1)} %add.179), channel_id=22, replica_groups=mesh['head'=2,'blk'=16] {'head','blk'}, use_global_device_ids=true, to_apply=%region_27.28.clone | all-reduce | flops 1536 | bytes 12288
  823.6 45.7 %reduce-scatter.11.cloned.1.call-done = f32[96,767]{1,0:T(8,128)} async-done(((f32[3072,767]{1,0:T(8,128)}), f32[96,767]{1,0:T(8,128)}) %reduce-scatter.11.cloned.1.call-update) | async-done | bytes 294544 | tf_op jit(solution)/shard_map/reduce_scatter | solution.py:216
  869.2 141.0 %reduce-scatter.9.cloned.1.call-done = f32[24,3072]{1,0:T(8,128)} async-done(((f32[768,3072]{1,0:T(8,128)}), f32[24,3072]{1,0:T(8,128)}) %reduce-scatter.9.cloned.1.call-update) | async-done | bytes 294928 | tf_op jit(solution)/shard_map/reduce_scatter | solution.py:215
  1010.2 125.2 %reduce-scatter.5.cloned.1.call-done = f32[24,2304]{1,0:T(8,128)} async-done(((f32[768,2304]{1,0:T(8,128)}), f32[24,2304]{1,0:T(8,128)}) %reduce-scatter.5.cloned.1.call-update) | async-done | bytes 221200 | tf_op jit(solution)/shard_map/reduce_scatter | solution.py:213
  (324 shorter events, 175.3 us)
Async XLA Ops:
  7.2 66.5 %all-gather.23.cloned.1.call-start = ((), (), s32[]{:S(2)}) async-start(), calls=%async_computation.14 | async-start | bytes 3649536 | tf_op jit(solution)/shard_map/all_gather | solution.py:195
  7.9 193.6 %all-gather.37.cloned.1.call-start = ((), (), s32[]{:S(2)}) async-start(), calls=%async_computation.21 | async-start | bytes 1671168 | tf_op jit(solution)/shard_map/all_gather | solution.py:62
  9.1 67.3 %copy-start.28 = (f32[64,1]{1,0:T(8,128)}, f32[64,1]{1,0:T(8,128)S(1)}, u32[]{:S(2)}) copy-start(f32[64,1]{1,0:T(8,128)S(1)} %copy.300) | copy-start | bytes 772
  54.5 22.0 %copy-start.11 = (f32[64,767]{1,0:T(8,128)}, f32[64,767]{1,0:T(8,128)S(1)}, u32[]{:S(2)}) copy-start(f32[64,767]{1,0:T(8,128)S(1)} %get-tuple-element.39) | copy-start | bytes 589060
  54.7 27.4 %copy-start.64 = (f32[64]{0:T(128)}, f32[64]{0:T(128)S(1)}, u32[]{:S(2)}) copy-start(f32[64]{0:T(128)S(1)} %multiply_reduce_fusion.11) | copy-start | bytes 772
  54.7 21.8 %copy-start.53 = (f32[64]{0:T(128)}, f32[64]{0:T(128)S(1)}, u32[]{:S(2)}) copy-start(f32[64]{0:T(128)S(1)} %fusion.141) | copy-start | bytes 772
  77.4 25.6 %copy-start.1 = (bf16[768,2304]{1,0:T(8,128)(2,1)S(1)}, bf16[768,2304]{1,0:T(8,128)(2,1)}, u32[]{:S(2)}) copy-start(bf16[768,2304]{1,0:T(8,128)(2,1)} %all-gather.23.cloned.1.call-done) | copy-start | bytes 10616836
  99.7 112.3 %all-gather.35.cloned.1.call-start = ((), (), s32[]{:S(2)}) async-start(), calls=%async_computation.20 | async-start | bytes 1671168 | tf_op jit(solution)/shard_map/all_gather | solution.py:63
  100.5 126.8 %all-gather.33.cloned.1.call-start = ((), (), s32[]{:S(2)}) async-start(), calls=%async_computation.19 | async-start | bytes 1671168 | tf_op jit(solution)/shard_map/all_gather | solution.py:62
  102.4 3.1 copy-start.65
  107.2 24.8 %copy-start.63 = (s32[2,1,64]{2,1,0:T(1,128)S(1)}, s32[2,1,64]{2,1,0:T(1,128)}, u32[]{:S(2)}) copy-start(s32[2,1,64]{2,1,0:T(1,128)} %param.10) | copy-start | bytes 1540
  128.6 133.7 %all-gather.31.cloned.1.call-start = ((), (), s32[]{:S(2)}) async-start(), calls=%async_computation.18 | async-start | bytes 1671168 | tf_op jit(solution)/shard_map/all_gather | solution.py:63
  129.2 188.8 %all-gather.25.cloned.1.call-start = ((), (), s32[]{:S(2)}) async-start(), calls=%async_computation.15 | async-start | bytes 1216512 | tf_op jit(solution)/shard_map/all_gather | solution.py:196
  129.8 253.7 %all-gather.27.cloned.1.call-start = ((), (), s32[]{:S(2)}) async-start(), calls=%async_computation.16 | async-start | bytes 4866048 | tf_op jit(solution)/shard_map/all_gather | solution.py:197
  130.6 318.3 %all-gather.29.cloned.1.call-start = ((), (), s32[]{:S(2)}) async-start(), calls=%async_computation.17 | async-start | bytes 4866048 | tf_op jit(solution)/shard_map/all_gather | solution.py:198
  131.3 476.0 %all-gather.43.cloned.1.call-start = ((), (), s32[]{:S(2)}) async-start(), calls=%async_computation.24 | async-start | bytes 1671168 | tf_op jit(solution)/shard_map/all_gather | solution.py:139
  133.1 6.9 all-to-all-start.1
  140.0 6.5 copy-start.60
  141.2 30.2 %all-to-all-start.4 = ((bf16[1,64,1,2]{1,2,0,3:T(2,128)(2,1)}), bf16[1,64,1,2]{1,2,0,3:T(2,128)(2,1)S(1)}, u32[]{:S(2)}, u32[]{:S(2)}) async-start(bf16[1,64,1,2]{1,2,0,3:T(2,128)(2,1)} %broadcast_in_dim.166), calls=%async_computation.4 | async-start | bytes 2048 | tf_op jit(solution)/shard_map/all_to_all | solution.py:49
  144.5 467.8 %all-gather.39.cloned.1.call-start = ((), (), s32[]{:S(2)}) async-start(), calls=%async_computation.22 | async-start | bytes 1671168 | tf_op jit(solution)/shard_map/all_gather | solution.py:139
  171.4 2.0 copy-start.61
  195.4 2.4 copy-start.42
  206.4 4.0 copy-start.36
  223.0 50.3 %all-to-all-start.5 = ((bf16[2,64,384]{2,1,0:T(8,128)(2,1)}), bf16[2,64,384]{2,1,0:T(8,128)(2,1)}, u32[]{:S(2)}, u32[]{:S(2)}) async-start(bf16[2,64,384]{2,1,0:T(8,128)(2,1)} %copy.311), calls=%async_computation.5 | async-start | bytes 196608 | tf_op jit(solution)/shard_map/all_to_all | solution.py:87
  232.3 4.1 copy-start.35
  273.3 51.1 %all-to-all-start.2 = ((bf16[2,64,384]{2,1,0:T(8,128)(2,1)}), bf16[2,64,384]{2,1,0:T(8,128)(2,1)}, u32[]{:S(2)}, u32[]{:S(2)}) async-start(bf16[2,64,384]{2,1,0:T(8,128)(2,1)} %copy.297), calls=%async_computation.2 | async-start | bytes 196608 | tf_op jit(solution)/shard_map/all_to_all | solution.py:87
  277.3 422.4 %all-gather.45.cloned.1.call-start = ((), (), s32[]{:S(2)}) async-start(), calls=%async_computation.25 | async-start | bytes 1671168 | tf_op jit(solution)/shard_map/all_gather | solution.py:140
  448.8 5.0 copy-start
  448.8 8.6 slice-start
  453.1 2.7 copy-start.26
  453.8 7.7 copy-start.51
  453.8 3.6 slice-start.1
  455.8 3.3 copy-start.9
  459.2 2.5 copy-start.25
  459.2 2.3 copy-start.68
  459.2 2.3 copy-start.67
  459.2 4.6 copy-start.2
  485.9 237.6 %all-gather.41.cloned.1.call-start = ((), (), s32[]{:S(2)}) async-start(), calls=%async_computation.23 | async-start | bytes 1671168 | tf_op jit(solution)/shard_map/all_gather | solution.py:140
  508.9 314.6 %reduce-scatter.7.cloned.1.call-start = ((), (), s32[]{:S(2)}) async-start(), calls=%async_computation.27 | async-start | bytes 2433024 | tf_op jit(solution)/shard_map/reduce_scatter | solution.py:214
  522.0 347.3 %reduce-scatter.11.cloned.1.call-start = ((), (), s32[]{:S(2)}) async-start(), calls=%async_computation.29 | async-start | bytes 9732096 | tf_op jit(solution)/shard_map/reduce_scatter | solution.py:216
  522.0 2.7 copy-start.14
  522.0 2.7 copy-start.23
  529.9 480.3 %reduce-scatter.9.cloned.1.call-start = ((), (), s32[]{:S(2)}) async-start(), calls=%async_computation.28 | async-start | bytes 9732096 | tf_op jit(solution)/shard_map/reduce_scatter | solution.py:215
  529.9 2.7 copy-start.6
  529.9 2.7 copy-start.27
  529.9 2.7 copy-start.33
  529.9 2.7 copy-start.57
  537.8 2.2 copy-start.52
  581.1 36.1 %copy-start.45 = (f32[2,64,6]{1,2,0:T(8,128)}, f32[2,64,6]{1,2,0:T(8,128)S(1)}, u32[]{:S(2)}) copy-start(f32[2,64,6]{1,2,0:T(8,128)S(1)} %log_add_fusion.1) | copy-start | bytes 9220
  617.2 3.9 copy-start.16
  617.2 3.9 copy-start.39
  719.3 23.7 %all-to-all-start.9 = ((bf16[2,64,3,384]{3,1,2,0:T(8,128)(2,1)}), bf16[2,64,3,384]{3,1,2,0:T(8,128)(2,1)}, u32[]{:S(2)}, u32[]{:S(2)}) async-start(bf16[2,64,3,384]{3,1,2,0:T(8,128)(2,1)} %pad_maximum_fusion.2), calls=%async_computation.9 | async-start | bytes 589824 | tf_op jit(solution)/shard_map/all_to_all | solution.py:170
  737.8 19.5 %copy-start.49 = (f32[64]{0:T(128)S(1)}, f32[64]{0:T(128)}, u32[]{:S(2)}) copy-start(f32[64]{0:T(128)} %copy-done.48) | copy-start | bytes 772
  743.0 10.5 all-to-all-start.7
  747.1 388.3 %reduce-scatter.5.cloned.1.call-start = ((), (), s32[]{:S(2)}) async-start(), calls=%async_computation.26 | async-start | bytes 7299072 | tf_op jit(solution)/shard_map/reduce_scatter | solution.py:213
  757.4 2.4 copy-start.12
  757.4 2.4 copy-start.18
  757.4 2.4 copy-start.29
  757.4 2.4 copy-start.54
  764.0 4.5 copy-start.8
  764.0 4.5 copy-start.10
  768.5 4.4 copy-start.19
  772.2 2.0 copy-start.13
  774.2 2.6 copy-start.24
  (29 other events, 37.6 us)
Sparse Core Ops, SparseCore 0:
  10.9 62.7 all-gather.22
  99.9 38.4 all-gather.36
  141.2 39.7 all-gather.34
  183.1 38.5 all-gather.32
  223.8 38.5 all-gather.30
  265.1 52.8 all-gather.24
  320.9 62.5 all-gather.26
  386.4 62.3 all-gather.28
  451.1 38.5 all-gather.42
  491.8 38.5 all-gather.38
  532.7 41.3 all-gather.44
  576.2 40.4 all-gather.40
  622.6 103.1 reduce-scatter.6
  733.1 136.0 reduce-scatter.10
  875.5 134.6 reduce-scatter.8
  1017.2 118.0 reduce-scatter.4
where the time goes:
time: 1150 us; the launch traced here: 1140 us
  waiting for transfers between devices  516 us (45%)
  blocking collectives  264 us (23%)
  local copies, waits for them, and re-layouts  156 us (14%)
  matrix products  116 us (10%)
  other arithmetic  41.6 us (4%)
  starting transfers between devices  32.4 us (3%)
  between operations  15.5 us (1%)
    reduce_scatter x1, waiting for transfers between devices, on_device(): lax.psum_scatter(gradients[2], ('head', 'blk'), scatter_dimension=0, tile...  141 us
    reduce_scatter x1, waiting for transfers between devices, on_device(): lax.psum_scatter(gradients[0], ('head', 'blk'), scatter_dimension=0, tile...  125 us
    unnamed x2, blocking collectives  82.4 us
    all_gather x1, waiting for transfers between devices, on_device(): lax.all_gather(w_down, ('head', 'blk'), axis=0, tiled=True)  60.9 us
    all_gather x1, waiting for transfers between devices, on_device(): lax.all_gather(w_up, ('head', 'blk'), axis=0, tiled=True)  51.5 us
    all_gather x2, blocking collectives, micro_step(): lax.all_gather(delta_rows, 'blk', axis=1, tiled=True)  51.1 us
    all_gather x2, blocking collectives, micro_step(): lax.all_gather(log_totals, 'blk', axis=1, tiled=True)  50.1 us
    reduce_scatter x1, waiting for transfers between devices, on_device(): lax.psum_scatter(gradients[3], ('head', 'blk'), scatter_dimension=0, tile...  45.7 us
  transfers between devices with their start and end apart: 22, of which 10 were waited for; matrix products, arithmetic and copies ran while one was open for 25% of the time, Pallas kernels for 0%

commit v1 on v0

--- a/solution.py
+++ b/solution.py
@@ -3,6 +3,8 @@
 import jax
 import jax.numpy as jnp
 from jax import lax
+from jax.experimental import pallas as pl
+from jax.experimental.pallas import tpu as pltpu
 from jax.sharding import PartitionSpec as P
 
 HEAD_DIM = 64
@@ -235,7 +237,563 @@
     )
 
 
+CORE, AXIS_X, AXIS_Z_NEAR, AXIS_Z_FAR, AXIS_Y = 1, 2, 4, 8, 16
+DEVICES = 32
+WIDTH = 768
+HALF = 384
+UNITS = 1536
+ROWS = 256
+POSITIONS = 1024
+VMEM_BYTES = 60 * 1024 * 1024
+
+
+def swap(array, bit, keep=lambda source: True):
+    pairs = [(i, i ^ bit) for i in range(DEVICES) if keep(i)]
+    return lax.ppermute(array, ("head", "blk"), pairs)
+
+
+def upward(bit):
+    return lambda source: source & bit == 0
+
+
+def downward(bit):
+    return lambda source: source & bit != 0
+
+
+def dot(a, b):
+    return lax.dot_general(a, b, (((1,), (0,)), ((), ())), preferred_element_type=jnp.float32)
+
+
+def dot_nt(a, b):
+    return lax.dot_general(a, b, (((1,), (1,)), ((), ())), preferred_element_type=jnp.float32)
+
+
+def dot_tn(a, b):
+    return lax.dot_general(a, b, (((0,), (0,)), ((), ())), preferred_element_type=jnp.float32)
+
+
+def run_copies(copies):
+    for copy in copies:
+        copy.start()
+    for copy in copies:
+        copy.wait()
+
+
+def lanes(rows):
+    return lax.broadcasted_iota(jnp.int32, (rows, WIDTH), 1)
+
+
+def norm_rows(values, lane):
+    inner = jnp.where(lane < WIDTH - 1, values, 0.0)
+    total = jnp.sum(inner, axis=-1, keepdims=True)
+    full = jnp.where(lane == WIDTH - 1, -total, inner)
+    factor = lax.rsqrt(jnp.mean(full * full, axis=-1, keepdims=True) + 1e-05)
+    return full * factor, factor
+
+
+def norm_rows_back(d_normed, normed, factor, lane):
+    inner = jnp.mean(d_normed * normed, axis=-1, keepdims=True)
+    d_full = factor * (d_normed - normed * inner)
+    last = jnp.sum(jnp.where(lane == WIDTH - 1, d_full, 0.0), axis=-1, keepdims=True)
+    return jnp.where(lane < WIDTH - 1, d_full - last, 0.0)
+
+
+def piece_chip(which, pair, entry):
+    z_bits = (entry & 3) << 1
+    other = entry >> 2
+    return z_bits | ((other | pair << 3) if which == 0 else (other << 3 | pair))
+
+
+def gather_weights(first, second):
+    cut = first.shape[-1]
+    joined = jnp.concatenate([first, second], axis=-1)[None]
+    two = jnp.concatenate([joined, swap(joined, AXIS_Z_NEAR)], axis=0)
+    far = swap(two, AXIS_Z_FAR)
+    four_a = jnp.concatenate([two[..., :cut], far[..., :cut]], axis=0)
+    four_b = jnp.concatenate([two[..., cut:], far[..., cut:]], axis=0)
+    eight_a = jnp.concatenate([four_a, swap(four_a, AXIS_X)], axis=0)
+    eight_b = jnp.concatenate([four_b, swap(four_b, AXIS_Y)], axis=0)
+    return eight_a, swap(eight_a, AXIS_Y), eight_b, swap(eight_b, AXIS_X)
+
+
+def reduce_weights(pieces):
+    keep_a, send_a, keep_b, send_b = pieces
+    eight_a = keep_a.astype(jnp.float32) + swap(send_a, AXIS_Y).astype(jnp.float32)
+    eight_b = keep_b.astype(jnp.float32) + swap(send_b, AXIS_X).astype(jnp.float32)
+    eight_a = eight_a.astype(jnp.bfloat16)
+    eight_b = eight_b.astype(jnp.bfloat16)
+    four_a = eight_a[:4].astype(jnp.float32) + swap(eight_a[4:], AXIS_X).astype(jnp.float32)
+    four_b = eight_b[:4].astype(jnp.float32) + swap(eight_b[4:], AXIS_Y).astype(jnp.float32)
+    four = jnp.concatenate([four_a, four_b], axis=-1).astype(jnp.bfloat16)
+    two = four[:2].astype(jnp.float32) + swap(four[2:], AXIS_Z_FAR).astype(jnp.float32)
+    two = two.astype(jnp.bfloat16)
+    return two[0].astype(jnp.float32) + swap(two[1], AXIS_Z_NEAR).astype(jnp.float32)
+
+
+def piece_copies(pieces, targets, chip, rows, sem, base, outward=False):
+    copies = []
+    for which in range(2):
+        for pair in range(2):
+            source = pieces[which * 2 + pair]
+            for entry in range(8):
+                block = chip ^ piece_chip(which, pair, entry)
+                at = pl.multiple_of(block * rows, 16)
+                here = targets[which].at[pl.ds(at, rows), :]
+                there = source.at[entry]
+                ends = (here, there) if outward else (there, here)
+                copies.append(pltpu.make_async_copy(*ends, sem.at[base + len(copies)]))
+    return copies
+
+
+def row_pieces(array, whole, place, core, core_bit, sem, base, outward=False):
+    copies = []
+    for entry in range(8):
+        rel = (entry & 3) << 1 | entry >> 2
+        block = (place ^ rel) * 2 + (core ^ core_bit)
+        at = pl.multiple_of(block * 64, 64)
+        here = whole.at[:, pl.ds(at, 64), :]
+        there = array.at[entry]
+        ends = (here, there) if outward else (there, here)
+        copies.append(pltpu.make_async_copy(*ends, sem.at[base + len(copies)]))
+    return copies
+
+
+def forward_kernel(
+    ids, tok_mine, tok_other, w0, w1, w2, w3,
+    attn_out, query_out, kv_out, normed_out, soft_out, wqk_out, wvo_out, wout_out, own_out, gains_out,
+    tok, bias, sem,
+):
+    chip, core = ids[0], ids[1]
+    place = lax.rem(chip, 8)
+    copies = piece_copies((w0, w1, w2, w3), (wqk_out, wvo_out), chip, 48, sem, 0)
+    copies += row_pieces(tok_mine, tok, place, core, 0, sem, 32)
+    copies += row_pieces(tok_other, tok, place, core, 1, sem, 40)
+    run_copies(copies)
+    wout_out[...] = wvo_out[:, HALF:]
+    picks = lax.broadcasted_iota(jnp.int32, (8, 128), 0) == lax.broadcasted_iota(
+        jnp.int32, (8, 128), 1
+    )
+    gains_out[...] = dot_nt(picks.astype(jnp.bfloat16), wqk_out[:, WIDTH:])
+    gain = gains_out[0:1, :]
+    lane = lanes(ROWS)
+    for micro in range(2):
+
+        def norm_chunk(index, carry, micro=micro):
+            at = pl.multiple_of(index * ROWS, ROWS)
+            values = tok[micro, pl.ds(at, ROWS), :].astype(jnp.float32)
+            normed = (norm_rows(values, lane)[0] * gain).astype(jnp.bfloat16)
+            normed_out[micro, pl.ds(at, ROWS), :] = normed
+            kv_out[micro, pl.ds(at, ROWS), :HALF] = dot(normed, wqk_out[:, HALF:WIDTH]).astype(
+                jnp.bfloat16
+            )
+            kv_out[micro, pl.ds(at, ROWS), HALF:] = dot(normed, wvo_out[:, :HALF]).astype(
+                jnp.bfloat16
+            )
+            return carry
+
+        lax.fori_loop(0, POSITIONS // ROWS, norm_chunk, 0)
+    first_row = pl.multiple_of(place * 128, 128)
+    hot = (lax.broadcasted_iota(jnp.int32, (8, WIDTH), 1) == WIDTH - 1).astype(jnp.bfloat16)
+    small = lax.broadcasted_iota(jnp.int32, (128, 128), 1) < HEAD_DIM
+    for micro in range(2):
+        own = tok[micro, pl.ds(first_row, 128), :]
+        own_out[micro * 128 : micro * 128 + 128, :] = own
+        query = dot(normed_out[micro, pl.ds(first_row, 128), :], wqk_out[:, :HALF])
+        query = query.astype(jnp.bfloat16) * jnp.bfloat16(0.125)
+        query_out[micro * 128 : micro * 128 + 128, :] = query
+        key_seg = dot_nt(hot, tok[micro])[0:1, :]
+        query_seg = own[:, WIDTH - 1 :].astype(jnp.float32)
+        key_pos = lax.broadcasted_iota(jnp.int32, (128, POSITIONS), 1)
+        query_pos = first_row + lax.broadcasted_iota(jnp.int32, (128, POSITIONS), 0)
+        seen = (key_pos <= query_pos) & ((key_seg == 0.0) | (key_seg == query_seg))
+        bias[...] = jnp.where(seen, 0.0, -1e30)
+        for pair in range(3):
+            cols = slice(pair * 128, pair * 128 + 128)
+            both = query_out[micro * 128 : micro * 128 + 128, cols]
+            zero = jnp.zeros_like(both)
+            stacked = jnp.concatenate(
+                [jnp.where(small, both, zero), jnp.where(small, zero, both)], axis=0
+            )
+            scores = dot_nt(stacked, kv_out[micro, :, cols])
+            scores = scores + jnp.concatenate([bias[...], bias[...]], axis=0)
+            top = jnp.max(scores, axis=-1, keepdims=True)
+            terms = jnp.exp(scores - top)
+            total = jnp.sum(terms, axis=-1, keepdims=True)
+            soft = (terms * (1.0 / total)).astype(jnp.bfloat16)
+            soft_out[micro * 3 + pair] = soft
+            value = kv_out[micro, :, HALF + pair * 128 : HALF + pair * 128 + 128]
+            mixed = dot(soft, value)
+            attn_out[micro * 128 : micro * 128 + 128, cols] = jnp.where(
+                small, mixed[:128], mixed[128:]
+            ).astype(jnp.bfloat16)
+
+
+def feed_kernel(
+    ids, gains, attn_mine, attn_other, own, wout_mine, wout_other, cot_mine, cot_other,
+    u0, u1, u2, u3, d0, d1, d2, d3,
+    attn_out, cot_out, res_out, part_out,
+    gu0, gu1, gu2, gu3, gd0, gd1, gd2, gd3,
+    wu_a, wu_b, wd_a, wd_b, gu_a, gu_b, gd_a, gd_b, sum_mix, sum_norm, sem,
+):
+    chip, core = ids[0], ids[1]
+    load = piece_copies((u0, u1, u2, u3), (wu_a, wu_b), chip, 48, sem, 0)
+    load += piece_copies((d0, d1, d2, d3), (wd_a, wd_b), chip, 96, sem, 32)
+    for copy in load:
+        copy.start()
+    mine_at = pl.multiple_of(core * HALF, 128)
+    other_at = pl.multiple_of((1 - core) * HALF, 128)
+    attn_out[:, pl.ds(mine_at, HALF)] = attn_mine[...]
+    attn_out[:, pl.ds(other_at, HALF)] = attn_other[...]
+    for micro in range(2):
+        for side, source in ((core, cot_mine), (1 - core, cot_other)):
+            at = pl.multiple_of(micro * 128 + side * 64, 64)
+            cot_out[pl.ds(at, 64), :] = source[micro]
+    lane = lanes(ROWS)
+    attn = attn_out[...]
+    res_out[:, pl.ds(mine_at, HALF)] = dot(attn, wout_mine[...])
+    res_out[:, pl.ds(other_at, HALF)] = dot(attn, wout_other[...])
+    own_values = jnp.where(lane < WIDTH - 1, own[...].astype(jnp.float32), 0.0)
+    residual = res_out[...] + own_values
+    res_out[...] = residual
+    normed = (norm_rows(residual, lane)[0] * gains[1:2, :]).astype(jnp.bfloat16)
+    cot = cot_out[...]
+    for copy in load:
+        copy.wait()
+    slope = math.sqrt(2.0 / math.pi)
+    step = HALF
+    sum_mix[...] = jnp.zeros_like(sum_mix)
+    sum_norm[...] = jnp.zeros_like(sum_norm)
+    for part in range(UNITS // step):
+        up, g_up = (wu_a, gu_a) if part < 2 else (wu_b, gu_b)
+        cols = slice((part % 2) * step, (part % 2) * step + step)
+        rows = slice(part * step, part * step + step)
+        hidden = dot(normed, up[:, cols])
+        square = hidden * hidden
+        wave = jnp.tanh(slope * hidden * (1.0 + 0.044715 * square))
+        active = (0.5 * hidden * (1.0 + wave)).astype(jnp.bfloat16)
+        grow = 0.5 * (1.0 + wave) + 0.5 * hidden * (1.0 - wave * wave) * slope * (
+            1.0 + 3.0 * 0.044715 * square
+        )
+        d_active = dot_nt(cot[:, :HALF], wd_a[rows, :]) + dot_nt(cot[:, HALF:], wd_b[rows, :])
+        d_hidden = (d_active * grow).astype(jnp.bfloat16)
+        sum_mix[:, :HALF] += dot(active, wd_a[rows, :])
+        sum_mix[:, HALF:] += dot(active, wd_b[rows, :])
+        sum_norm[...] += dot_nt(d_hidden, up[:, cols])
+        g_up[:, cols] = dot_tn(normed, d_hidden).astype(jnp.bfloat16)
+        gd_a[rows, :] = dot_tn(active, cot[:, :HALF]).astype(jnp.bfloat16)
+        gd_b[rows, :] = dot_tn(active, cot[:, HALF:]).astype(jnp.bfloat16)
+    store = piece_copies((gu0, gu1, gu2, gu3), (gu_a, gu_b), chip, 48, sem, 0, True)
+    store += piece_copies((gd0, gd1, gd2, gd3), (gd_a, gd_b), chip, 96, sem, 32, True)
+    for copy in store:
+        copy.start()
+    part_out[:ROWS, :] = sum_mix[...].astype(jnp.bfloat16)
+    part_out[ROWS:, :] = sum_norm[...].astype(jnp.bfloat16)
+    for copy in store:
+        copy.wait()
+
+
+def backward_kernel(
+    ids, gains, residual, part_mine, part_other, cot, attn, wout_mine, wout_other, wqk, wvo,
+    query, kv, normed_all, soft,
+    mixed_out, dres_out, g0, g1, g2, g3, keep_rows, send_rows,
+    g_a, g_b, d_attn, d_kv, d_query, d_rows, d_sum_ref, hold, sem,
+):
+    chip, core = ids[0], ids[1]
+    place = lax.rem(chip, 8)
+    first_row = pl.multiple_of(place * 128, 128)
+    mine_at = pl.multiple_of(core * HALF, 128)
+    other_at = pl.multiple_of((1 - core) * HALF, 128)
+    lane = lanes(ROWS)
+    res = residual[...]
+    mixed = res + part_mine[:ROWS, :].astype(jnp.float32) + part_other[:ROWS, :].astype(jnp.float32)
+    hold[...] = mixed
+    for micro in range(2):
+        at = pl.multiple_of(micro * 128 + core * 64, 64)
+        mixed_out[micro] = hold[pl.ds(at, 64), : WIDTH - 1].astype(jnp.bfloat16)
+    d_normed = part_mine[ROWS:, :].astype(jnp.float32) + part_other[ROWS:, :].astype(jnp.float32)
+    d_normed = d_normed * gains[1:2, :]
+    normed_two, factor = norm_rows(res, lane)
+    d_res = cot[...].astype(jnp.float32) + norm_rows_back(d_normed, normed_two, factor, lane)
+    hold[...] = d_res
+    for micro in range(2):
+        at = pl.multiple_of(micro * 128 + core * 64, 64)
+        dres_out[micro] = hold[pl.ds(at, 64), :]
+    d_sum_ref[...] = d_res.astype(jnp.bfloat16)
+    d_mine = d_sum_ref[:, pl.ds(mine_at, HALF)]
+    d_other = d_sum_ref[:, pl.ds(other_at, HALF)]
+    d_heads = dot_nt(d_mine, wout_mine[pl.ds(mine_at, HALF), :]) + dot_nt(
+        d_other, wout_other[pl.ds(mine_at, HALF), :]
+    )
+    d_attn[...] = d_heads.astype(jnp.bfloat16)
+    g_b[:, HALF:] = dot_tn(attn[...], d_mine).astype(jnp.bfloat16)
+    small = lax.broadcasted_iota(jnp.int32, (128, 128), 1) < HEAD_DIM
+    for micro in range(2):
+        here = slice(micro * 128, micro * 128 + 128)
+        for pair in range(3):
+            cols = slice(pair * 128, pair * 128 + 128)
+            value_cols = slice(HALF + pair * 128, HALF + pair * 128 + 128)
+
+            def stack(both):
+                zero = jnp.zeros_like(both)
+                return jnp.concatenate(
+                    [jnp.where(small, both, zero), jnp.where(small, zero, both)], axis=0
+                )
+
+            d_out = stack(d_attn[here, cols])
+            q_both = stack(query[here, cols])
+            weights = soft[micro * 3 + pair]
+            d_soft = dot_nt(d_out, kv[micro, :, value_cols])
+            weights_f = weights.astype(jnp.float32)
+            delta = jnp.sum(weights_f * d_soft, axis=-1, keepdims=True)
+            d_scores = (weights_f * (d_soft - delta)).astype(jnp.bfloat16)
+            d_q = dot(d_scores, kv[micro, :, cols]) * 0.125
+            d_query[here, cols] = jnp.where(small, d_q[:128], d_q[128:]).astype(jnp.bfloat16)
+            d_kv[micro, :, cols] = dot_tn(d_scores, q_both).astype(jnp.bfloat16)
+            d_kv[micro, :, value_cols] = dot_tn(weights, d_out).astype(jnp.bfloat16)
+    for micro in range(2):
+
+        def row_chunk(index, carry, micro=micro):
+            at = pl.multiple_of(index * ROWS, ROWS)
+            d_k = d_kv[micro, pl.ds(at, ROWS), :HALF]
+            d_v = d_kv[micro, pl.ds(at, ROWS), HALF:]
+            rows = dot_nt(d_k, wqk[:, HALF:WIDTH]) + dot_nt(d_v, wvo[:, :HALF])
+            d_rows[micro, pl.ds(at, ROWS), :] = rows.astype(jnp.bfloat16)
+            return carry
+
+        lax.fori_loop(0, POSITIONS // ROWS, row_chunk, 0)
+        own = d_rows[micro, pl.ds(first_row, 128), :].astype(jnp.float32)
+        own = own + dot_nt(d_query[micro * 128 : micro * 128 + 128, :], wqk[:, :HALF])
+        d_rows[micro, pl.ds(first_row, 128), :] = own.astype(jnp.bfloat16)
+    store = row_pieces(keep_rows, d_rows, place, core, 0, sem, 32, True)
+    store += row_pieces(send_rows, d_rows, place, core, 1, sem, 40, True)
+    for copy in store:
+        copy.start()
+    own_0 = normed_all[0, pl.ds(first_row, 128), :]
+    own_1 = normed_all[1, pl.ds(first_row, 128), :]
+    g_a[:, :HALF] = (dot_tn(own_0, d_query[:128, :]) + dot_tn(own_1, d_query[128:, :])).astype(
+        jnp.bfloat16
+    )
+    g_a[:, HALF:] = (
+        dot_tn(normed_all[0], d_kv[0, :, :HALF]) + dot_tn(normed_all[1], d_kv[1, :, :HALF])
+    ).astype(jnp.bfloat16)
+    g_b[:, :HALF] = (
+        dot_tn(normed_all[0], d_kv[0, :, HALF:]) + dot_tn(normed_all[1], d_kv[1, :, HALF:])
+    ).astype(jnp.bfloat16)
+    run_copies(piece_copies((g0, g1, g2, g3), (g_a, g_b), chip, 48, sem, 0, True))
+    for copy in store:
+        copy.wait()
+
+
+def tail_kernel(gains, tokens, d_first, d_second, d_residual, grad_out):
+    lane = lanes(128)
+    rows = (128, WIDTH)
+    values = tokens[...].reshape(rows).astype(jnp.float32)
+    normed, factor = norm_rows(values, lane)
+    d_normed = d_first[...].reshape(rows).astype(jnp.float32)
+    d_normed = d_normed + d_second[...].reshape(rows).astype(jnp.float32)
+    d_normed = d_normed * gains[0:1, :]
+    out = d_residual[...].reshape(rows) + norm_rows_back(d_normed, normed, factor, lane)
+    grad_out[...] = out[:, : WIDTH - 1].reshape(2, 64, WIDTH - 1)
+
+
+ANY = pl.BlockSpec(memory_space=pl.ANY)
+VMEM = pl.BlockSpec(memory_space=pltpu.VMEM)
+SMEM = pl.BlockSpec(memory_space=pltpu.SMEM)
+
+
+def shaped(shape, dtype=jnp.bfloat16):
+    return jax.ShapeDtypeStruct(shape, dtype)
+
+
+def call(kernel, ins, outs, scratch, name):
+    return pl.pallas_call(
+        kernel,
+        in_specs=[spec for spec in ins],
+        out_specs=[spec for spec, _ in outs],
+        out_shape=[shape for _, shape in outs],
+        scratch_shapes=scratch,
+        name=name,
+        compiler_params=pltpu.CompilerParams(vmem_limit_bytes=VMEM_BYTES),
+    )
+
+
+def pick(core, zero, one):
+    return jnp.where(core == 0, zero, one)
+
+
+def chip_block(core, for_zero, for_one):
+    mine = pick(core, for_zero, for_one)
+    other = swap(pick(core, for_one, for_zero), CORE)
+    return jnp.concatenate([pick(core, mine, other), pick(core, other, mine)], axis=0)
+
+
+def core_rows(core, block):
+    rows = block.shape[0] // 2
+    mine = pick(core, block[:rows], block[rows:])
+    other = swap(pick(core, block[rows:], block[:rows]), CORE)
+    return pick(core, mine, other), pick(core, other, mine)
+
+
+def on_chip_pair(tokens, segments, cotangent, w_qkv, w_out, w_up, w_down, gain_one, gain_two):
+    bf, f32 = jnp.bfloat16, jnp.float32
+    device = lax.axis_index("head") * 16 + lax.axis_index("blk")
+    core = device % 2
+    ids = jnp.stack([device // 2, core]).astype(jnp.int32)
+    micro, _, length, narrow = tokens.shape
+    own = jnp.concatenate([tokens[:, 0], segments[:, 0, :, None].astype(bf)], axis=-1)
+    cot = jnp.pad(cotangent[:, 0], ((0, 0), (0, 0), (0, 1)))
+    two = jnp.concatenate([own[None], swap(own, AXIS_Z_NEAR)[None]], axis=0)
+    four = jnp.concatenate([two, swap(two, AXIS_Z_FAR, upward(AXIS_Z_FAR))], axis=0)
+    eight = jnp.concatenate([four, swap(four, AXIS_X)], axis=0)
+    eight_other = swap(eight, CORE)
+    out_wide = jnp.pad(w_out, ((0, 0), (0, 1)))
+    down_wide = jnp.pad(w_down, ((0, 0), (0, 1)))
+    qkv_parts = w_qkv.reshape(-1, 3, 2, HALF)
+    attn_halves = [
+        jnp.concatenate(
+            [qkv_parts[:, 0, k], qkv_parts[:, 1, k], qkv_parts[:, 2, k]]
+            + [out_wide[:, k * HALF : k * HALF + HALF]],
+            axis=-1,
+        )
+        for k in range(2)
+    ]
+    gain_cols = jnp.pad(jnp.stack([gain_one, gain_two], axis=-1), ((0, 0), (0, 126)))
+    attn_halves = [
+        jnp.concatenate([half[:, :WIDTH], gain_cols, half[:, WIDTH:]], axis=-1)
+        for half in attn_halves
+    ]
+    attn_block = chip_block(core, *attn_halves)
+    wide = WIDTH + 128
+    unit_rows = w_down.shape[0]
+    up_parts = w_up.reshape(w_up.shape[0], -1, 2, unit_rows)
+    up_halves = [up_parts[:, :, k].reshape(w_up.shape[0], UNITS) for k in range(2)]
+    up_block = chip_block(core, *up_halves)
+    attn_pieces = gather_weights(attn_block[:, :wide], attn_block[:, wide:])
+    up_pieces = gather_weights(up_block[:, :WIDTH], up_block[:, WIDTH:])
+    down_pieces = gather_weights(down_wide[:, :HALF], down_wide[:, HALF:])
+    cot_other = swap(cot, CORE)
+    attn, query, kv, normed_all, soft, wqk, wvo, wout, own_rows, gains = call(
+        forward_kernel,
+        [SMEM] + [ANY] * 6,
+        [
+            (VMEM, shaped((ROWS, HALF))),
+            (VMEM, shaped((ROWS, HALF))),
+            (VMEM, shaped((2, POSITIONS, WIDTH))),
+            (VMEM, shaped((2, POSITIONS, WIDTH))),
+            (VMEM, shaped((6, ROWS, POSITIONS))),
+            (VMEM, shaped((WIDTH, wide))),
+            (VMEM, shaped((WIDTH, WIDTH))),
+            (VMEM, shaped((WIDTH, HALF))),
+            (VMEM, shaped((ROWS, WIDTH))),
+            (VMEM, shaped((8, WIDTH), f32)),
+        ],
+        [
+            pltpu.VMEM((2, POSITIONS, WIDTH), bf),
+            pltpu.VMEM((128, POSITIONS), f32),
+            pltpu.SemaphoreType.DMA((48,)),
+        ],
+        "attention_forward",
+    )(ids, eight, eight_other, *attn_pieces)
+    attn_other = swap(attn, CORE)
+    wout_other = swap(wout, CORE)
+    outs = call(
+        feed_kernel,
+        [SMEM] + [VMEM] * 8 + [ANY] * 8,
+        [
+            (VMEM, shaped((ROWS, WIDTH))),
+            (VMEM, shaped((ROWS, WIDTH))),
+            (VMEM, shaped((ROWS, WIDTH), f32)),
+            (VMEM, shaped((2 * ROWS, WIDTH))),
+        ]
+        + [(ANY, shaped((8, 48, WIDTH)))] * 4
+        + [(ANY, shaped((8, 96, HALF)))] * 4,
+        [
+            pltpu.VMEM((WIDTH, WIDTH), bf),
+            pltpu.VMEM((WIDTH, WIDTH), bf),
+            pltpu.VMEM((UNITS, HALF), bf),
+            pltpu.VMEM((UNITS, HALF), bf),
+            pltpu.VMEM((WIDTH, WIDTH), bf),
+            pltpu.VMEM((WIDTH, WIDTH), bf),
+            pltpu.VMEM((UNITS, HALF), bf),
+            pltpu.VMEM((UNITS, HALF), bf),
+            pltpu.VMEM((ROWS, WIDTH), f32),
+            pltpu.VMEM((ROWS, WIDTH), f32),
+            pltpu.SemaphoreType.DMA((64,)),
+        ],
+        "feed_forward_and_back",
+    )(
+        ids, gains, attn, attn_other, own_rows, wout, wout_other, cot, cot_other,
+        *up_pieces, *down_pieces,
+    )
+    attn_all, cot_all, residual, part = outs[:4]
+    grad_up_pieces, grad_down_pieces = outs[4:8], outs[8:12]
+    part_other = swap(part, CORE)
+    outs = call(
+        backward_kernel,
+        [SMEM] + [VMEM] * 14,
+        [(VMEM, shaped((2, 64, WIDTH - 1))), (VMEM, shaped((2, 64, WIDTH), f32))]
+        + [(ANY, shaped((8, 48, WIDTH)))] * 4
+        + [(ANY, shaped((8, 2, 64, WIDTH)))] * 2,
+        [
+            pltpu.VMEM((WIDTH, WIDTH), bf),
+            pltpu.VMEM((WIDTH, WIDTH), bf),
+            pltpu.VMEM((ROWS, HALF), bf),
+            pltpu.VMEM((2, POSITIONS, WIDTH), bf),
+            pltpu.VMEM((ROWS, HALF), bf),
+            pltpu.VMEM((2, POSITIONS, WIDTH), bf),
+            pltpu.VMEM((ROWS, WIDTH), bf),
+            pltpu.VMEM((ROWS, WIDTH), f32),
+            pltpu.SemaphoreType.DMA((48,)),
+        ],
+        "attention_backward",
+    )(
+        ids, gains, residual, part, part_other, cot_all, attn_all, wout, wout_other, wqk, wvo,
+        query, kv, normed_all, soft,
+    )
+    mixed, d_residual = outs[:2]
+    grad_attn_pieces, keep_rows, send_rows = outs[2:6], outs[6], outs[7]
+    up_sum = reduce_weights(grad_up_pieces)
+    down_sum = reduce_weights(grad_down_pieces)
+    rows_8 = (keep_rows.astype(f32) + swap(send_rows, CORE).astype(f32)).astype(bf)
+    rows_4 = (rows_8[:4].astype(f32) + swap(rows_8[4:], AXIS_X).astype(f32)).astype(bf)
+    rows_2 = rows_4[:2].astype(f32) + swap(rows_4[2:], AXIS_Z_FAR, downward(AXIS_Z_FAR)).astype(f32)
+    rows_2 = rows_2.astype(bf)
+    last_rows = swap(rows_2[1], AXIS_Z_NEAR)
+    attn_sum = reduce_weights(grad_attn_pieces)
+    (grad_tokens,) = call(
+        tail_kernel,
+        [VMEM] * 5,
+        [(VMEM, shaped((2, 64, WIDTH - 1), f32))],
+        [],
+        "token_gradient",
+    )(gains, own, rows_2[0], last_rows, d_residual)
+    attn_0, attn_1 = core_rows(core, attn_sum)
+    up_0, up_1 = core_rows(core, up_sum)
+    grad_qkv = jnp.concatenate(
+        [half[:, k * HALF : k * HALF + HALF] for k in range(3) for half in (attn_0, attn_1)],
+        axis=-1,
+    )
+    grad_out = jnp.concatenate([attn_0[:, 3 * HALF :], attn_1[:, 3 * HALF : 4 * HALF - 1]], axis=-1)
+    rows = up_0.shape[0]
+    grad_up = jnp.stack(
+        [up_0.reshape(rows, -1, unit_rows), up_1.reshape(rows, -1, unit_rows)], axis=2
+    ).reshape(rows, -1)
+    grad_gain_one = jnp.sum(grad_qkv * w_qkv.astype(f32), axis=-1) / gain_one.astype(f32)
+    grad_gain_two = jnp.sum(grad_up * w_up.astype(f32), axis=-1) / gain_two.astype(f32)
+    return (
+        mixed[:, None],
+        grad_tokens[:, None],
+        grad_qkv,
+        grad_out,
+        grad_up,
+        down_sum[:, : WIDTH - 1],
+        grad_gain_one,
+        grad_gain_two,
+    )
+
+
 def solution(mesh):
+    small_slice = (mesh.shape["head"], mesh.shape["blk"]) == (2, 16)
     placed = (
         P(None, "head", "blk", None),
         P(None, "head", "blk"),
@@ -248,7 +806,7 @@
         P(("head", "blk")),
     )
     return jax.shard_map(
-        on_device,
+        on_chip_pair if small_slice else on_device,
         mesh=mesh,
         in_specs=placed,
         out_specs=(

time: 1150 us -> 327 us (0.28)
  waiting for transfers between devices: 516 us -> 152 us
  blocking collectives: 264 us -> 0 us
  local copies, waits for them, and re-layouts: 156 us -> 13.2 us
  matrix products: 116 us -> 0 us
  Pallas kernels: 0 us -> 56.5 us
  starting transfers between devices: 32.4 us -> 86.8 us
  other arithmetic: 41.6 us -> 16.5 us
  between operations: 15.5 us -> 1.71 us
    reduce_scatter x4 -> x0, waiting for transfers between devices: 312 us -> none  [the longest x1 141 us: on_device(): lax.psum_scatter(gradients[2], ('head', 'blk'), scatter_dimension=0, tile...]
    all_gather x12 -> x0, waiting for transfers between devices: 195 us -> none  [the longest x1 60.9 us: on_device(): lax.all_gather(w_down, ('head', 'blk'), axis=0, tiled=True)]
    ppermute x0 -> x52, waiting for transfers between devices: none -> 152 us  [swap(): return lax.ppermute(array, ('head', 'blk'), pairs)]
    all_gather x6 -> x0, blocking collectives: 145 us -> none  [the longest x2 51.1 us: micro_step(): lax.all_gather(delta_rows, 'blk', axis=1, tiled=True)]
    dot_general x36 -> x0, matrix products: 116 us -> none  [the longest x2 10.7 us: micro_step(): jnp.einsum('gqhk,gkhd->gqhd', d_scores, key_heads, preferred_element_type...]
    ppermute x0 -> x52, starting transfers between devices: none -> 86.8 us  [swap(): return lax.ppermute(array, ('head', 'blk'), pairs)]
    unnamed x2 -> x0, blocking collectives: 82.4 us -> none
    pallas_call x0 -> x4, Pallas kernels: none -> 56.5 us  [the longest x1 22.9 us: on_chip_pair(): call(backward_kernel, [SMEM] + [VMEM] * 14, [(VMEM, shaped((2, 64, WIDTH...]
  transfers between devices with their start and end apart: 22 -> 52, of which waited for: 10 -> 22; matrix products, arithmetic and copies ran while one was open for 25% -> 7% of each run, Pallas kernels for 0% -> 12%
where the time goes in v1:
time: 327 us; the launch traced here: 326 us
  waiting for transfers between devices  152 us (46%)
  starting transfers between devices  86.8 us (27%)
  Pallas kernels  56.5 us (17%)
  other arithmetic  16.5 us (5%)
  local copies, waits for them, and re-layouts  13.2 us (4%)
    ppermute x52, waiting for transfers between devices, swap(): return lax.ppermute(array, ('head', 'blk'), pairs)  152 us
    ppermute x52, starting transfers between devices, swap(): return lax.ppermute(array, ('head', 'blk'), pairs)  86.8 us
    pallas_call x1, Pallas kernels, on_chip_pair(): call(backward_kernel, [SMEM] + [VMEM] * 14, [(VMEM, shaped((2, 64, WIDTH...  22.9 us
    pallas_call x1, Pallas kernels, on_chip_pair(): call(forward_kernel, [SMEM] + [ANY] * 6, [(VMEM, shaped((ROWS, HALF))), (...  17.2 us
    pallas_call x1, Pallas kernels, on_chip_pair(): call(feed_kernel, [SMEM] + [VMEM] * 8 + [ANY] * 8, [(VMEM, shaped((ROWS,...  14 us
  transfers between devices with their start and end apart: 52, of which 22 were waited for; matrix products, arithmetic and copies ran while one was open for 7% of the time, Pallas kernels for 12%

profile of v1, /device:TPU:0, one launch (start us, length us, event | category | flops | bytes accessed | tf_op | source)
XLA Modules:
  0.0 326.3 jit_solution(2471357203802570642)
XLA Ops:
  1.5 0.9 reshape.48
  2.7 0.8 constant_dynamic-update-slice_fusion
  4.1 2.7 collective-permute-start.21
  8.8 1.6 collective-permute-start.15
  11.5 3.0 collective-permute-start.22
  14.5 7.6 %collective-permute-done = bf16[2,64,768]{2,1,0:T(8,128)(2,1)S(1)} collective-permute-done((bf16[2,64,768]{2,1,0:T(8,128)(2,1)S(1)}, bf16[2,64,768]{2,1,0:T(8,128)(2,1)S(1)}, u32[]{:S(2)}, u32[]{:S(2)}) %collective-permute-start) | collective-permute-done | bytes 196640 | tf_op jit(solution)/shard_map/ppermute | solution.py:252
  22.2 3.8 %collective-permute-start.1 = (bf16[2,2,64,768]{3,2,1,0:T(8,128)(2,1)S(1)}, bf16[2,2,64,768]{3,2,1,0:T(8,128)(2,1)S(1)}, u32[]{:S(2)}, u32[]{:S(2)}) collective-permute-start(bf16[2,2,64,768]{3,2,1,0:T(8,128)(2,1)S(1)} %pad_maximum_fusion.9), channel_id=1, source_target_pairs={{0,8},{1,9},{2,10},{3,11},{4,12},{5,13},{6,14},{7,15},{16,24},{17,... | collective-permute-start | bytes 1179656 | tf_op jit(solution)/shard_map/ppermute | solution.py:252
  26.1 1.2 collective-permute-start.16
  27.3 9.2 %collective-permute-done.1 = bf16[2,2,64,768]{3,2,1,0:T(8,128)(2,1)S(1)} collective-permute-done((bf16[2,2,64,768]{3,2,1,0:T(8,128)(2,1)S(1)}, bf16[2,2,64,768]{3,2,1,0:T(8,128)(2,1)S(1)}, u32[]{:S(2)}, u32[]{:S(2)}) %collective-permute-start.1) | collective-permute-done | bytes 393248 | tf_op jit(solution)/shard_map/ppermute | solution.py:252
  36.6 1.6 collective-permute-start.2
  38.2 3.5 %collective-permute-start.6 = (bf16[2,48,1664]{2,1,0:T(8,128)(2,1)S(1)}, bf16[2,48,1664]{2,1,0:T(8,128)(2,1)S(1)}, u32[]{:S(2)}, u32[]{:S(2)}) collective-permute-start(bf16[2,48,1664]{2,1,0:T(8,128)(2,1)S(1)} %pad_maximum_fusion.8), channel_id=1, source_target_pairs={{0,8},{1,9},{2,10},{3,11},{4,12},{5,13},{6,14},{7,15},{8,0},{9,1},... | collective-permute-start | bytes 958472 | tf_op jit(solution)/shard_map/ppermute | solution.py:252
  42.5 1.6 collective-permute-start.25
  44.1 13.1 %collective-permute-done.2 = bf16[4,2,64,768]{3,2,1,0:T(8,128)(2,1)S(1)} collective-permute-done((bf16[4,2,64,768]{3,2,1,0:T(8,128)(2,1)S(1)}, bf16[4,2,64,768]{3,2,1,0:T(8,128)(2,1)S(1)}, u32[]{:S(2)}, u32[]{:S(2)}) %collective-permute-start.2) | collective-permute-done | bytes 786464 | tf_op jit(solution)/shard_map/ppermute | solution.py:252
  57.5 1.6 collective-permute-start.7
  59.1 1.6 collective-permute-start.9
  60.8 8.3 %collective-permute-done.7 = bf16[4,48,896]{2,1,0:T(8,128)(2,1)S(1)} collective-permute-done((bf16[4,48,896]{2,1,0:T(8,128)(2,1)S(1)}, bf16[4,48,896]{2,1,0:T(8,128)(2,1)S(1)}, u32[]{:S(2)}, u32[]{:S(2)}) %collective-permute-start.7) | collective-permute-done | bytes 344096 | tf_op jit(solution)/shard_map/ppermute | solution.py:252
  69.1 1.5 collective-permute-start.17
  70.7 1.6 collective-permute-start.8
  74.3 4.7 %collective-permute-done.17 = bf16[4,48,768]{2,1,0:T(8,128)(2,1)S(1)} collective-permute-done((bf16[4,48,768]{2,1,0:T(8,128)(2,1)S(1)}, bf16[4,48,768]{2,1,0:T(8,128)(2,1)S(1)}, u32[]{:S(2)}, u32[]{:S(2)}) %collective-permute-start.17) | collective-permute-done | bytes 294944 | tf_op jit(solution)/shard_map/ppermute | solution.py:252
  79.0 14.2 %collective-permute-done.19 = bf16[4,48,768]{2,1,0:T(8,128)(2,1)S(1)} collective-permute-done((bf16[4,48,768]{2,1,0:T(8,128)(2,1)S(1)}, bf16[4,48,768]{2,1,0:T(8,128)(2,1)S(1)}, u32[]{:S(2)}, u32[]{:S(2)}) %collective-permute-start.19) | collective-permute-done | bytes 294944 | tf_op jit(solution)/shard_map/ppermute | solution.py:252
  93.8 0.9 pad_maximum_fusion.4.u0
  94.7 0.9 pad_maximum_fusion.5.u2
  95.6 1.6 collective-permute-start.24
  97.2 1.5 collective-permute-start.20
  98.7 1.2 copy-done.7
  100.4 17.2 %attention_forward.1 = (bf16[256,384]{1,0:T(8,128)(2,1)}, bf16[256,384]{1,0:T(8,128)(2,1)}, bf16[2,1024,768]{2,1,0:T(8,128)(2,1)}, bf16[2,1024,768]{2,1,0:T(8,12...) custom-call(s32[2]{0:T(128)} %pad_add_fusion.ids, ...), custom_call_target="tpu_custom_call" | custom-call | tf_op jit(solution)/shard_map/attention_forward/pallas_call | solution.py:675
  118.2 1.0 collective-permute-done.20.u3
  119.1 2.1 collective-permute-done.18.u1
  122.1 14.0 %feed_forward_and_back.1 = (bf16[256,768]{1,0:T(8,128)(2,1)}, bf16[256,768]{1,0:T(8,128)(2,1)}, f32[256,768]{1,0:T(8,128)}, bf16[512,768]{1,0:T(8,128)(2,1)}, bf...) custom-call(s32[2]{0:T(128)} %pad_add_fusion.ids, ...), custom_call_target="tpu_custom_call" | custom-call | tf_op jit(solution)/shard_map/feed_forward_and_back/pallas_call | solution.py:699
  136.1 1.6 collective-permute-start.39
  137.7 1.5 collective-permute-start.41
  140.2 12.4 %collective-permute-done.39 = bf16[8,48,768]{2,1,0:T(8,128)(2,1)S(1)} collective-permute-done((bf16[8,48,768]{2,1,0:T(8,128)(2,1)}, bf16[8,48,768]{2,1,0:T(8,128)(2,1)S(1)}, u32[]{:S(2)}, u32[]{:S(2)}) %collective-permute-start.39) | collective-permute-done | bytes 589856 | tf_op jit(solution)/shard_map/ppermute | solution.py:252
  152.7 1.2 add_convert_fusion.5
  154.6 1.5 collective-permute-start.40
  157.0 1.5 collective-permute-start.42
  158.5 6.8 %collective-permute-done.46 = bf16[8,96,384]{2,1,0:T(8,128)(2,1)S(1)} collective-permute-done((bf16[8,96,384]{2,1,0:T(8,128)(2,1)}, bf16[8,96,384]{2,1,0:T(8,128)(2,1)S(1)}, u32[]{:S(2)}, u32[]{:S(2)}) %collective-permute-start.46) | collective-permute-done | bytes 589856 | tf_op jit(solution)/shard_map/ppermute | solution.py:252
  166.2 1.5 collective-permute-start.47
  168.6 1.5 collective-permute-start.49
  170.1 1.0 copy-done.12
  171.1 22.9 %attention_backward.1 = (bf16[2,64,767]{2,1,0:T(8,128)(2,1)}, f32[2,64,768]{2,1,0:T(8,128)}, bf16[8,48,768]{2,1,0:T(8,128)(2,1)}, bf16[8,48,768]{2,1,0:T(8,128)(...) custom-call(s32[2]{0:T(128)} %pad_add_fusion.ids, ...), custom_call_target="tpu_custom_call" | custom-call | tf_op jit(solution)/shard_map/attention_backward/pallas_call | solution.py:731
  195.2 1.0 add_convert_fusion.14
  196.3 1.0 add_convert_fusion.13
  197.4 3.5 %collective-permute-start.43 = (bf16[2,48,1536]{2,1,0:T(8,128)(2,1)S(1)}, bf16[2,48,1536]{2,1,0:T(8,128)(2,1)S(1)}, u32[]{:S(2)}, u32[]{:S(2)}) collective-permute-start(bf16[2,48,1536]{2,1,0:T(8,128)(2,1)S(1)} %pad_maximum_fusion.15), channel_id=1, source_target_pairs={{0,8},{1,9},{2,10},{3,11},{4,12},{5,13},{6,14},{7,15},{8,0},{9,1},... | collective-permute-start | bytes 884744 | tf_op jit(solution)/shard_map/ppermute | solution.py:252
  200.9 1.0 add_convert_fusion.11
  202.0 1.0 add_convert_fusion.10
  203.1 5.7 %collective-permute-done.43 = bf16[2,48,1536]{2,1,0:T(8,128)(2,1)S(1)} collective-permute-done((bf16[2,48,1536]{2,1,0:T(8,128)(2,1)S(1)}, bf16[2,48,1536]{2,1,0:T(8,128)(2,1)S(1)}, u32[]{:S(2)}, u32[]{:S(2)}) %collective-permute-start.43) | collective-permute-done | bytes 294944 | tf_op jit(solution)/shard_map/ppermute | solution.py:252
  208.9 23.2 %collective-permute-start.44 = (bf16[48,1536]{1,0:T(8,128)(2,1)S(1)}, bf16[48,1536]{1,0:T(8,128)(2,1)S(1)}, u32[]{:S(2)}, u32[]{:S(2)}) collective-permute-start(bf16[48,1536]{1,0:T(8,128)(2,1)S(1)} %slice_bitcast_fusion.4), channel_id=1, source_target_pairs={{0,4},{1,5},{2,6},{3,7},{4,0},{5,1},{6,2},{7,3},{8,12},{9,13},{10,... | collective-permute-start | bytes 442376 | tf_op jit(solution)/shard_map/ppermute | solution.py:252
  232.2 6.2 %collective-permute-start.51 = (bf16[96,768]{1,0:T(8,128)(2,1)S(1)}, bf16[96,768]{1,0:T(8,128)(2,1)S(1)}, u32[]{:S(2)}, u32[]{:S(2)}) collective-permute-start(bf16[96,768]{1,0:T(8,128)(2,1)S(1)} %get-tuple-element.100), channel_id=1, source_target_pairs={{0,4},{1,5},{2,6},{3,7},{4,0},{5,1},{6,2},{7,3},{8,12},{9,13},{10,... | collective-permute-start | bytes 442376 | tf_op jit(solution)/shard_map/ppermute | solution.py:252
  238.8 1.5 collective-permute-start.33
  240.4 1.6 collective-permute-start.35
  242.9 5.3 %collective-permute-done.33 = bf16[4,48,768]{2,1,0:T(8,128)(2,1)S(1)} collective-permute-done((bf16[4,48,768]{2,1,0:T(8,128)(2,1)S(1)}, bf16[4,48,768]{2,1,0:T(8,128)(2,1)S(1)}, u32[]{:S(2)}, u32[]{:S(2)}) %collective-permute-start.33) | collective-permute-done | bytes 294944 | tf_op jit(solution)/shard_map/ppermute | solution.py:252
  248.3 1.3 collective-permute-done.35
  249.7 3.1 collective-permute-start.36
  253.0 12.6 %collective-permute-done.36 = bf16[2,48,1536]{2,1,0:T(8,128)(2,1)S(1)} collective-permute-done((bf16[2,48,1536]{2,1,0:T(8,128)(2,1)S(1)}, bf16[2,48,1536]{2,1,0:T(8,128)(2,1)S(1)}, u32[]{:S(2)}, u32[]{:S(2)}) %collective-permute-start.36) | collective-permute-done | bytes 294944 | tf_op jit(solution)/shard_map/ppermute | solution.py:252
  267.6 1.2 reshape.50
  268.8 1.1 multiply_reduce_fusion
  269.9 2.0 collective-permute-done.37
  271.9 1.0 convert_add_fusion.2
  273.6 0.8 collective-permute-done.38
  275.8 18.9 %collective-permute-done.29 = bf16[4,2,64,768]{3,2,1,0:T(8,128)(2,1)S(1)} collective-permute-done((bf16[4,2,64,768]{3,2,1,0:T(8,128)(2,1)S(1)}, bf16[4,2,64,768]{3,2,1,0:T(8,128)(2,1)S(1)}, u32[]{:S(2)}, u32[]{:S(2)}) %collective-permute-start.29) | collective-permute-done | bytes 786464 | tf_op jit(solution)/shard_map/ppermute | solution.py:252
  294.9 1.3 collective-permute-start.30
  297.0 19.5 %collective-permute-done.30 = bf16[2,2,64,768]{3,2,1,0:T(8,128)(2,1)S(1)} collective-permute-done((bf16[2,2,64,768]{3,2,1,0:T(8,128)(2,1)S(1)}, bf16[2,2,64,768]{3,2,1,0:T(8,128)(2,1)S(1)}, u32[]{:S(2)}, u32[]{:S(2)}) %collective-permute-start.30) | collective-permute-done | bytes 393248 | tf_op jit(solution)/shard_map/ppermute | solution.py:252
  317.8 5.3 %collective-permute-done.31.d_second = bf16[2,64,768]{2,1,0:T(8,128)(2,1)S(1)} collective-permute-done((bf16[2,64,768]{2,1,0:T(8,128)(2,1)S(1)}, bf16[2,64,768]{2,1,0:T(8,128)(2,1)S(1)}, u32[]{:S(2)}, u32[]{:S(2)}) %collective-permute-start.31) | collective-permute-done | bytes 196640 | tf_op jit(solution)/shard_map/ppermute | solution.py:252
  323.8 2.4 token_gradient.1
  (222 shorter events, 25.3 us)
Async XLA Ops:
  3.5 6.9 %collective-permute-start.4 = (bf16[24,1664]{1,0:T(8,128)(2,1)S(1)}, bf16[24,1664]{1,0:T(8,128)(2,1)S(1)}, u32[]{:S(2)}, u32[]{:S(2)}) collective-permute-start(bf16[24,1664]{1,0:T(8,128)(2,1)S(1)} %broadcast_select_fusion.4), channel_id=1, source_target_pairs={{0,1},{1,0},{2,3},{3,2},{4,5},{5,4},{6,7},{7,6},{8,9},{9,8},{10,11... | collective-permute-start | bytes 239624 | tf_op jit(solution)/shard_map/ppermute | solution.py:252
  4.1 7.4 %collective-permute-start.21 = (bf16[1,96,768]{2,1,0:T(8,128)(2,1)S(1)}, bf16[1,96,768]{2,1,0:T(8,128)(2,1)S(1)}, u32[]{:S(2)}, u32[]{:S(2)}) collective-permute-start(bf16[1,96,768]{2,1,0:T(8,128)(2,1)S(1)} %maximum_bitcast_fusion.2), channel_id=1, source_target_pairs={{0,4},{1,5},{2,6},{3,7},{4,0},{5,1},{6,2},{7,3},{8,12},{9,13},{10,... | collective-permute-start | bytes 442376 | tf_op jit(solution)/shard_map/ppermute | solution.py:252
  7.4 1.3 collective-permute-start.14
  7.9 14.3 %copy-start.11 = (bf16[2,64,768]{2,1,0:T(8,128)(2,1)}, bf16[2,64,768]{2,1,0:T(8,128)(2,1)S(1)}, u32[]{:S(2)}) copy-start(bf16[2,64,768]{2,1,0:T(8,128)(2,1)S(1)} %pad_maximum_fusion.22.tokens) | copy-start | bytes 589828
  7.9 14.2 %collective-permute-start = (bf16[2,64,768]{2,1,0:T(8,128)(2,1)S(1)}, bf16[2,64,768]{2,1,0:T(8,128)(2,1)S(1)}, u32[]{:S(2)}, u32[]{:S(2)}) collective-permute-start(bf16[2,64,768]{2,1,0:T(8,128)(2,1)S(1)} %pad_maximum_fusion.22.tokens), channel_id=1, source_target_pairs={{0,4},{1,5},{2,6},{3,7},{4,0},{5,1},{6,2},{7,3},{8,12},{9,13},{10,... | collective-permute-start | bytes 589832 | tf_op jit(solution)/shard_map/ppermute | solution.py:252
  8.8 17.3 %collective-permute-start.15 = (bf16[1,48,1536]{2,1,0:T(8,128)(2,1)S(1)}, bf16[1,48,1536]{2,1,0:T(8,128)(2,1)S(1)}, u32[]{:S(2)}, u32[]{:S(2)}) collective-permute-start(bf16[1,48,1536]{2,1,0:T(8,128)(2,1)S(1)} %maximum_bitcast_fusion.1), channel_id=1, source_target_pairs={{0,4},{1,5},{2,6},{3,7},{4,0},{5,1},{6,2},{7,3},{8,12},{9,13},{10,... | collective-permute-start | bytes 442376 | tf_op jit(solution)/shard_map/ppermute | solution.py:252
  10.4 27.7 %collective-permute-start.5 = (bf16[1,48,1664]{2,1,0:T(8,128)(2,1)S(1)}, bf16[1,48,1664]{2,1,0:T(8,128)(2,1)S(1)}, u32[]{:S(2)}, u32[]{:S(2)}) collective-permute-start(bf16[1,48,1664]{2,1,0:T(8,128)(2,1)S(1)} %maximum_bitcast_fusion), channel_id=1, source_target_pairs={{0,4},{1,5},{2,6},{3,7},{4,0},{5,1},{6,2},{7,3},{8,12},{9,13},{10,... | collective-permute-start | bytes 479240 | tf_op jit(solution)/shard_map/ppermute | solution.py:252
  11.5 30.2 %collective-permute-start.22 = (bf16[2,96,768]{2,1,0:T(8,128)(2,1)S(1)}, bf16[2,96,768]{2,1,0:T(8,128)(2,1)S(1)}, u32[]{:S(2)}, u32[]{:S(2)}) collective-permute-start(bf16[2,96,768]{2,1,0:T(8,128)(2,1)S(1)} %pad_maximum_fusion.12), channel_id=1, source_target_pairs={{0,8},{1,9},{2,10},{3,11},{4,12},{5,13},{6,14},{7,15},{8,0},{9,1},... | collective-permute-start | bytes 884744 | tf_op jit(solution)/shard_map/ppermute | solution.py:252
  22.2 14.3 %collective-permute-start.1 = (bf16[2,2,64,768]{3,2,1,0:T(8,128)(2,1)S(1)}, bf16[2,2,64,768]{3,2,1,0:T(8,128)(2,1)S(1)}, u32[]{:S(2)}, u32[]{:S(2)}) collective-permute-start(bf16[2,2,64,768]{3,2,1,0:T(8,128)(2,1)S(1)} %pad_maximum_fusion.9), channel_id=1, source_target_pairs={{0,8},{1,9},{2,10},{3,11},{4,12},{5,13},{6,14},{7,15},{16,24},{17,... | collective-permute-start | bytes 1179656 | tf_op jit(solution)/shard_map/ppermute | solution.py:252
  26.1 31.3 %collective-permute-start.16 = (bf16[2,48,1536]{2,1,0:T(8,128)(2,1)S(1)}, bf16[2,48,1536]{2,1,0:T(8,128)(2,1)S(1)}, u32[]{:S(2)}, u32[]{:S(2)}) collective-permute-start(bf16[2,48,1536]{2,1,0:T(8,128)(2,1)S(1)} %pad_maximum_fusion.11), channel_id=1, source_target_pairs={{0,8},{1,9},{2,10},{3,11},{4,12},{5,13},{6,14},{7,15},{8,0},{9,1},... | collective-permute-start | bytes 884744 | tf_op jit(solution)/shard_map/ppermute | solution.py:252
  36.6 20.5 %collective-permute-start.2 = (bf16[4,2,64,768]{3,2,1,0:T(8,128)(2,1)S(1)}, bf16[4,2,64,768]{3,2,1,0:T(8,128)(2,1)S(1)}, u32[]{:S(2)}, u32[]{:S(2)}) collective-permute-start(bf16[4,2,64,768]{3,2,1,0:T(8,128)(2,1)S(1)} %pad_maximum_fusion.1), channel_id=1, source_target_pairs={{0,2},{1,3},{2,0},{3,1},{4,6},{5,7},{6,4},{7,5},{8,10},{9,11},{10,... | collective-permute-start | bytes 2359304 | tf_op jit(solution)/shard_map/ppermute | solution.py:252
  38.2 19.2 %collective-permute-start.6 = (bf16[2,48,1664]{2,1,0:T(8,128)(2,1)S(1)}, bf16[2,48,1664]{2,1,0:T(8,128)(2,1)S(1)}, u32[]{:S(2)}, u32[]{:S(2)}) collective-permute-start(bf16[2,48,1664]{2,1,0:T(8,128)(2,1)S(1)} %pad_maximum_fusion.8), channel_id=1, source_target_pairs={{0,8},{1,9},{2,10},{3,11},{4,12},{5,13},{6,14},{7,15},{8,0},{9,1},... | collective-permute-start | bytes 958472 | tf_op jit(solution)/shard_map/ppermute | solution.py:252
  41.8 30.5 %collective-permute-start.23 = (bf16[4,96,384]{2,1,0:T(8,128)(2,1)S(1)}, bf16[4,96,384]{2,1,0:T(8,128)(2,1)S(1)}, u32[]{:S(2)}, u32[]{:S(2)}) collective-permute-start(bf16[4,96,384]{2,1,0:T(8,128)(2,1)S(1)} %pad_maximum_fusion.20), channel_id=1, source_target_pairs={{0,2},{1,3},{2,0},{3,1},{4,6},{5,7},{6,4},{7,5},{8,10},{9,11},{10,... | collective-permute-start | bytes 884744 | tf_op jit(solution)/shard_map/ppermute | solution.py:252
  42.5 30.5 %collective-permute-start.25 = (bf16[4,96,384]{2,1,0:T(8,128)(2,1)S(1)}, bf16[4,96,384]{2,1,0:T(8,128)(2,1)S(1)}, u32[]{:S(2)}, u32[]{:S(2)}) collective-permute-start(bf16[4,96,384]{2,1,0:T(8,128)(2,1)S(1)} %pad_maximum_fusion.21), channel_id=1, source_target_pairs={{0,16},{1,17},{2,18},{3,19},{4,20},{5,21},{6,22},{7,23},{8,24},{9,... | collective-permute-start | bytes 884744 | tf_op jit(solution)/shard_map/ppermute | solution.py:252
  57.3 41.3 %collective-permute-start.3 = (bf16[8,2,64,768]{3,2,1,0:T(8,128)(2,1)S(1)}, bf16[8,2,64,768]{3,2,1,0:T(8,128)(2,1)S(1)}, u32[]{:S(2)}, u32[]{:S(2)}) collective-permute-start(bf16[8,2,64,768]{3,2,1,0:T(8,128)(2,1)S(1)} %pad_maximum_fusion.tok_mine), channel_id=1, source_target_pairs={{0,1},{1,0},{2,3},{3,2},{4,5},{5,4},{6,7},{7,6},{8,9},{9,8},{10,11... | collective-permute-start | bytes 4718600 | tf_op jit(solution)/shard_map/ppermute | solution.py:252
  57.5 11.6 %collective-permute-start.7 = (bf16[4,48,896]{2,1,0:T(8,128)(2,1)S(1)}, bf16[4,48,896]{2,1,0:T(8,128)(2,1)S(1)}, u32[]{:S(2)}, u32[]{:S(2)}) collective-permute-start(bf16[4,48,896]{2,1,0:T(8,128)(2,1)S(1)} %pad_maximum_fusion.13), channel_id=1, source_target_pairs={{0,2},{1,3},{2,0},{3,1},{4,6},{5,7},{6,4},{7,5},{8,10},{9,11},{10,... | collective-permute-start | bytes 1032200 | tf_op jit(solution)/shard_map/ppermute | solution.py:252
  59.1 11.6 %collective-permute-start.9 = (bf16[4,48,768]{2,1,0:T(8,128)(2,1)S(1)}, bf16[4,48,768]{2,1,0:T(8,128)(2,1)S(1)}, u32[]{:S(2)}, u32[]{:S(2)}) collective-permute-start(bf16[4,48,768]{2,1,0:T(8,128)(2,1)S(1)} %pad_maximum_fusion.17), channel_id=1, source_target_pairs={{0,16},{1,17},{2,18},{3,19},{4,20},{5,21},{6,22},{7,23},{8,24},{9,... | collective-permute-start | bytes 884744 | tf_op jit(solution)/shard_map/ppermute | solution.py:252
  60.7 13.3 %copy-start.28 = (bf16[2,1,64,767]{3,2,1,0:T(8,128)(2,1)S(1)}, bf16[2,1,64,767]{3,2,1,0:T(8,128)(2,1)}, u32[]{:S(2)}) copy-start(bf16[2,1,64,767]{3,2,1,0:T(8,128)(2,1)} %param.11) | copy-start | bytes 589060
  69.1 9.9 %collective-permute-start.17 = (bf16[4,48,768]{2,1,0:T(8,128)(2,1)S(1)}, bf16[4,48,768]{2,1,0:T(8,128)(2,1)S(1)}, u32[]{:S(2)}, u32[]{:S(2)}) collective-permute-start(bf16[4,48,768]{2,1,0:T(8,128)(2,1)S(1)} %pad_maximum_fusion.18), channel_id=1, source_target_pairs={{0,2},{1,3},{2,0},{3,1},{4,6},{5,7},{6,4},{7,5},{8,10},{9,11},{10,... | collective-permute-start | bytes 884744 | tf_op jit(solution)/shard_map/ppermute | solution.py:252
  70.7 26.5 %collective-permute-start.8 = (bf16[8,48,896]{2,1,0:T(8,128)(2,1)S(1)}, bf16[8,48,896]{2,1,0:T(8,128)(2,1)S(1)}, u32[]{:S(2)}, u32[]{:S(2)}) collective-permute-start(bf16[8,48,896]{2,1,0:T(8,128)(2,1)S(1)} %pad_maximum_fusion.2.w0), channel_id=1, source_target_pairs={{0,16},{1,17},{2,18},{3,19},{4,20},{5,21},{6,22},{7,23},{8,24},{9,... | collective-permute-start | bytes 2064392 | tf_op jit(solution)/shard_map/ppermute | solution.py:252
  72.3 22.3 %copy-start.2 = (bf16[8,48,768]{2,1,0:T(8,128)(2,1)}, bf16[8,48,768]{2,1,0:T(8,128)(2,1)S(1)}, u32[]{:S(2)}) copy-start(bf16[8,48,768]{2,1,0:T(8,128)(2,1)S(1)} %pad_maximum_fusion.3.w2) | copy-start | bytes 1769476
  72.4 20.9 %collective-permute-start.19 = (bf16[4,48,768]{2,1,0:T(8,128)(2,1)S(1)}, bf16[4,48,768]{2,1,0:T(8,128)(2,1)S(1)}, u32[]{:S(2)}, u32[]{:S(2)}) collective-permute-start(bf16[4,48,768]{2,1,0:T(8,128)(2,1)S(1)} %pad_maximum_fusion.19), channel_id=1, source_target_pairs={{0,16},{1,17},{2,18},{3,19},{4,20},{5,21},{6,22},{7,23},{8,24},{9,... | collective-permute-start | bytes 884744 | tf_op jit(solution)/shard_map/ppermute | solution.py:252
  72.9 22.6 %collective-permute-start.10 = (bf16[8,48,768]{2,1,0:T(8,128)(2,1)S(1)}, bf16[8,48,768]{2,1,0:T(8,128)(2,1)S(1)}, u32[]{:S(2)}, u32[]{:S(2)}) collective-permute-start(bf16[8,48,768]{2,1,0:T(8,128)(2,1)S(1)} %pad_maximum_fusion.3.w2), channel_id=1, source_target_pairs={{0,2},{1,3},{2,0},{3,1},{4,6},{5,7},{6,4},{7,5},{8,10},{9,11},{10,... | collective-permute-start | bytes 1769480 | tf_op jit(solution)/shard_map/ppermute | solution.py:252
  74.1 20.6 %copy-start.9 = (bf16[2,64,768]{2,1,0:T(8,128)(2,1)}, bf16[2,64,768]{2,1,0:T(8,128)(2,1)S(1)}, u32[]{:S(2)}) copy-start(bf16[2,64,768]{2,1,0:T(8,128)(2,1)S(1)} %pad.18.cot_mine) | copy-start | bytes 589828
  74.2 21.4 %copy-start.3 = (bf16[8,96,384]{2,1,0:T(8,128)(2,1)}, bf16[8,96,384]{2,1,0:T(8,128)(2,1)S(1)}, u32[]{:S(2)}) copy-start(bf16[8,96,384]{2,1,0:T(8,128)(2,1)S(1)} %pad_maximum_fusion.6.d0) | copy-start | bytes 1769476
  74.3 43.3 %copy-start.4 = (bf16[8,96,384]{2,1,0:T(8,128)(2,1)}, bf16[8,96,384]{2,1,0:T(8,128)(2,1)S(1)}, u32[]{:S(2)}) copy-start(bf16[8,96,384]{2,1,0:T(8,128)(2,1)S(1)} %pad_maximum_fusion.7.d2) | copy-start | bytes 1769476
  79.0 38.5 %collective-permute-start.13 = (bf16[2,64,768]{2,1,0:T(8,128)(2,1)S(1)}, bf16[2,64,768]{2,1,0:T(8,128)(2,1)S(1)}, u32[]{:S(2)}, u32[]{:S(2)}) collective-permute-start(bf16[2,64,768]{2,1,0:T(8,128)(2,1)S(1)} %pad.18.cot_mine), channel_id=1, source_target_pairs={{0,1},{1,0},{2,3},{3,2},{4,5},{5,4},{6,7},{7,6},{8,9},{9,8},{10,11... | collective-permute-start | bytes 589832 | tf_op jit(solution)/shard_map/ppermute | solution.py:252
  93.3 24.4 %collective-permute-start.26 = (bf16[8,96,384]{2,1,0:T(8,128)(2,1)S(1)}, bf16[8,96,384]{2,1,0:T(8,128)(2,1)S(1)}, u32[]{:S(2)}, u32[]{:S(2)}) collective-permute-start(bf16[8,96,384]{2,1,0:T(8,128)(2,1)S(1)} %pad_maximum_fusion.7.d2), channel_id=1, source_target_pairs={{0,2},{1,3},{2,0},{3,1},{4,6},{5,7},{6,4},{7,5},{8,10},{9,11},{10,... | collective-permute-start | bytes 1769480 | tf_op jit(solution)/shard_map/ppermute | solution.py:252
  95.6 22.6 %collective-permute-start.24 = (bf16[8,96,384]{2,1,0:T(8,128)(2,1)S(1)}, bf16[8,96,384]{2,1,0:T(8,128)(2,1)S(1)}, u32[]{:S(2)}, u32[]{:S(2)}) collective-permute-start(bf16[8,96,384]{2,1,0:T(8,128)(2,1)S(1)} %pad_maximum_fusion.6.d0), channel_id=1, source_target_pairs={{0,16},{1,17},{2,18},{3,19},{4,20},{5,21},{6,22},{7,23},{8,24},{9,... | collective-permute-start | bytes 1769480 | tf_op jit(solution)/shard_map/ppermute | solution.py:252
  97.2 22.0 %collective-permute-start.20 = (bf16[8,48,768]{2,1,0:T(8,128)(2,1)}, bf16[8,48,768]{2,1,0:T(8,128)(2,1)}, u32[]{:S(2)}, u32[]{:S(2)}) collective-permute-start(bf16[8,48,768]{2,1,0:T(8,128)(2,1)} %pad_maximum_fusion.5.u2), channel_id=1, source_target_pairs={{0,2},{1,3},{2,0},{3,1},{4,6},{5,7},{6,4},{7,5},{8,10},{9,11},{10,... | collective-permute-start | bytes 1769480 | tf_op jit(solution)/shard_map/ppermute | solution.py:252
  99.9 21.4 %collective-permute-start.18 = (bf16[8,48,768]{2,1,0:T(8,128)(2,1)}, bf16[8,48,768]{2,1,0:T(8,128)(2,1)}, u32[]{:S(2)}, u32[]{:S(2)}) collective-permute-start(bf16[8,48,768]{2,1,0:T(8,128)(2,1)} %pad_maximum_fusion.4.u0), channel_id=1, source_target_pairs={{0,16},{1,17},{2,18},{3,19},{4,20},{5,21},{6,22},{7,23},{8,24},{9,... | collective-permute-start | bytes 1769480 | tf_op jit(solution)/shard_map/ppermute | solution.py:252
  117.6 3.7 %collective-permute-start.12 = (bf16[768,384]{1,0:T(8,128)(2,1)}, bf16[768,384]{1,0:T(8,128)(2,1)S(1)}, u32[]{:S(2)}, u32[]{:S(2)}) collective-permute-start(bf16[768,384]{1,0:T(8,128)(2,1)} %get-tuple-element.41.wout_mine), channel_id=1, source_target_pairs={{0,1},{1,0},{2,3},{3,2},{4,5},{5,4},{6,7},{7,6},{8,9},{9,8},{10,11... | collective-permute-start | bytes 1769480 | tf_op jit(solution)/shard_map/ppermute | solution.py:252
  117.7 3.5 %collective-permute-start.11 = (bf16[256,384]{1,0:T(8,128)(2,1)}, bf16[256,384]{1,0:T(8,128)(2,1)S(1)}, u32[]{:S(2)}, u32[]{:S(2)}) collective-permute-start(bf16[256,384]{1,0:T(8,128)(2,1)} %get-tuple-element.39.attn_mine), channel_id=1, source_target_pairs={{0,1},{1,0},{2,3},{3,2},{4,5},{5,4},{6,7},{7,6},{8,9},{9,8},{10,11... | collective-permute-start | bytes 589832 | tf_op jit(solution)/shard_map/ppermute | solution.py:252
  136.1 20.0 %copy-start.19 = (bf16[8,48,768]{2,1,0:T(8,128)(2,1)S(1)}, bf16[8,48,768]{2,1,0:T(8,128)(2,1)}, u32[]{:S(2)}) copy-start(bf16[8,48,768]{2,1,0:T(8,128)(2,1)} %get-tuple-element.62) | copy-start | bytes 1769476
  136.1 16.5 %collective-permute-start.39 = (bf16[8,48,768]{2,1,0:T(8,128)(2,1)}, bf16[8,48,768]{2,1,0:T(8,128)(2,1)S(1)}, u32[]{:S(2)}, u32[]{:S(2)}) collective-permute-start(bf16[8,48,768]{2,1,0:T(8,128)(2,1)} %get-tuple-element.61), channel_id=1, source_target_pairs={{0,16},{1,17},{2,18},{3,19},{4,20},{5,21},{6,22},{7,23},{8,24},{9,... | collective-permute-start | bytes 1769480 | tf_op jit(solution)/shard_map/ppermute | solution.py:252
  137.7 18.4 %collective-permute-start.41 = (bf16[8,48,768]{2,1,0:T(8,128)(2,1)}, bf16[8,48,768]{2,1,0:T(8,128)(2,1)S(1)}, u32[]{:S(2)}, u32[]{:S(2)}) collective-permute-start(bf16[8,48,768]{2,1,0:T(8,128)(2,1)} %get-tuple-element.63), channel_id=1, source_target_pairs={{0,2},{1,3},{2,0},{3,1},{4,6},{5,7},{6,4},{7,5},{8,10},{9,11},{10,... | collective-permute-start | bytes 1769480 | tf_op jit(solution)/shard_map/ppermute | solution.py:252
  139.2 26.1 %collective-permute-start.46 = (bf16[8,96,384]{2,1,0:T(8,128)(2,1)}, bf16[8,96,384]{2,1,0:T(8,128)(2,1)S(1)}, u32[]{:S(2)}, u32[]{:S(2)}) collective-permute-start(bf16[8,96,384]{2,1,0:T(8,128)(2,1)} %get-tuple-element.65), channel_id=1, source_target_pairs={{0,16},{1,17},{2,18},{3,19},{4,20},{5,21},{6,22},{7,23},{8,24},{9,... | collective-permute-start | bytes 1769480 | tf_op jit(solution)/shard_map/ppermute | solution.py:252
  139.7 28.0 %collective-permute-start.48 = (bf16[8,96,384]{2,1,0:T(8,128)(2,1)}, bf16[8,96,384]{2,1,0:T(8,128)(2,1)S(1)}, u32[]{:S(2)}, u32[]{:S(2)}) collective-permute-start(bf16[8,96,384]{2,1,0:T(8,128)(2,1)} %get-tuple-element.67), channel_id=1, source_target_pairs={{0,2},{1,3},{2,0},{3,1},{4,6},{5,7},{6,4},{7,5},{8,10},{9,11},{10,... | collective-permute-start | bytes 1769480 | tf_op jit(solution)/shard_map/ppermute | solution.py:252
  140.2 29.9 %collective-permute-start.27 = (bf16[512,768]{1,0:T(8,128)(2,1)}, bf16[512,768]{1,0:T(8,128)(2,1)S(1)}, u32[]{:S(2)}, u32[]{:S(2)}) collective-permute-start(bf16[512,768]{1,0:T(8,128)(2,1)} %get-tuple-element.43.part_mine), channel_id=1, source_target_pairs={{0,1},{1,0},{2,3},{3,2},{4,5},{5,4},{6,7},{7,6},{8,9},{9,8},{10,11... | collective-permute-start | bytes 2359304 | tf_op jit(solution)/shard_map/ppermute | solution.py:252
  154.6 39.9 %collective-permute-start.40 = (bf16[4,48,768]{2,1,0:T(8,128)(2,1)}, bf16[4,48,768]{2,1,0:T(8,128)(2,1)}, u32[]{:S(2)}, u32[]{:S(2)}) collective-permute-start(bf16[4,48,768]{2,1,0:T(8,128)(2,1)} %slice.339), channel_id=1, source_target_pairs={{0,2},{1,3},{2,0},{3,1},{4,6},{5,7},{6,4},{7,5},{8,10},{9,11},{10,... | collective-permute-start | bytes 884744 | tf_op jit(solution)/shard_map/ppermute | solution.py:252
  156.3 11.5 %copy-start.17 = (bf16[8,96,384]{2,1,0:T(8,128)(2,1)S(1)}, bf16[8,96,384]{2,1,0:T(8,128)(2,1)}, u32[]{:S(2)}) copy-start(bf16[8,96,384]{2,1,0:T(8,128)(2,1)} %get-tuple-element.66) | copy-start | bytes 1769476
  157.0 39.2 %collective-permute-start.42 = (bf16[4,48,768]{2,1,0:T(8,128)(2,1)}, bf16[4,48,768]{2,1,0:T(8,128)(2,1)}, u32[]{:S(2)}, u32[]{:S(2)}) collective-permute-start(bf16[4,48,768]{2,1,0:T(8,128)(2,1)} %slice.341), channel_id=1, source_target_pairs={{0,16},{1,17},{2,18},{3,19},{4,20},{5,21},{6,22},{7,23},{8,24},{9,... | collective-permute-start | bytes 884744 | tf_op jit(solution)/shard_map/ppermute | solution.py:252
  166.2 31.2 %collective-permute-start.47 = (bf16[4,96,384]{2,1,0:T(8,128)(2,1)}, bf16[4,96,384]{2,1,0:T(8,128)(2,1)}, u32[]{:S(2)}, u32[]{:S(2)}) collective-permute-start(bf16[4,96,384]{2,1,0:T(8,128)(2,1)} %slice.349), channel_id=1, source_target_pairs={{0,2},{1,3},{2,0},{3,1},{4,6},{5,7},{6,4},{7,5},{8,10},{9,11},{10,... | collective-permute-start | bytes 884744 | tf_op jit(solution)/shard_map/ppermute | solution.py:252
  168.6 33.4 %collective-permute-start.49 = (bf16[4,96,384]{2,1,0:T(8,128)(2,1)}, bf16[4,96,384]{2,1,0:T(8,128)(2,1)}, u32[]{:S(2)}, u32[]{:S(2)}) collective-permute-start(bf16[4,96,384]{2,1,0:T(8,128)(2,1)} %slice.351), channel_id=1, source_target_pairs={{0,16},{1,17},{2,18},{3,19},{4,20},{5,21},{6,22},{7,23},{8,24},{9,... | collective-permute-start | bytes 884744 | tf_op jit(solution)/shard_map/ppermute | solution.py:252
  194.0 44.6 %collective-permute-start.32 = (bf16[8,48,768]{2,1,0:T(8,128)(2,1)}, bf16[8,48,768]{2,1,0:T(8,128)(2,1)S(1)}, u32[]{:S(2)}, u32[]{:S(2)}) collective-permute-start(bf16[8,48,768]{2,1,0:T(8,128)(2,1)} %get-tuple-element.57), channel_id=1, source_target_pairs={{0,16},{1,17},{2,18},{3,19},{4,20},{5,21},{6,22},{7,23},{8,24},{9,... | collective-permute-start | bytes 1769480 | tf_op jit(solution)/shard_map/ppermute | solution.py:252
  194.6 45.7 %collective-permute-start.34 = (bf16[8,48,768]{2,1,0:T(8,128)(2,1)}, bf16[8,48,768]{2,1,0:T(8,128)(2,1)S(1)}, u32[]{:S(2)}, u32[]{:S(2)}) collective-permute-start(bf16[8,48,768]{2,1,0:T(8,128)(2,1)} %get-tuple-element.59), channel_id=1, source_target_pairs={{0,2},{1,3},{2,0},{3,1},{4,6},{5,7},{6,4},{7,5},{8,10},{9,11},{10,... | collective-permute-start | bytes 1769480 | tf_op jit(solution)/shard_map/ppermute | solution.py:252
  196.2 78.3 %collective-permute-start.28 = (bf16[8,2,64,768]{3,2,1,0:T(8,128)(2,1)}, bf16[8,2,64,768]{3,2,1,0:T(8,128)(2,1)S(1)}, u32[]{:S(2)}, u32[]{:S(2)}) collective-permute-start(bf16[8,2,64,768]{3,2,1,0:T(8,128)(2,1)} %get-tuple-element.54), channel_id=1, source_target_pairs={{0,1},{1,0},{2,3},{3,2},{4,5},{5,4},{6,7},{7,6},{8,9},{9,8},{10,11... | collective-permute-start | bytes 4718600 | tf_op jit(solution)/shard_map/ppermute | solution.py:252
  197.4 11.4 %collective-permute-start.43 = (bf16[2,48,1536]{2,1,0:T(8,128)(2,1)S(1)}, bf16[2,48,1536]{2,1,0:T(8,128)(2,1)S(1)}, u32[]{:S(2)}, u32[]{:S(2)}) collective-permute-start(bf16[2,48,1536]{2,1,0:T(8,128)(2,1)S(1)} %pad_maximum_fusion.15), channel_id=1, source_target_pairs={{0,8},{1,9},{2,10},{3,11},{4,12},{5,13},{6,14},{7,15},{8,0},{9,1},... | collective-permute-start | bytes 884744 | tf_op jit(solution)/shard_map/ppermute | solution.py:252
  203.0 29.1 %collective-permute-start.50 = (bf16[2,96,768]{2,1,0:T(8,128)(2,1)S(1)}, bf16[2,96,768]{2,1,0:T(8,128)(2,1)S(1)}, u32[]{:S(2)}, u32[]{:S(2)}) collective-permute-start(bf16[2,96,768]{2,1,0:T(8,128)(2,1)S(1)} %pad_maximum_fusion.14), channel_id=1, source_target_pairs={{0,8},{1,9},{2,10},{3,11},{4,12},{5,13},{6,14},{7,15},{8,0},{9,1},... | collective-permute-start | bytes 884744 | tf_op jit(solution)/shard_map/ppermute | solution.py:252
  208.9 29.7 %copy-start.16 = (bf16[8,48,768]{2,1,0:T(8,128)(2,1)S(1)}, bf16[8,48,768]{2,1,0:T(8,128)(2,1)}, u32[]{:S(2)}) copy-start(bf16[8,48,768]{2,1,0:T(8,128)(2,1)} %get-tuple-element.56) | copy-start | bytes 1769476
  208.9 29.5 %collective-permute-start.44 = (bf16[48,1536]{1,0:T(8,128)(2,1)S(1)}, bf16[48,1536]{1,0:T(8,128)(2,1)S(1)}, u32[]{:S(2)}, u32[]{:S(2)}) collective-permute-start(bf16[48,1536]{1,0:T(8,128)(2,1)S(1)} %slice_bitcast_fusion.4), channel_id=1, source_target_pairs={{0,4},{1,5},{2,6},{3,7},{4,0},{5,1},{6,2},{7,3},{8,12},{9,13},{10,... | collective-permute-start | bytes 442376 | tf_op jit(solution)/shard_map/ppermute | solution.py:252
  232.2 9.9 %collective-permute-start.51 = (bf16[96,768]{1,0:T(8,128)(2,1)S(1)}, bf16[96,768]{1,0:T(8,128)(2,1)S(1)}, u32[]{:S(2)}, u32[]{:S(2)}) collective-permute-start(bf16[96,768]{1,0:T(8,128)(2,1)S(1)} %get-tuple-element.100), channel_id=1, source_target_pairs={{0,4},{1,5},{2,6},{3,7},{4,0},{5,1},{6,2},{7,3},{8,12},{9,13},{10,... | collective-permute-start | bytes 442376 | tf_op jit(solution)/shard_map/ppermute | solution.py:252
  238.5 14.3 %collective-permute-start.45 = (f32[24,1536]{1,0:T(8,128)S(1)}, f32[24,1536]{1,0:T(8,128)S(1)}, u32[]{:S(2)}, u32[]{:S(2)}) collective-permute-start(f32[24,1536]{1,0:T(8,128)S(1)} %slice_select_fusion), channel_id=1, source_target_pairs={{0,1},{1,0},{2,3},{3,2},{4,5},{5,4},{6,7},{7,6},{8,9},{9,8},{10,11... | collective-permute-start | bytes 442376 | tf_op jit(solution)/shard_map/ppermute | solution.py:252
  238.8 9.5 %collective-permute-start.33 = (bf16[4,48,768]{2,1,0:T(8,128)(2,1)S(1)}, bf16[4,48,768]{2,1,0:T(8,128)(2,1)S(1)}, u32[]{:S(2)}, u32[]{:S(2)}) collective-permute-start(bf16[4,48,768]{2,1,0:T(8,128)(2,1)S(1)} %slice.321), channel_id=1, source_target_pairs={{0,2},{1,3},{2,0},{3,1},{4,6},{5,7},{6,4},{7,5},{8,10},{9,11},{10,... | collective-permute-start | bytes 884744 | tf_op jit(solution)/shard_map/ppermute | solution.py:252
  240.4 9.2 %collective-permute-start.35 = (bf16[4,48,768]{2,1,0:T(8,128)(2,1)S(1)}, bf16[4,48,768]{2,1,0:T(8,128)(2,1)S(1)}, u32[]{:S(2)}, u32[]{:S(2)}) collective-permute-start(bf16[4,48,768]{2,1,0:T(8,128)(2,1)S(1)} %slice.323), channel_id=1, source_target_pairs={{0,16},{1,17},{2,18},{3,19},{4,20},{5,21},{6,22},{7,23},{8,24},{9,... | collective-permute-start | bytes 884744 | tf_op jit(solution)/shard_map/ppermute | solution.py:252
  249.7 16.0 %collective-permute-start.36 = (bf16[2,48,1536]{2,1,0:T(8,128)(2,1)S(1)}, bf16[2,48,1536]{2,1,0:T(8,128)(2,1)S(1)}, u32[]{:S(2)}, u32[]{:S(2)}) collective-permute-start(bf16[2,48,1536]{2,1,0:T(8,128)(2,1)S(1)} %pad_maximum_fusion.16), channel_id=1, source_target_pairs={{0,8},{1,9},{2,10},{3,11},{4,12},{5,13},{6,14},{7,15},{8,0},{9,1},... | collective-permute-start | bytes 884744 | tf_op jit(solution)/shard_map/ppermute | solution.py:252
  266.5 5.5 %collective-permute-start.37 = (bf16[48,1536]{1,0:T(8,128)(2,1)}, bf16[48,1536]{1,0:T(8,128)(2,1)}, u32[]{:S(2)}, u32[]{:S(2)}) collective-permute-start(bf16[48,1536]{1,0:T(8,128)(2,1)} %slice_bitcast_fusion.6), channel_id=1, source_target_pairs={{0,4},{1,5},{2,6},{3,7},{4,0},{5,1},{6,2},{7,3},{8,12},{9,13},{10,... | collective-permute-start | bytes 442376 | tf_op jit(solution)/shard_map/ppermute | solution.py:252
  273.0 1.4 collective-permute-start.38
  275.0 19.7 %collective-permute-start.29 = (bf16[4,2,64,768]{3,2,1,0:T(8,128)(2,1)S(1)}, bf16[4,2,64,768]{3,2,1,0:T(8,128)(2,1)S(1)}, u32[]{:S(2)}, u32[]{:S(2)}) collective-permute-start(bf16[4,2,64,768]{3,2,1,0:T(8,128)(2,1)S(1)} %slice.315), channel_id=1, source_target_pairs={{0,2},{1,3},{2,0},{3,1},{4,6},{5,7},{6,4},{7,5},{8,10},{9,11},{10,... | collective-permute-start | bytes 2359304 | tf_op jit(solution)/shard_map/ppermute | solution.py:252
  275.8 21.1 %copy-start.23 = (bf16[24,2304]{1,0:T(8,128)(2,1)S(1)}, bf16[24,2304]{1,0:T(8,128)(2,1)}, u32[]{:S(2)}) copy-start(bf16[24,2304]{1,0:T(8,128)(2,1)} %param.12) | copy-start | bytes 331780
  294.9 22.4 %copy-start.32 = (bf16[24]{0:T(256)(128)(2,1)S(1)}, bf16[24]{0:T(256)(128)(2,1)}, u32[]{:S(2)}) copy-start(bf16[24]{0:T(256)(128)(2,1)} %param.16) | copy-start | bytes 148
  294.9 21.6 %collective-permute-start.30 = (bf16[2,2,64,768]{3,2,1,0:T(8,128)(2,1)S(1)}, bf16[2,2,64,768]{3,2,1,0:T(8,128)(2,1)S(1)}, u32[]{:S(2)}, u32[]{:S(2)}) collective-permute-start(bf16[2,2,64,768]{3,2,1,0:T(8,128)(2,1)S(1)} %slice.317), channel_id=1, source_target_pairs={{8,0},{9,1},{10,2},{11,3},{12,4},{13,5},{14,6},{15,7},{24,16},{25,... | collective-permute-start | bytes 1179656 | tf_op jit(solution)/shard_map/ppermute | solution.py:252
  296.9 29.4 %copy-start.25 = (f32[24,2304]{1,0:T(8,128)}, f32[24,2304]{1,0:T(8,128)S(1)}, u32[]{:S(2)}) copy-start(f32[24,2304]{1,0:T(8,128)S(1)} %slice_dynamic-update-slice_fusion) | copy-start | bytes 663556
  317.3 5.8 %collective-permute-start.31 = (bf16[2,64,768]{2,1,0:T(8,128)(2,1)S(1)}, bf16[2,64,768]{2,1,0:T(8,128)(2,1)S(1)}, u32[]{:S(2)}, u32[]{:S(2)}) collective-permute-start(bf16[2,64,768]{2,1,0:T(8,128)(2,1)S(1)} %get-tuple-element.96), channel_id=1, source_target_pairs={{0,4},{1,5},{2,6},{3,7},{4,0},{5,1},{6,2},{7,3},{8,12},{9,13},{10,... | collective-permute-start | bytes 589832 | tf_op jit(solution)/shard_map/ppermute | solution.py:252
  (21 other events, 82.6 us)

commit v2 on v1

--- a/solution.py
+++ b/solution.py
@@ -304,30 +304,59 @@
     return z_bits | ((other | pair << 3) if which == 0 else (other << 3 | pair))
 
 
-def gather_weights(first, second):
-    cut = first.shape[-1]
-    joined = jnp.concatenate([first, second], axis=-1)[None]
-    two = jnp.concatenate([joined, swap(joined, AXIS_Z_NEAR)], axis=0)
-    far = swap(two, AXIS_Z_FAR)
-    four_a = jnp.concatenate([two[..., :cut], far[..., :cut]], axis=0)
-    four_b = jnp.concatenate([two[..., cut:], far[..., cut:]], axis=0)
-    eight_a = jnp.concatenate([four_a, swap(four_a, AXIS_X)], axis=0)
-    eight_b = jnp.concatenate([four_b, swap(four_b, AXIS_Y)], axis=0)
+def gather_z(block):
+    near = swap(block, AXIS_Z_NEAR)
+    far = swap(block, AXIS_Z_FAR)
+    end = swap(block, AXIS_Z_NEAR | AXIS_Z_FAR)
+    return block, near, far, end
+
+
+def gather_first(four, cut):
+    four_a = jnp.stack([array[:, :cut] for array in four])
+    four_b = jnp.stack([array[:, cut:] for array in four])
+    return four_a, swap(four_a, AXIS_X), four_b, swap(four_b, AXIS_Y)
+
+
+def gather_second(four_a, got_a, four_b, got_b):
+    eight_a = jnp.concatenate([four_a, got_a], axis=0)
+    eight_b = jnp.concatenate([four_b, got_b], axis=0)
     return eight_a, swap(eight_a, AXIS_Y), eight_b, swap(eight_b, AXIS_X)
 
 
-def reduce_weights(pieces):
+def add(first, *others):
+    total = first.astype(jnp.float32)
+    for other in others:
+        total = total + other.astype(jnp.float32)
+    return total
+
+
+def reduce_start(pieces):
     keep_a, send_a, keep_b, send_b = pieces
-    eight_a = keep_a.astype(jnp.float32) + swap(send_a, AXIS_Y).astype(jnp.float32)
-    eight_b = keep_b.astype(jnp.float32) + swap(send_b, AXIS_X).astype(jnp.float32)
-    eight_a = eight_a.astype(jnp.bfloat16)
-    eight_b = eight_b.astype(jnp.bfloat16)
-    four_a = eight_a[:4].astype(jnp.float32) + swap(eight_a[4:], AXIS_X).astype(jnp.float32)
-    four_b = eight_b[:4].astype(jnp.float32) + swap(eight_b[4:], AXIS_Y).astype(jnp.float32)
-    four = jnp.concatenate([four_a, four_b], axis=-1).astype(jnp.bfloat16)
-    two = four[:2].astype(jnp.float32) + swap(four[2:], AXIS_Z_FAR).astype(jnp.float32)
-    two = two.astype(jnp.bfloat16)
-    return two[0].astype(jnp.float32) + swap(two[1], AXIS_Z_NEAR).astype(jnp.float32)
+    return keep_a, swap(send_a, AXIS_Y), keep_b, swap(send_b, AXIS_X)
+
+
+def reduce_middle(keep_a, got_a, keep_b, got_b):
+    send_a = add(keep_a[4:], got_a[4:]).astype(jnp.bfloat16)
+    send_b = add(keep_b[4:], got_b[4:]).astype(jnp.bfloat16)
+    left_a = (keep_a[:4], got_a[:4], swap(send_a, AXIS_X))
+    left_b = (keep_b[:4], got_b[:4], swap(send_b, AXIS_Y))
+    return left_a, left_b
+
+
+def along_z(four):
+    near = swap(four[1], AXIS_Z_NEAR)
+    far = swap(four[2], AXIS_Z_FAR)
+    end = swap(four[3], AXIS_Z_NEAR | AXIS_Z_FAR)
+    return near, far, end
+
+
+def reduce_z(left_a, left_b):
+    four = jnp.concatenate([add(*left_a), add(*left_b)], axis=-1).astype(jnp.bfloat16)
+    return (four[0], *along_z(four))
+
+
+def fence(*arrays):
+    return lax.optimization_barrier(arrays)
 
 
 def piece_copies(pieces, targets, chip, rows, sem, base, outward=False):
@@ -360,20 +389,19 @@
 
 def forward_kernel(
     ids, tok_mine, tok_other, w0, w1, w2, w3,
-    attn_out, query_out, kv_out, normed_out, soft_out, wqk_out, wvo_out, wout_out, own_out, gains_out,
+    attn_out, query_out, kv_out, normed_out, soft_out, wqkv_out, wout_out, own_out, gains_out,
     tok, bias, sem,
 ):
     chip, core = ids[0], ids[1]
     place = lax.rem(chip, 8)
-    copies = piece_copies((w0, w1, w2, w3), (wqk_out, wvo_out), chip, 48, sem, 0)
+    copies = piece_copies((w0, w1, w2, w3), (wqkv_out, wout_out), chip, 48, sem, 0)
     copies += row_pieces(tok_mine, tok, place, core, 0, sem, 32)
     copies += row_pieces(tok_other, tok, place, core, 1, sem, 40)
     run_copies(copies)
-    wout_out[...] = wvo_out[:, HALF:]
     picks = lax.broadcasted_iota(jnp.int32, (8, 128), 0) == lax.broadcasted_iota(
         jnp.int32, (8, 128), 1
     )
-    gains_out[...] = dot_nt(picks.astype(jnp.bfloat16), wqk_out[:, WIDTH:])
+    gains_out[...] = dot_nt(picks.astype(jnp.bfloat16), wqkv_out[:, 3 * HALF :])
     gain = gains_out[0:1, :]
     lane = lanes(ROWS)
     for micro in range(2):
@@ -383,10 +411,7 @@
             values = tok[micro, pl.ds(at, ROWS), :].astype(jnp.float32)
             normed = (norm_rows(values, lane)[0] * gain).astype(jnp.bfloat16)
             normed_out[micro, pl.ds(at, ROWS), :] = normed
-            kv_out[micro, pl.ds(at, ROWS), :HALF] = dot(normed, wqk_out[:, HALF:WIDTH]).astype(
-                jnp.bfloat16
-            )
-            kv_out[micro, pl.ds(at, ROWS), HALF:] = dot(normed, wvo_out[:, :HALF]).astype(
+            kv_out[micro, pl.ds(at, ROWS), :] = dot(normed, wqkv_out[:, HALF : 3 * HALF]).astype(
                 jnp.bfloat16
             )
             return carry
@@ -398,7 +423,7 @@
     for micro in range(2):
         own = tok[micro, pl.ds(first_row, 128), :]
         own_out[micro * 128 : micro * 128 + 128, :] = own
-        query = dot(normed_out[micro, pl.ds(first_row, 128), :], wqk_out[:, :HALF])
+        query = dot(normed_out[micro, pl.ds(first_row, 128), :], wqkv_out[:, :HALF])
         query = query.astype(jnp.bfloat16) * jnp.bfloat16(0.125)
         query_out[micro * 128 : micro * 128 + 128, :] = query
         key_seg = dot_nt(hot, tok[micro])[0:1, :]
@@ -428,16 +453,32 @@
             ).astype(jnp.bfloat16)
 
 
-def feed_kernel(
+def feed_half(normed, cot, up, down, g_up, g_down, sum_mix, sum_norm):
+    slope = math.sqrt(2.0 / math.pi)
+    for part in range(2):
+        units = slice(part * HALF, part * HALF + HALF)
+        hidden = dot(normed, up[:, units])
+        square = hidden * hidden
+        wave = jnp.tanh(slope * hidden * (1.0 + 0.044715 * square))
+        active = (0.5 * hidden * (1.0 + wave)).astype(jnp.bfloat16)
+        grow = 0.5 * (1.0 + wave) + 0.5 * hidden * (1.0 - wave * wave) * slope * (
+            1.0 + 3.0 * 0.044715 * square
+        )
+        d_hidden = (dot_nt(cot, down[units, :]) * grow).astype(jnp.bfloat16)
+        sum_mix[...] += dot(active, down[units, :])
+        sum_norm[...] += dot_nt(d_hidden, up[:, units])
+        g_up[:, units] = dot_tn(normed, d_hidden).astype(jnp.bfloat16)
+        g_down[units, :] = dot_tn(active, cot).astype(jnp.bfloat16)
+
+
+def feed_first_kernel(
     ids, gains, attn_mine, attn_other, own, wout_mine, wout_other, cot_mine, cot_other,
-    u0, u1, u2, u3, d0, d1, d2, d3,
-    attn_out, cot_out, res_out, part_out,
-    gu0, gu1, gu2, gu3, gd0, gd1, gd2, gd3,
-    wu_a, wu_b, wd_a, wd_b, gu_a, gu_b, gd_a, gd_b, sum_mix, sum_norm, sem,
+    w0, w1, w2, w3,
+    attn_out, cot_out, res_out, normed_out, sum_mix, sum_norm, g0, g1, g2, g3,
+    up, down, g_up, g_down, sem,
 ):
     chip, core = ids[0], ids[1]
-    load = piece_copies((u0, u1, u2, u3), (wu_a, wu_b), chip, 48, sem, 0)
-    load += piece_copies((d0, d1, d2, d3), (wd_a, wd_b), chip, 96, sem, 32)
+    load = piece_copies((w0, w1, w2, w3), (up, down), chip, 48, sem, 0)
     for copy in load:
         copy.start()
     mine_at = pl.multiple_of(core * HALF, 128)
@@ -456,34 +497,30 @@
     residual = res_out[...] + own_values
     res_out[...] = residual
     normed = (norm_rows(residual, lane)[0] * gains[1:2, :]).astype(jnp.bfloat16)
-    cot = cot_out[...]
+    normed_out[...] = normed
+    sum_mix[...] = jnp.zeros_like(sum_mix)
+    sum_norm[...] = jnp.zeros_like(sum_norm)
     for copy in load:
         copy.wait()
-    slope = math.sqrt(2.0 / math.pi)
-    step = HALF
-    sum_mix[...] = jnp.zeros_like(sum_mix)
-    sum_norm[...] = jnp.zeros_like(sum_norm)
-    for part in range(UNITS // step):
-        up, g_up = (wu_a, gu_a) if part < 2 else (wu_b, gu_b)
-        cols = slice((part % 2) * step, (part % 2) * step + step)
-        rows = slice(part * step, part * step + step)
-        hidden = dot(normed, up[:, cols])
-        square = hidden * hidden
-        wave = jnp.tanh(slope * hidden * (1.0 + 0.044715 * square))
-        active = (0.5 * hidden * (1.0 + wave)).astype(jnp.bfloat16)
-        grow = 0.5 * (1.0 + wave) + 0.5 * hidden * (1.0 - wave * wave) * slope * (
-            1.0 + 3.0 * 0.044715 * square
-        )
-        d_active = dot_nt(cot[:, :HALF], wd_a[rows, :]) + dot_nt(cot[:, HALF:], wd_b[rows, :])
-        d_hidden = (d_active * grow).astype(jnp.bfloat16)
-        sum_mix[:, :HALF] += dot(active, wd_a[rows, :])
-        sum_mix[:, HALF:] += dot(active, wd_b[rows, :])
-        sum_norm[...] += dot_nt(d_hidden, up[:, cols])
-        g_up[:, cols] = dot_tn(normed, d_hidden).astype(jnp.bfloat16)
-        gd_a[rows, :] = dot_tn(active, cot[:, :HALF]).astype(jnp.bfloat16)
-        gd_b[rows, :] = dot_tn(active, cot[:, HALF:]).astype(jnp.bfloat16)
-    store = piece_copies((gu0, gu1, gu2, gu3), (gu_a, gu_b), chip, 48, sem, 0, True)
-    store += piece_copies((gd0, gd1, gd2, gd3), (gd_a, gd_b), chip, 96, sem, 32, True)
+    feed_half(normed, cot_out[...], up, down, g_up, g_down, sum_mix, sum_norm)
+    run_copies(piece_copies((g0, g1, g2, g3), (g_up, g_down), chip, 48, sem, 0, True))
+
+
+def feed_second_kernel(
+    ids, normed, cot, mix_in, norm_in, w0, w1, w2, w3,
+    part_out, g0, g1, g2, g3,
+    up, down, g_up, g_down, sum_mix, sum_norm, sem,
+):
+    chip = ids[0]
+    load = piece_copies((w0, w1, w2, w3), (up, down), chip, 48, sem, 0)
+    for copy in load:
+        copy.start()
+    sum_mix[...] = mix_in[...]
+    sum_norm[...] = norm_in[...]
+    for copy in load:
+        copy.wait()
+    feed_half(normed[...], cot[...], up, down, g_up, g_down, sum_mix, sum_norm)
+    store = piece_copies((g0, g1, g2, g3), (g_up, g_down), chip, 48, sem, 0, True)
     for copy in store:
         copy.start()
     part_out[:ROWS, :] = sum_mix[...].astype(jnp.bfloat16)
@@ -493,10 +530,10 @@
 
 
 def backward_kernel(
-    ids, gains, residual, part_mine, part_other, cot, attn, wout_mine, wout_other, wqk, wvo,
-    query, kv, normed_all, soft,
-    mixed_out, dres_out, g0, g1, g2, g3, keep_rows, send_rows,
-    g_a, g_b, d_attn, d_kv, d_query, d_rows, d_sum_ref, hold, sem,
+    ids, gains, residual, part_mine, part_other, cot, wout_mine, wout_other, wqkv,
+    query, kv, soft,
+    mixed_out, dres_out, keep_rows, send_rows, d_kv, d_query, d_sum_half,
+    d_attn, d_rows, d_sum_ref, hold, sem,
 ):
     chip, core = ids[0], ids[1]
     place = lax.rem(chip, 8)
@@ -505,13 +542,12 @@
     other_at = pl.multiple_of((1 - core) * HALF, 128)
     lane = lanes(ROWS)
     res = residual[...]
-    mixed = res + part_mine[:ROWS, :].astype(jnp.float32) + part_other[:ROWS, :].astype(jnp.float32)
+    mixed = add(res, part_mine[:ROWS, :], part_other[:ROWS, :])
     hold[...] = mixed
     for micro in range(2):
         at = pl.multiple_of(micro * 128 + core * 64, 64)
         mixed_out[micro] = hold[pl.ds(at, 64), : WIDTH - 1].astype(jnp.bfloat16)
-    d_normed = part_mine[ROWS:, :].astype(jnp.float32) + part_other[ROWS:, :].astype(jnp.float32)
-    d_normed = d_normed * gains[1:2, :]
+    d_normed = add(part_mine[ROWS:, :], part_other[ROWS:, :]) * gains[1:2, :]
     normed_two, factor = norm_rows(res, lane)
     d_res = cot[...].astype(jnp.float32) + norm_rows_back(d_normed, normed_two, factor, lane)
     hold[...] = d_res
@@ -521,11 +557,11 @@
     d_sum_ref[...] = d_res.astype(jnp.bfloat16)
     d_mine = d_sum_ref[:, pl.ds(mine_at, HALF)]
     d_other = d_sum_ref[:, pl.ds(other_at, HALF)]
+    d_sum_half[...] = d_mine
     d_heads = dot_nt(d_mine, wout_mine[pl.ds(mine_at, HALF), :]) + dot_nt(
         d_other, wout_other[pl.ds(mine_at, HALF), :]
     )
     d_attn[...] = d_heads.astype(jnp.bfloat16)
-    g_b[:, HALF:] = dot_tn(attn[...], d_mine).astype(jnp.bfloat16)
     small = lax.broadcasted_iota(jnp.int32, (128, 128), 1) < HEAD_DIM
     for micro in range(2):
         here = slice(micro * 128, micro * 128 + 128)
@@ -550,48 +586,45 @@
             d_query[here, cols] = jnp.where(small, d_q[:128], d_q[128:]).astype(jnp.bfloat16)
             d_kv[micro, :, cols] = dot_tn(d_scores, q_both).astype(jnp.bfloat16)
             d_kv[micro, :, value_cols] = dot_tn(weights, d_out).astype(jnp.bfloat16)
-    for micro in range(2):
 
         def row_chunk(index, carry, micro=micro):
             at = pl.multiple_of(index * ROWS, ROWS)
-            d_k = d_kv[micro, pl.ds(at, ROWS), :HALF]
-            d_v = d_kv[micro, pl.ds(at, ROWS), HALF:]
-            rows = dot_nt(d_k, wqk[:, HALF:WIDTH]) + dot_nt(d_v, wvo[:, :HALF])
+            rows = dot_nt(d_kv[micro, pl.ds(at, ROWS), :], wqkv[:, HALF : 3 * HALF])
             d_rows[micro, pl.ds(at, ROWS), :] = rows.astype(jnp.bfloat16)
             return carry
 
         lax.fori_loop(0, POSITIONS // ROWS, row_chunk, 0)
         own = d_rows[micro, pl.ds(first_row, 128), :].astype(jnp.float32)
-        own = own + dot_nt(d_query[micro * 128 : micro * 128 + 128, :], wqk[:, :HALF])
+        own = own + dot_nt(d_query[here, :], wqkv[:, :HALF])
         d_rows[micro, pl.ds(first_row, 128), :] = own.astype(jnp.bfloat16)
-    store = row_pieces(keep_rows, d_rows, place, core, 0, sem, 32, True)
-    store += row_pieces(send_rows, d_rows, place, core, 1, sem, 40, True)
-    for copy in store:
-        copy.start()
+    store = row_pieces(keep_rows, d_rows, place, core, 0, sem, 0, True)
+    store += row_pieces(send_rows, d_rows, place, core, 1, sem, 8, True)
+    run_copies(store)
+
+
+def gradient_kernel(
+    ids, attn, d_sum_half, d_query, d_kv, normed_all, g0, g1, g2, g3, g_a, g_b, sem
+):
+    chip = ids[0]
+    first_row = pl.multiple_of(lax.rem(chip, 8) * 128, 128)
     own_0 = normed_all[0, pl.ds(first_row, 128), :]
     own_1 = normed_all[1, pl.ds(first_row, 128), :]
+    g_b[...] = dot_tn(attn[...], d_sum_half[...]).astype(jnp.bfloat16)
     g_a[:, :HALF] = (dot_tn(own_0, d_query[:128, :]) + dot_tn(own_1, d_query[128:, :])).astype(
         jnp.bfloat16
     )
-    g_a[:, HALF:] = (
-        dot_tn(normed_all[0], d_kv[0, :, :HALF]) + dot_tn(normed_all[1], d_kv[1, :, :HALF])
-    ).astype(jnp.bfloat16)
-    g_b[:, :HALF] = (
-        dot_tn(normed_all[0], d_kv[0, :, HALF:]) + dot_tn(normed_all[1], d_kv[1, :, HALF:])
-    ).astype(jnp.bfloat16)
+    g_a[:, HALF:] = (dot_tn(normed_all[0], d_kv[0]) + dot_tn(normed_all[1], d_kv[1])).astype(
+        jnp.bfloat16
+    )
     run_copies(piece_copies((g0, g1, g2, g3), (g_a, g_b), chip, 48, sem, 0, True))
-    for copy in store:
-        copy.wait()
-
-
-def tail_kernel(gains, tokens, d_first, d_second, d_residual, grad_out):
+
+
+def tail_kernel(gains, tokens, d_0, d_1, d_2, d_3, d_residual, grad_out):
     lane = lanes(128)
     rows = (128, WIDTH)
     values = tokens[...].reshape(rows).astype(jnp.float32)
     normed, factor = norm_rows(values, lane)
-    d_normed = d_first[...].reshape(rows).astype(jnp.float32)
-    d_normed = d_normed + d_second[...].reshape(rows).astype(jnp.float32)
-    d_normed = d_normed * gains[0:1, :]
+    d_normed = add(d_0[...], d_1[...], d_2[...], d_3[...]).reshape(rows) * gains[0:1, :]
     out = d_residual[...].reshape(rows) + norm_rows_back(d_normed, normed, factor, lane)
     grad_out[...] = out[:, : WIDTH - 1].reshape(2, 64, WIDTH - 1)
 
@@ -613,6 +646,7 @@
         out_shape=[shape for _, shape in outs],
         scratch_shapes=scratch,
         name=name,
+        cost_estimate=pl.CostEstimate(flops=0, transcendentals=0, bytes_accessed=0),
         compiler_params=pltpu.CompilerParams(vmem_limit_bytes=VMEM_BYTES),
     )
 
@@ -634,45 +668,65 @@
     return pick(core, mine, other), pick(core, other, mine)
 
 
+def split_units(w_up, blocks):
+    rows = w_up.shape[0]
+    parts = w_up.reshape(rows, blocks, 2, 2, -1)
+    return [parts[:, :, k].swapaxes(1, 2).reshape(rows, -1) for k in range(2)]
+
+
+def join_units(first, second, blocks):
+    rows = first.shape[0]
+    parts = [half.reshape(rows, 2, blocks, -1).swapaxes(1, 2) for half in (first, second)]
+    return jnp.stack(parts, axis=2).reshape(rows, -1)
+
+
 def on_chip_pair(tokens, segments, cotangent, w_qkv, w_out, w_up, w_down, gain_one, gain_two):
     bf, f32 = jnp.bfloat16, jnp.float32
     device = lax.axis_index("head") * 16 + lax.axis_index("blk")
     core = device % 2
     ids = jnp.stack([device // 2, core]).astype(jnp.int32)
-    micro, _, length, narrow = tokens.shape
     own = jnp.concatenate([tokens[:, 0], segments[:, 0, :, None].astype(bf)], axis=-1)
     cot = jnp.pad(cotangent[:, 0], ((0, 0), (0, 0), (0, 1)))
-    two = jnp.concatenate([own[None], swap(own, AXIS_Z_NEAR)[None]], axis=0)
-    four = jnp.concatenate([two, swap(two, AXIS_Z_FAR, upward(AXIS_Z_FAR))], axis=0)
+    four = jnp.stack(
+        [
+            own,
+            swap(own, AXIS_Z_NEAR, upward(AXIS_Z_NEAR)),
+            swap(own, AXIS_Z_FAR, upward(AXIS_Z_FAR)),
+            swap(own, AXIS_Z_NEAR | AXIS_Z_FAR, upward(AXIS_Z_FAR)),
+        ]
+    )
     eight = jnp.concatenate([four, swap(four, AXIS_X)], axis=0)
     eight_other = swap(eight, CORE)
+    gain_cols = jnp.pad(jnp.stack([gain_one, gain_two], axis=-1), ((0, 0), (0, 126)))
     out_wide = jnp.pad(w_out, ((0, 0), (0, 1)))
     down_wide = jnp.pad(w_down, ((0, 0), (0, 1)))
     qkv_parts = w_qkv.reshape(-1, 3, 2, HALF)
     attn_halves = [
         jnp.concatenate(
-            [qkv_parts[:, 0, k], qkv_parts[:, 1, k], qkv_parts[:, 2, k]]
+            [qkv_parts[:, 0, k], qkv_parts[:, 1, k], qkv_parts[:, 2, k], gain_cols]
             + [out_wide[:, k * HALF : k * HALF + HALF]],
             axis=-1,
         )
         for k in range(2)
     ]
-    gain_cols = jnp.pad(jnp.stack([gain_one, gain_two], axis=-1), ((0, 0), (0, 126)))
-    attn_halves = [
-        jnp.concatenate([half[:, :WIDTH], gain_cols, half[:, WIDTH:]], axis=-1)
-        for half in attn_halves
+    wide = 3 * HALF + 128
+    attn_four = gather_z(chip_block(core, *attn_halves))
+    attn_first = gather_first(attn_four, wide)
+    up_block = chip_block(core, *split_units(w_up, 16))
+    feed_blocks = [
+        jnp.concatenate(
+            [up_block[:, half * WIDTH :][:, :WIDTH], down_wide[half * 48 : half * 48 + 48]], axis=-1
+        )
+        for half in range(2)
     ]
-    attn_block = chip_block(core, *attn_halves)
-    wide = WIDTH + 128
-    unit_rows = w_down.shape[0]
-    up_parts = w_up.reshape(w_up.shape[0], -1, 2, unit_rows)
-    up_halves = [up_parts[:, :, k].reshape(w_up.shape[0], UNITS) for k in range(2)]
-    up_block = chip_block(core, *up_halves)
-    attn_pieces = gather_weights(attn_block[:, :wide], attn_block[:, wide:])
-    up_pieces = gather_weights(up_block[:, :WIDTH], up_block[:, WIDTH:])
-    down_pieces = gather_weights(down_wide[:, :HALF], down_wide[:, HALF:])
+    four_0 = gather_z(fence(feed_blocks[0], *attn_four[1:])[0])
+    four_1 = gather_z(fence(feed_blocks[1], *four_0[1:])[0])
+    attn_pieces = gather_second(*attn_first)
+    first_0 = gather_first(fence(*four_0, *attn_first)[:4], WIDTH)
+    first_1 = gather_first(fence(*four_1, *first_0)[:4], WIDTH)
+    pieces_0 = gather_second(*fence(*first_0, *attn_pieces)[:4])
     cot_other = swap(cot, CORE)
-    attn, query, kv, normed_all, soft, wqk, wvo, wout, own_rows, gains = call(
+    attn, query, kv, normed_all, soft, wqkv, wout, own_rows, gains = call(
         forward_kernel,
         [SMEM] + [ANY] * 6,
         [
@@ -682,7 +736,6 @@
             (VMEM, shaped((2, POSITIONS, WIDTH))),
             (VMEM, shaped((6, ROWS, POSITIONS))),
             (VMEM, shaped((WIDTH, wide))),
-            (VMEM, shaped((WIDTH, WIDTH))),
             (VMEM, shaped((WIDTH, HALF))),
             (VMEM, shaped((ROWS, WIDTH))),
             (VMEM, shaped((8, WIDTH), f32)),
@@ -696,88 +749,111 @@
     )(ids, eight, eight_other, *attn_pieces)
     attn_other = swap(attn, CORE)
     wout_other = swap(wout, CORE)
+    pieces_1 = gather_second(*fence(*first_1, *pieces_0, attn)[:4])
+    weight_scratch = [pltpu.VMEM((WIDTH, WIDTH), bf)] * 4
+    sums_scratch = [pltpu.VMEM((ROWS, WIDTH), f32)] * 2
+    piece_shapes = [(ANY, shaped((8, 48, WIDTH)))] * 4
     outs = call(
-        feed_kernel,
-        [SMEM] + [VMEM] * 8 + [ANY] * 8,
+        feed_first_kernel,
+        [SMEM] + [VMEM] * 8 + [ANY] * 4,
         [
             (VMEM, shaped((ROWS, WIDTH))),
             (VMEM, shaped((ROWS, WIDTH))),
             (VMEM, shaped((ROWS, WIDTH), f32)),
-            (VMEM, shaped((2 * ROWS, WIDTH))),
+            (VMEM, shaped((ROWS, WIDTH))),
+            (VMEM, shaped((ROWS, WIDTH), f32)),
+            (VMEM, shaped((ROWS, WIDTH), f32)),
         ]
-        + [(ANY, shaped((8, 48, WIDTH)))] * 4
-        + [(ANY, shaped((8, 96, HALF)))] * 4,
-        [
-            pltpu.VMEM((WIDTH, WIDTH), bf),
-            pltpu.VMEM((WIDTH, WIDTH), bf),
-            pltpu.VMEM((UNITS, HALF), bf),
-            pltpu.VMEM((UNITS, HALF), bf),
-            pltpu.VMEM((WIDTH, WIDTH), bf),
-            pltpu.VMEM((WIDTH, WIDTH), bf),
-            pltpu.VMEM((UNITS, HALF), bf),
-            pltpu.VMEM((UNITS, HALF), bf),
-            pltpu.VMEM((ROWS, WIDTH), f32),
-            pltpu.VMEM((ROWS, WIDTH), f32),
-            pltpu.SemaphoreType.DMA((64,)),
-        ],
-        "feed_forward_and_back",
+        + piece_shapes,
+        weight_scratch + [pltpu.SemaphoreType.DMA((32,))],
+        "feed_forward_and_back_first",
     )(
-        ids, gains, attn, attn_other, own_rows, wout, wout_other, cot, cot_other,
-        *up_pieces, *down_pieces,
-    )
-    attn_all, cot_all, residual, part = outs[:4]
-    grad_up_pieces, grad_down_pieces = outs[4:8], outs[8:12]
+        ids, gains, attn, attn_other, own_rows, wout, wout_other, cot, cot_other, *pieces_0
+    )
+    attn_all, cot_all, residual, normed_two, sum_mix, sum_norm = outs[:6]
+    feed_0 = reduce_start(outs[6:])
+    part, *grads_1 = call(
+        feed_second_kernel,
+        [SMEM] + [VMEM] * 4 + [ANY] * 4,
+        [(VMEM, shaped((2 * ROWS, WIDTH)))] + piece_shapes,
+        weight_scratch + sums_scratch + [pltpu.SemaphoreType.DMA((32,))],
+        "feed_forward_and_back_second",
+    )(ids, normed_two, cot_all, sum_mix, sum_norm, *pieces_1)
+    feed_0, part, grads_1 = fence(feed_0, part, grads_1)
     part_other = swap(part, CORE)
+    feed_0 = reduce_middle(*feed_0)
+    feed_1 = reduce_start(grads_1)
     outs = call(
         backward_kernel,
-        [SMEM] + [VMEM] * 14,
-        [(VMEM, shaped((2, 64, WIDTH - 1))), (VMEM, shaped((2, 64, WIDTH), f32))]
-        + [(ANY, shaped((8, 48, WIDTH)))] * 4
-        + [(ANY, shaped((8, 2, 64, WIDTH)))] * 2,
+        [SMEM] + [VMEM] * 11,
         [
-            pltpu.VMEM((WIDTH, WIDTH), bf),
-            pltpu.VMEM((WIDTH, WIDTH), bf),
-            pltpu.VMEM((ROWS, HALF), bf),
-            pltpu.VMEM((2, POSITIONS, WIDTH), bf),
+            (VMEM, shaped((2, 64, WIDTH - 1))),
+            (VMEM, shaped((2, 64, WIDTH), f32)),
+            (ANY, shaped((8, 2, 64, WIDTH))),
+            (ANY, shaped((8, 2, 64, WIDTH))),
+            (VMEM, shaped((2, POSITIONS, WIDTH))),
+            (VMEM, shaped((ROWS, HALF))),
+            (VMEM, shaped((ROWS, HALF))),
+        ],
+        [
             pltpu.VMEM((ROWS, HALF), bf),
             pltpu.VMEM((2, POSITIONS, WIDTH), bf),
             pltpu.VMEM((ROWS, WIDTH), bf),
             pltpu.VMEM((ROWS, WIDTH), f32),
-            pltpu.SemaphoreType.DMA((48,)),
+            pltpu.SemaphoreType.DMA((16,)),
         ],
         "attention_backward",
     )(
-        ids, gains, residual, part, part_other, cot_all, attn_all, wout, wout_other, wqk, wvo,
-        query, kv, normed_all, soft,
-    )
-    mixed, d_residual = outs[:2]
-    grad_attn_pieces, keep_rows, send_rows = outs[2:6], outs[6], outs[7]
-    up_sum = reduce_weights(grad_up_pieces)
-    down_sum = reduce_weights(grad_down_pieces)
-    rows_8 = (keep_rows.astype(f32) + swap(send_rows, CORE).astype(f32)).astype(bf)
-    rows_4 = (rows_8[:4].astype(f32) + swap(rows_8[4:], AXIS_X).astype(f32)).astype(bf)
-    rows_2 = rows_4[:2].astype(f32) + swap(rows_4[2:], AXIS_Z_FAR, downward(AXIS_Z_FAR)).astype(f32)
-    rows_2 = rows_2.astype(bf)
-    last_rows = swap(rows_2[1], AXIS_Z_NEAR)
-    attn_sum = reduce_weights(grad_attn_pieces)
+        ids, gains, residual, part, part_other, cot_all, wout, wout_other, wqkv,
+        query, kv, soft,
+    )
+    mixed, d_residual, *outs = outs
+    outs, feed_0, feed_1 = fence(outs, feed_0, feed_1)
+    keep_rows, send_rows, d_kv, d_query, d_sum_half = outs
+    feed_0 = reduce_z(*feed_0)
+    feed_1 = reduce_middle(*feed_1)
+    got_rows = swap(send_rows, CORE)
+    grad_attn_pieces = call(
+        gradient_kernel,
+        [SMEM] + [VMEM] * 5,
+        [(ANY, shaped((8, 48, 3 * HALF)))] * 2 + [(ANY, shaped((8, 48, HALF)))] * 2,
+        [
+            pltpu.VMEM((WIDTH, 3 * HALF), bf),
+            pltpu.VMEM((WIDTH, HALF), bf),
+            pltpu.SemaphoreType.DMA((32,)),
+        ],
+        "attention_weight_gradients",
+    )(ids, attn_all, d_sum_half, d_query, d_kv, normed_all)
+    keep_rows, got_rows, grad_attn_pieces, feed_0, feed_1 = fence(
+        keep_rows, got_rows, grad_attn_pieces, feed_0, feed_1
+    )
+    crossed = swap(add(keep_rows[4:], got_rows[4:]).astype(bf), AXIS_X)
+    attn_first = reduce_start(grad_attn_pieces)
+    feed_1 = reduce_z(*feed_1)
+    feed_1, crossed, attn_first = fence(feed_1, crossed, attn_first)
+    rows_4 = add(keep_rows[:4], got_rows[:4], crossed).astype(bf)
+    to_near = swap(rows_4[1], AXIS_Z_NEAR, downward(AXIS_Z_NEAR))
+    to_far = swap(rows_4[2], AXIS_Z_FAR, downward(AXIS_Z_FAR))
+    to_end = swap(rows_4[3], AXIS_Z_NEAR | AXIS_Z_FAR, downward(AXIS_Z_FAR))
+    attn_last = reduce_z(*reduce_middle(*attn_first))
+    sum_0, sum_1, attn_sum = add(*feed_0), add(*feed_1), add(*attn_last)
     (grad_tokens,) = call(
         tail_kernel,
-        [VMEM] * 5,
+        [VMEM] * 7,
         [(VMEM, shaped((2, 64, WIDTH - 1), f32))],
         [],
         "token_gradient",
-    )(gains, own, rows_2[0], last_rows, d_residual)
+    )(gains, own, rows_4[0], to_near, to_far, to_end, d_residual)
     attn_0, attn_1 = core_rows(core, attn_sum)
+    up_sum = jnp.concatenate([sum_0[:, :WIDTH], sum_1[:, :WIDTH]], axis=-1)
     up_0, up_1 = core_rows(core, up_sum)
     grad_qkv = jnp.concatenate(
         [half[:, k * HALF : k * HALF + HALF] for k in range(3) for half in (attn_0, attn_1)],
         axis=-1,
     )
     grad_out = jnp.concatenate([attn_0[:, 3 * HALF :], attn_1[:, 3 * HALF : 4 * HALF - 1]], axis=-1)
-    rows = up_0.shape[0]
-    grad_up = jnp.stack(
-        [up_0.reshape(rows, -1, unit_rows), up_1.reshape(rows, -1, unit_rows)], axis=2
-    ).reshape(rows, -1)
+    grad_up = join_units(up_0, up_1, 16)
+    grad_down = jnp.concatenate([sum_0[:, WIDTH:], sum_1[:, WIDTH:]], axis=0)
     grad_gain_one = jnp.sum(grad_qkv * w_qkv.astype(f32), axis=-1) / gain_one.astype(f32)
     grad_gain_two = jnp.sum(grad_up * w_up.astype(f32), axis=-1) / gain_two.astype(f32)
     return (
@@ -786,7 +862,7 @@
         grad_qkv,
         grad_out,
         grad_up,
-        down_sum[:, : WIDTH - 1],
+        grad_down[:, : WIDTH - 1],
         grad_gain_one,
         grad_gain_two,
     )

time: 327 us -> 266 us (0.81)
  waiting for transfers between devices: 152 us -> 86 us
  starting transfers between devices: 86.8 us -> 74 us
  Pallas kernels: 56.5 us -> 64.4 us
  other arithmetic: 16.5 us -> 21.9 us
    ppermute x52 -> x60, waiting for transfers between devices: 152 us -> 86 us  [swap(): return lax.ppermute(array, ('head', 'blk'), pairs)]
    ppermute x52 -> x60, starting transfers between devices: 86.8 us -> 74 us  [swap(): return lax.ppermute(array, ('head', 'blk'), pairs)]
    pallas_call x3 -> x5, Pallas kernels: 39.3 us -> 48.1 us  [the longest x1 19.1 us: on_chip_pair(): call(backward_kernel, [SMEM] + [VMEM] * 11, [(VMEM, shaped((2, 64, WIDTH...]
    another operation x7 -> x14, other arithmetic: 4.31 us -> 8.16 us
    unnamed x76 -> x113, local copies, waits for them, and re-layouts: 3.93 us -> 7.01 us
  transfers between devices with their start and end apart: 52 -> 60, of which waited for: 22 -> 22; matrix products, arithmetic and copies ran while one was open for 7% -> 11% of each run, Pallas kernels for 12% -> 24%
where the time goes in v2:
time: 266 us; the launch traced here: 265 us
  waiting for transfers between devices  86 us (32%)
  starting transfers between devices  74 us (28%)
  Pallas kernels  64.4 us (24%)
  other arithmetic  21.9 us (8%)
  local copies, waits for them, and re-layouts  16.1 us (6%)
    ppermute x60, waiting for transfers between devices, swap(): return lax.ppermute(array, ('head', 'blk'), pairs)  86 us
    ppermute x60, starting transfers between devices, swap(): return lax.ppermute(array, ('head', 'blk'), pairs)  74 us
    pallas_call x1, Pallas kernels, on_chip_pair(): call(backward_kernel, [SMEM] + [VMEM] * 11, [(VMEM, shaped((2, 64, WIDTH...  19.1 us
    pallas_call x1, Pallas kernels, on_chip_pair(): call(forward_kernel, [SMEM] + [ANY] * 6, [(VMEM, shaped((ROWS, HALF))), (...  16.3 us
    pallas_call x1, Pallas kernels, on_chip_pair(): call(feed_first_kernel, [SMEM] + [VMEM] * 8 + [ANY] * 4, [(VMEM, shaped((...  9.93 us
    pallas_call x1, Pallas kernels, on_chip_pair(): call(feed_second_kernel, [SMEM] + [VMEM] * 4 + [ANY] * 4, [(VMEM, shaped(...  8.42 us
    pallas_call x1, Pallas kernels, on_chip_pair(): call(gradient_kernel, [SMEM] + [VMEM] * 5, [(ANY, shaped((8, 48, 3 * HALF...  8.07 us
    another operation x6, other arithmetic  7.02 us
  transfers between devices with their start and end apart: 60, of which 22 were waited for; matrix products, arithmetic and copies ran while one was open for 11% of the time, Pallas kernels for 24%

profile of v2, /device:TPU:0, one launch (start us, length us, event | category | flops | bytes accessed | tf_op | source)
XLA Modules:
  0.0 264.5 jit_solution(13596919064036697068)
XLA Ops:
  2.5 7.0 %collective-permute-start.2 = (bf16[2,64,768]{2,1,0:T(8,128)(2,1)S(1)}, bf16[2,64,768]{2,1,0:T(8,128)(2,1)S(1)}, u32[]{:S(2)}, u32[]{:S(2)}) collective-permute-start(bf16[2,64,768]{2,1,0:T(8,128)(2,1)S(1)} %get-tuple-element.241.tokens), channel_id=1, source_target_pairs={{0,12},{1,13},{2,14},{3,15},{4,8},{5,9},{6,10},{7,11},{16,28},{17,... | collective-permute-start | bytes 589832 | tf_op jit(solution)/shard_map/ppermute | solution.py:252
  9.5 1.3 collective-permute-start.1
  10.8 2.5 collective-permute-start
  18.2 5.0 %collective-permute-done = bf16[2,64,768]{2,1,0:T(8,128)(2,1)S(1)} collective-permute-done((bf16[2,64,768]{2,1,0:T(8,128)(2,1)S(1)}, bf16[2,64,768]{2,1,0:T(8,128)(2,1)S(1)}, u32[]{:S(2)}, u32[]{:S(2)}) %collective-permute-start) | collective-permute-done | bytes 196640 | tf_op jit(solution)/shard_map/ppermute | solution.py:252
  23.4 4.8 %collective-permute-done.7 = bf16[48,1664]{1,0:T(8,128)(2,1)S(1)} collective-permute-done((bf16[48,1664]{1,0:T(8,128)(2,1)S(1)}, bf16[48,1664]{1,0:T(8,128)(2,1)S(1)}, u32[]{:S(2)}, u32[]{:S(2)}) %collective-permute-start.7) | collective-permute-done | bytes 159776 | tf_op jit(solution)/shard_map/ppermute | solution.py:252
  28.3 3.1 %collective-permute-done.6 = bf16[48,1664]{1,0:T(8,128)(2,1)S(1)} collective-permute-done((bf16[48,1664]{1,0:T(8,128)(2,1)S(1)}, bf16[48,1664]{1,0:T(8,128)(2,1)S(1)}, u32[]{:S(2)}, u32[]{:S(2)}) %collective-permute-start.6) | collective-permute-done | bytes 159776 | tf_op jit(solution)/shard_map/ppermute | solution.py:252
  31.4 1.1 collective-permute-done.8
  32.5 7.6 %collective-permute-start.19 = (bf16[48,1536]{1,0:T(8,128)(2,1)S(1)}, bf16[48,1536]{1,0:T(8,128)(2,1)S(1)}, u32[]{:S(2)}, u32[]{:S(2)}) collective-permute-start(bf16[48,1536]{1,0:T(8,128)(2,1)S(1)} %pad_maximum_fusion.16), channel_id=1, source_target_pairs={{0,12},{1,13},{2,14},{3,15},{4,8},{5,9},{6,10},{7,11},{8,4},{9,5},... | collective-permute-start | bytes 442376 | tf_op jit(solution)/shard_map/ppermute | solution.py:252
  40.1 1.4 collective-permute-start.18
  42.1 1.6 collective-permute-start.11
  43.8 1.6 collective-permute-start.9
  46.0 6.3 %collective-permute-done.18 = bf16[48,1536]{1,0:T(8,128)(2,1)S(1)} collective-permute-done((bf16[48,1536]{1,0:T(8,128)(2,1)S(1)}, bf16[48,1536]{1,0:T(8,128)(2,1)S(1)}, u32[]{:S(2)}, u32[]{:S(2)}) %collective-permute-start.18) | collective-permute-done | bytes 147488 | tf_op jit(solution)/shard_map/ppermute | solution.py:252
  52.3 2.7 %collective-permute-start.28 = (bf16[48,1536]{1,0:T(8,128)(2,1)S(1)}, bf16[48,1536]{1,0:T(8,128)(2,1)S(1)}, u32[]{:S(2)}, u32[]{:S(2)}) collective-permute-start(bf16[48,1536]{1,0:T(8,128)(2,1)S(1)} %fusion.24), channel_id=1, source_target_pairs={{0,12},{1,13},{2,14},{3,15},{4,8},{5,9},{6,10},{7,11},{8,4},{9,5},... | collective-permute-start | bytes 442376 | tf_op jit(solution)/shard_map/ppermute | solution.py:252
  55.0 3.0 %collective-permute-done.9 = bf16[4,48,1280]{2,1,0:T(8,128)(2,1)S(1)} collective-permute-done((bf16[4,48,1280]{2,1,0:T(8,128)(2,1)S(1)}, bf16[4,48,1280]{2,1,0:T(8,128)(2,1)S(1)}, u32[]{:S(2)}, u32[]{:S(2)}) %collective-permute-start.9) | collective-permute-done | bytes 491552 | tf_op jit(solution)/shard_map/ppermute | solution.py:252
  58.1 1.6 collective-permute-start.20
  60.3 1.6 collective-permute-start.10
  61.9 3.0 %collective-permute-start.27 = (bf16[48,1536]{1,0:T(8,128)(2,1)S(1)}, bf16[48,1536]{1,0:T(8,128)(2,1)S(1)}, u32[]{:S(2)}, u32[]{:S(2)}) collective-permute-start(bf16[48,1536]{1,0:T(8,128)(2,1)S(1)} %fusion.24), channel_id=1, source_target_pairs={{0,8},{1,9},{2,10},{3,11},{4,12},{5,13},{6,14},{7,15},{8,0},{9,1},... | collective-permute-start | bytes 442376 | tf_op jit(solution)/shard_map/ppermute | solution.py:252
  64.9 9.9 %collective-permute-done.3 = bf16[4,2,64,768]{3,2,1,0:T(8,128)(2,1)S(1)} collective-permute-done((bf16[4,2,64,768]{3,2,1,0:T(8,128)(2,1)S(1)}, bf16[4,2,64,768]{3,2,1,0:T(8,128)(2,1)S(1)}, u32[]{:S(2)}, u32[]{:S(2)}) %collective-permute-start.3) | collective-permute-done | bytes 786464 | tf_op jit(solution)/shard_map/ppermute | solution.py:252
  74.8 1.5 collective-permute-start.26
  76.4 1.6 collective-permute-start.12
  78.0 2.0 collective-permute-done.26
  80.0 1.2 collective-permute-done.20
  81.2 3.3 %collective-permute-done.12.w3 = bf16[8,48,384]{2,1,0:T(8,128)(2,1)S(1)} collective-permute-done((bf16[8,48,384]{2,1,0:T(8,128)(2,1)S(1)}, bf16[8,48,384]{2,1,0:T(8,128)(2,1)S(1)}, u32[]{:S(2)}, u32[]{:S(2)}) %collective-permute-start.12) | collective-permute-done | bytes 294944 | tf_op jit(solution)/shard_map/ppermute | solution.py:252
  89.1 1.2 collective-permute-start.22
  90.4 1.6 collective-permute-start.29
  93.9 1.2 copy-done.4
  95.0 16.3 %attention_forward.1 = (bf16[256,384]{1,0:T(8,128)(2,1)}, bf16[256,384]{1,0:T(8,128)(2,1)}, bf16[2,1024,768]{2,1,0:T(8,128)(2,1)}, bf16[2,1024,768]{2,1,0:T(8,12...) custom-call(s32[2]{0:T(128)} %pad_add_fusion.ids, ...), custom_call_target="tpu_custom_call" | custom-call | tf_op jit(solution)/shard_map/attention_forward/pallas_call | solution.py:729
  116.0 1.3 collective-permute-start.31
  118.3 9.9 %feed_forward_and_back_first.1 = (bf16[256,768]{1,0:T(8,128)(2,1)}, bf16[256,768]{1,0:T(8,128)(2,1)}, f32[256,768]{1,0:T(8,128)}, bf16[256,768]{1,0:T(8,128)(2,1...) custom-call(s32[2]{0:T(128)} %pad_add_fusion.ids, ...), custom_call_target="tpu_custom_call" | custom-call | tf_op jit(solution)/shard_map/feed_forward_and_back_first/pallas_call | solution.py:756
  129.1 1.2 collective-permute-start.25
  130.3 1.7 collective-permute-done.31.w1
  132.0 8.4 %feed_forward_and_back_second.1 = (bf16[512,768]{1,0:T(8,128)(2,1)}, bf16[8,48,768]{2,1,0:T(8,128)(2,1)}, bf16[8,48,768]{2,1,0:T(8,128)(2,1)}, bf16[8,48,768]{2,1,0:T(8,128)(2,1)}, bf16[8,48,768]{2,1,0:T(8,128)(2,1)}) custom-call(s32[2]{0:T(128)} %pad_add_fusion.ids, bf16[256,768]{1,0:T(8,128)(2,1)} %get-tuple-element.128.normed, ...), custom_call_target="tpu_custom_call" | custom-call | tf_op jit(solution)/shard_map/feed_forward_and_back_second/pallas_call | solution.py:775
  140.4 3.7 %collective-permute-done.24 = bf16[8,48,768]{2,1,0:T(8,128)(2,1)S(1)} collective-permute-done((bf16[8,48,768]{2,1,0:T(8,128)(2,1)}, bf16[8,48,768]{2,1,0:T(8,128)(2,1)S(1)}, u32[]{:S(2)}, u32[]{:S(2)}) %collective-permute-start.24) | collective-permute-done | bytes 589856 | tf_op jit(solution)/shard_map/ppermute | solution.py:252
  144.1 1.3 collective-permute-start.36
  145.4 1.5 collective-permute-start.37
  146.9 1.0 add_convert_fusion.10
  148.7 1.7 add_convert_fusion.11
  152.3 19.1 %attention_backward.1 = (bf16[2,64,767]{2,1,0:T(8,128)(2,1)}, f32[2,64,768]{2,1,0:T(8,128)}, bf16[8,2,64,768]{3,2,1,0:T(8,128)(2,1)}, bf16[8,2,64,768]{3,2,1,0:T...) custom-call(s32[2]{0:T(128)} %pad_add_fusion.ids, ...), custom_call_target="tpu_custom_call" | custom-call | tf_op jit(solution)/shard_map/attention_backward/pallas_call | solution.py:786
  171.5 1.5 add_convert_fusion.9
  173.1 1.1 add_convert_fusion.8
  174.9 2.4 collective-permute-start.41
  179.5 1.5 collective-permute-start.42
  181.0 1.7 collective-permute-done.41
  182.6 3.9 %collective-permute-start.40 = (bf16[48,1536]{1,0:T(8,128)(2,1)S(1)}, bf16[48,1536]{1,0:T(8,128)(2,1)}, u32[]{:S(2)}, u32[]{:S(2)}) collective-permute-start(bf16[48,1536]{1,0:T(8,128)(2,1)S(1)} %get-tuple-element.256), channel_id=1, source_target_pairs={{0,8},{1,9},{2,10},{3,11},{4,12},{5,13},{6,14},{7,15},{8,0},{9,1},... | collective-permute-start | bytes 442376 | tf_op jit(solution)/shard_map/ppermute | solution.py:252
  186.6 8.1 %attention_weight_gradients.1 = (bf16[8,48,1152]{2,1,0:T(8,128)(2,1)}, bf16[8,48,1152]{2,1,0:T(8,128)(2,1)}, bf16[8,48,384]{2,1,0:T(8,128)(2,1)}, bf16[8,48,384]{2,1,0:T(8,128)(2,1)}) custom-call(s32[2]{0:T(128)} %pad_add_fusion.ids, bf16[256,768]{1,0:T(8,128)(2,1)} %get-tuple-element.167.attn, bf16[256,384]{1,0:T(8,128)(2,1)} %get-tuple-element.168.d_sum_half, ...), custom_call_target="tpu_custom_call" | custom-call | tf_op jit(solution)/shard_map/attention_weight_gradients/pallas_call | solution.py:816
  196.4 1.1 add_convert_fusion.5
  197.5 1.1 add_convert_fusion.4
  198.6 1.2 collective-permute-start.46
  199.9 1.2 collective-permute-start.49
  201.1 1.1 convert_add_fusion.2
  202.1 5.1 %collective-permute-done.46 = bf16[48,1536]{1,0:T(8,128)(2,1)S(1)} collective-permute-done((bf16[48,1536]{1,0:T(8,128)(2,1)S(1)}, bf16[48,1536]{1,0:T(8,128)(2,1)S(1)}, u32[]{:S(2)}, u32[]{:S(2)}) %collective-permute-start.46) | collective-permute-done | bytes 147488 | tf_op jit(solution)/shard_map/ppermute | solution.py:252
  207.3 6.0 %collective-permute-done.45 = bf16[48,1536]{1,0:T(8,128)(2,1)S(1)} collective-permute-done((bf16[48,1536]{1,0:T(8,128)(2,1)S(1)}, bf16[48,1536]{1,0:T(8,128)(2,1)S(1)}, u32[]{:S(2)}, u32[]{:S(2)}) %collective-permute-start.45) | collective-permute-done | bytes 147488 | tf_op jit(solution)/shard_map/ppermute | solution.py:252
  213.3 6.7 %collective-permute-done.49 = bf16[8,48,384]{2,1,0:T(8,128)(2,1)S(1)} collective-permute-done((bf16[8,48,384]{2,1,0:T(8,128)(2,1)S(1)}, bf16[8,48,384]{2,1,0:T(8,128)(2,1)S(1)}, u32[]{:S(2)}, u32[]{:S(2)}) %collective-permute-start.49) | collective-permute-done | bytes 294944 | tf_op jit(solution)/shard_map/ppermute | solution.py:252
  222.7 1.3 collective-permute-start.52
  224.0 1.3 collective-permute-start.51
  227.7 1.0 add_convert_fusion.12
  228.8 9.6 %collective-permute-done.53 = bf16[4,48,1152]{2,1,0:T(8,128)(2,1)} collective-permute-done((bf16[4,48,1152]{2,1,0:T(8,128)(2,1)S(1)}, bf16[4,48,1152]{2,1,0:T(8,128)(2,1)}, u32[]{:S(2)}, u32[]{:S(2)}) %collective-permute-start.53) | collective-permute-done | bytes 442400 | tf_op jit(solution)/shard_map/ppermute | solution.py:252
  238.4 1.2 add_convert_fusion.2
  239.7 5.8 %collective-permute-start.57 = (bf16[48,1536]{1,0:T(8,128)(2,1)S(1)}, bf16[48,1536]{1,0:T(8,128)(2,1)S(1)}, u32[]{:S(2)}, u32[]{:S(2)}) collective-permute-start(bf16[48,1536]{1,0:T(8,128)(2,1)S(1)} %get-tuple-element.247), channel_id=1, source_target_pairs={{0,12},{1,13},{2,14},{3,15},{4,8},{5,9},{6,10},{7,11},{8,4},{9,5},... | collective-permute-start | bytes 442376 | tf_op jit(solution)/shard_map/ppermute | solution.py:252
  246.5 1.1 reshape.60
  247.8 1.3 collective-permute-start.50
  249.1 4.3 %collective-permute-done.57 = bf16[48,1536]{1,0:T(8,128)(2,1)S(1)} collective-permute-done((bf16[48,1536]{1,0:T(8,128)(2,1)S(1)}, bf16[48,1536]{1,0:T(8,128)(2,1)S(1)}, u32[]{:S(2)}, u32[]{:S(2)}) %collective-permute-start.57) | collective-permute-done | bytes 147488 | tf_op jit(solution)/shard_map/ppermute | solution.py:252
  253.4 5.6 %collective-permute-done.56 = bf16[48,1536]{1,0:T(8,128)(2,1)S(1)} collective-permute-done((bf16[48,1536]{1,0:T(8,128)(2,1)S(1)}, bf16[48,1536]{1,0:T(8,128)(2,1)S(1)}, u32[]{:S(2)}, u32[]{:S(2)}) %collective-permute-start.56) | collective-permute-done | bytes 147488 | tf_op jit(solution)/shard_map/ppermute | solution.py:252
  260.4 2.6 token_gradient.1
  (281 shorter events, 38.2 us)
Async XLA Ops:
  2.5 20.8 %copy-start.2 = (bf16[2,64,768]{2,1,0:T(8,128)(2,1)}, bf16[2,64,768]{2,1,0:T(8,128)(2,1)S(1)}, u32[]{:S(2)}) copy-start(bf16[2,64,768]{2,1,0:T(8,128)(2,1)S(1)} %get-tuple-element.241.tokens) | copy-start | bytes 589828
  2.5 20.8 %collective-permute-start.2 = (bf16[2,64,768]{2,1,0:T(8,128)(2,1)S(1)}, bf16[2,64,768]{2,1,0:T(8,128)(2,1)S(1)}, u32[]{:S(2)}, u32[]{:S(2)}) collective-permute-start(bf16[2,64,768]{2,1,0:T(8,128)(2,1)S(1)} %get-tuple-element.241.tokens), channel_id=1, source_target_pairs={{0,12},{1,13},{2,14},{3,15},{4,8},{5,9},{6,10},{7,11},{16,28},{17,... | collective-permute-start | bytes 589832 | tf_op jit(solution)/shard_map/ppermute | solution.py:252
  9.5 13.8 %collective-permute-start.1 = (bf16[2,64,768]{2,1,0:T(8,128)(2,1)S(1)}, bf16[2,64,768]{2,1,0:T(8,128)(2,1)S(1)}, u32[]{:S(2)}, u32[]{:S(2)}) collective-permute-start(bf16[2,64,768]{2,1,0:T(8,128)(2,1)S(1)} %get-tuple-element.241.tokens), channel_id=1, source_target_pairs={{0,8},{1,9},{2,10},{3,11},{4,12},{5,13},{6,14},{7,15},{16,24},{17,... | collective-permute-start | bytes 589832 | tf_op jit(solution)/shard_map/ppermute | solution.py:252
  10.8 12.4 %collective-permute-start = (bf16[2,64,768]{2,1,0:T(8,128)(2,1)S(1)}, bf16[2,64,768]{2,1,0:T(8,128)(2,1)S(1)}, u32[]{:S(2)}, u32[]{:S(2)}) collective-permute-start(bf16[2,64,768]{2,1,0:T(8,128)(2,1)S(1)} %get-tuple-element.241.tokens), channel_id=1, source_target_pairs={{0,4},{1,5},{2,6},{3,7},{8,12},{9,13},{10,14},{11,15},{16,20},{17,... | collective-permute-start | bytes 589832 | tf_op jit(solution)/shard_map/ppermute | solution.py:252
  15.3 2.6 collective-permute-start.5
  16.4 1.5 collective-permute-start.16
  18.0 10.3 %collective-permute-start.7 = (bf16[48,1664]{1,0:T(8,128)(2,1)S(1)}, bf16[48,1664]{1,0:T(8,128)(2,1)S(1)}, u32[]{:S(2)}, u32[]{:S(2)}) collective-permute-start(bf16[48,1664]{1,0:T(8,128)(2,1)S(1)} %pad_maximum_fusion.8), channel_id=1, source_target_pairs={{0,8},{1,9},{2,10},{3,11},{4,12},{5,13},{6,14},{7,15},{8,0},{9,1},... | collective-permute-start | bytes 479240 | tf_op jit(solution)/shard_map/ppermute | solution.py:252
  18.1 13.3 %collective-permute-start.6 = (bf16[48,1664]{1,0:T(8,128)(2,1)S(1)}, bf16[48,1664]{1,0:T(8,128)(2,1)S(1)}, u32[]{:S(2)}, u32[]{:S(2)}) collective-permute-start(bf16[48,1664]{1,0:T(8,128)(2,1)S(1)} %pad_maximum_fusion.8), channel_id=1, source_target_pairs={{0,4},{1,5},{2,6},{3,7},{4,0},{5,1},{6,2},{7,3},{8,12},{9,13},{10,... | collective-permute-start | bytes 479240 | tf_op jit(solution)/shard_map/ppermute | solution.py:252
  23.2 9.3 %collective-permute-start.8 = (bf16[48,1664]{1,0:T(8,128)(2,1)S(1)}, bf16[48,1664]{1,0:T(8,128)(2,1)S(1)}, u32[]{:S(2)}, u32[]{:S(2)}) collective-permute-start(bf16[48,1664]{1,0:T(8,128)(2,1)S(1)} %pad_maximum_fusion.8), channel_id=1, source_target_pairs={{0,12},{1,13},{2,14},{3,15},{4,8},{5,9},{6,10},{7,11},{8,4},{9,5},... | collective-permute-start | bytes 479240 | tf_op jit(solution)/shard_map/ppermute | solution.py:252
  32.5 12.9 %collective-permute-start.19 = (bf16[48,1536]{1,0:T(8,128)(2,1)S(1)}, bf16[48,1536]{1,0:T(8,128)(2,1)S(1)}, u32[]{:S(2)}, u32[]{:S(2)}) collective-permute-start(bf16[48,1536]{1,0:T(8,128)(2,1)S(1)} %pad_maximum_fusion.16), channel_id=1, source_target_pairs={{0,12},{1,13},{2,14},{3,15},{4,8},{5,9},{6,10},{7,11},{8,4},{9,5},... | collective-permute-start | bytes 442376 | tf_op jit(solution)/shard_map/ppermute | solution.py:252
  40.1 12.2 %collective-permute-start.18 = (bf16[48,1536]{1,0:T(8,128)(2,1)S(1)}, bf16[48,1536]{1,0:T(8,128)(2,1)S(1)}, u32[]{:S(2)}, u32[]{:S(2)}) collective-permute-start(bf16[48,1536]{1,0:T(8,128)(2,1)S(1)} %pad_maximum_fusion.16), channel_id=1, source_target_pairs={{0,8},{1,9},{2,10},{3,11},{4,12},{5,13},{6,14},{7,15},{8,0},{9,1},... | collective-permute-start | bytes 442376 | tf_op jit(solution)/shard_map/ppermute | solution.py:252
  41.4 10.9 %collective-permute-start.17 = (bf16[48,1536]{1,0:T(8,128)(2,1)S(1)}, bf16[48,1536]{1,0:T(8,128)(2,1)S(1)}, u32[]{:S(2)}, u32[]{:S(2)}) collective-permute-start(bf16[48,1536]{1,0:T(8,128)(2,1)S(1)} %pad_maximum_fusion.16), channel_id=1, source_target_pairs={{0,4},{1,5},{2,6},{3,7},{4,0},{5,1},{6,2},{7,3},{8,12},{9,13},{10,... | collective-permute-start | bytes 442376 | tf_op jit(solution)/shard_map/ppermute | solution.py:252
  42.1 12.9 %collective-permute-start.11 = (bf16[4,48,384]{2,1,0:T(8,128)(2,1)S(1)}, bf16[4,48,384]{2,1,0:T(8,128)(2,1)S(1)}, u32[]{:S(2)}, u32[]{:S(2)}) collective-permute-start(bf16[4,48,384]{2,1,0:T(8,128)(2,1)S(1)} %pad_maximum_fusion.15), channel_id=1, source_target_pairs={{0,16},{1,17},{2,18},{3,19},{4,20},{5,21},{6,22},{7,23},{8,24},{9,... | collective-permute-start | bytes 442376 | tf_op jit(solution)/shard_map/ppermute | solution.py:252
  43.8 14.2 %collective-permute-start.9 = (bf16[4,48,1280]{2,1,0:T(8,128)(2,1)S(1)}, bf16[4,48,1280]{2,1,0:T(8,128)(2,1)S(1)}, u32[]{:S(2)}, u32[]{:S(2)}) collective-permute-start(bf16[4,48,1280]{2,1,0:T(8,128)(2,1)S(1)} %pad_maximum_fusion.2), channel_id=1, source_target_pairs={{0,2},{1,3},{2,0},{3,1},{4,6},{5,7},{6,4},{7,5},{8,10},{9,11},{10,... | collective-permute-start | bytes 1474568 | tf_op jit(solution)/shard_map/ppermute | solution.py:252
  45.4 29.4 %collective-permute-start.3 = (bf16[4,2,64,768]{3,2,1,0:T(8,128)(2,1)S(1)}, bf16[4,2,64,768]{3,2,1,0:T(8,128)(2,1)S(1)}, u32[]{:S(2)}, u32[]{:S(2)}) collective-permute-start(bf16[4,2,64,768]{3,2,1,0:T(8,128)(2,1)S(1)} %pad_maximum_fusion), channel_id=1, source_target_pairs={{0,2},{1,3},{2,0},{3,1},{4,6},{5,7},{6,4},{7,5},{8,10},{9,11},{10,... | collective-permute-start | bytes 2359304 | tf_op jit(solution)/shard_map/ppermute | solution.py:252
  52.3 9.6 %collective-permute-start.28 = (bf16[48,1536]{1,0:T(8,128)(2,1)S(1)}, bf16[48,1536]{1,0:T(8,128)(2,1)S(1)}, u32[]{:S(2)}, u32[]{:S(2)}) collective-permute-start(bf16[48,1536]{1,0:T(8,128)(2,1)S(1)} %fusion.24), channel_id=1, source_target_pairs={{0,12},{1,13},{2,14},{3,15},{4,8},{5,9},{6,10},{7,11},{8,4},{9,5},... | collective-permute-start | bytes 442376 | tf_op jit(solution)/shard_map/ppermute | solution.py:252
  58.1 23.0 %collective-permute-start.20 = (bf16[4,48,768]{2,1,0:T(8,128)(2,1)S(1)}, bf16[4,48,768]{2,1,0:T(8,128)(2,1)S(1)}, u32[]{:S(2)}, u32[]{:S(2)}) collective-permute-start(bf16[4,48,768]{2,1,0:T(8,128)(2,1)S(1)} %pad_maximum_fusion.4), channel_id=1, source_target_pairs={{0,2},{1,3},{2,0},{3,1},{4,6},{5,7},{6,4},{7,5},{8,10},{9,11},{10,... | collective-permute-start | bytes 884744 | tf_op jit(solution)/shard_map/ppermute | solution.py:252
  59.7 21.5 %collective-permute-start.21 = (bf16[4,48,768]{2,1,0:T(8,128)(2,1)S(1)}, bf16[4,48,768]{2,1,0:T(8,128)(2,1)S(1)}, u32[]{:S(2)}, u32[]{:S(2)}) collective-permute-start(bf16[4,48,768]{2,1,0:T(8,128)(2,1)S(1)} %pad_maximum_fusion.5), channel_id=1, source_target_pairs={{0,16},{1,17},{2,18},{3,19},{4,20},{5,21},{6,22},{7,23},{8,24},{9,... | collective-permute-start | bytes 884744 | tf_op jit(solution)/shard_map/ppermute | solution.py:252
  60.3 25.7 %copy-start.7 = (bf16[8,48,1280]{2,1,0:T(8,128)(2,1)}, bf16[8,48,1280]{2,1,0:T(8,128)(2,1)S(1)}, u32[]{:S(2)}) copy-start(bf16[8,48,1280]{2,1,0:T(8,128)(2,1)S(1)} %constant_dynamic-update-slice_fusion.15.w0) | copy-start | bytes 2949124
  60.3 24.9 %collective-permute-start.10 = (bf16[8,48,1280]{2,1,0:T(8,128)(2,1)S(1)}, bf16[8,48,1280]{2,1,0:T(8,128)(2,1)S(1)}, u32[]{:S(2)}, u32[]{:S(2)}) collective-permute-start(bf16[8,48,1280]{2,1,0:T(8,128)(2,1)S(1)} %constant_dynamic-update-slice_fusion.15.w0), channel_id=1, source_target_pairs={{0,16},{1,17},{2,18},{3,19},{4,20},{5,21},{6,22},{7,23},{8,24},{9,... | collective-permute-start | bytes 2949128 | tf_op jit(solution)/shard_map/ppermute | solution.py:252
  61.9 14.5 %collective-permute-start.27 = (bf16[48,1536]{1,0:T(8,128)(2,1)S(1)}, bf16[48,1536]{1,0:T(8,128)(2,1)S(1)}, u32[]{:S(2)}, u32[]{:S(2)}) collective-permute-start(bf16[48,1536]{1,0:T(8,128)(2,1)S(1)} %fusion.24), channel_id=1, source_target_pairs={{0,8},{1,9},{2,10},{3,11},{4,12},{5,13},{6,14},{7,15},{8,0},{9,1},... | collective-permute-start | bytes 442376 | tf_op jit(solution)/shard_map/ppermute | solution.py:252
  74.8 5.1 %collective-permute-start.26 = (bf16[48,1536]{1,0:T(8,128)(2,1)S(1)}, bf16[48,1536]{1,0:T(8,128)(2,1)S(1)}, u32[]{:S(2)}, u32[]{:S(2)}) collective-permute-start(bf16[48,1536]{1,0:T(8,128)(2,1)S(1)} %fusion.24), channel_id=1, source_target_pairs={{0,4},{1,5},{2,6},{3,7},{4,0},{5,1},{6,2},{7,3},{8,12},{9,13},{10,... | collective-permute-start | bytes 442376 | tf_op jit(solution)/shard_map/ppermute | solution.py:252
  76.4 8.1 %collective-permute-start.12 = (bf16[8,48,384]{2,1,0:T(8,128)(2,1)S(1)}, bf16[8,48,384]{2,1,0:T(8,128)(2,1)S(1)}, u32[]{:S(2)}, u32[]{:S(2)}) collective-permute-start(bf16[8,48,384]{2,1,0:T(8,128)(2,1)S(1)} %constant_dynamic-update-slice_fusion.20.w2), channel_id=1, source_target_pairs={{0,2},{1,3},{2,0},{3,1},{4,6},{5,7},{6,4},{7,5},{8,10},{9,11},{10,... | collective-permute-start | bytes 884744 | tf_op jit(solution)/shard_map/ppermute | solution.py:252
  80.0 13.9 %collective-permute-start.4 = (bf16[8,2,64,768]{3,2,1,0:T(8,128)(2,1)S(1)}, bf16[8,2,64,768]{3,2,1,0:T(8,128)(2,1)S(1)}, u32[]{:S(2)}, u32[]{:S(2)}) collective-permute-start(bf16[8,2,64,768]{3,2,1,0:T(8,128)(2,1)S(1)} %constant_dynamic-update-slice_fusion.tok_mine), channel_id=1, source_target_pairs={{0,1},{1,0},{2,3},{3,2},{4,5},{5,4},{6,7},{7,6},{8,9},{9,8},{10,11... | collective-permute-start | bytes 4718600 | tf_op jit(solution)/shard_map/ppermute | solution.py:252
  86.8 25.3 %collective-permute-start.23 = (bf16[8,48,768]{2,1,0:T(8,128)(2,1)}, bf16[8,48,768]{2,1,0:T(8,128)(2,1)}, u32[]{:S(2)}, u32[]{:S(2)}) collective-permute-start(bf16[8,48,768]{2,1,0:T(8,128)(2,1)} %constant_dynamic-update-slice_fusion.27.w2), channel_id=1, source_target_pairs={{0,2},{1,3},{2,0},{3,1},{4,6},{5,7},{6,4},{7,5},{8,10},{9,11},{10,... | collective-permute-start | bytes 1769480 | tf_op jit(solution)/shard_map/ppermute | solution.py:252
  89.1 23.0 %collective-permute-start.22 = (bf16[8,48,768]{2,1,0:T(8,128)(2,1)}, bf16[8,48,768]{2,1,0:T(8,128)(2,1)}, u32[]{:S(2)}, u32[]{:S(2)}) collective-permute-start(bf16[8,48,768]{2,1,0:T(8,128)(2,1)} %constant_dynamic-update-slice_fusion.25.w0), channel_id=1, source_target_pairs={{0,16},{1,17},{2,18},{3,19},{4,20},{5,21},{6,22},{7,23},{8,24},{9,... | collective-permute-start | bytes 1769480 | tf_op jit(solution)/shard_map/ppermute | solution.py:252
  90.4 21.1 %collective-permute-start.29 = (bf16[4,48,768]{2,1,0:T(8,128)(2,1)S(1)}, bf16[4,48,768]{2,1,0:T(8,128)(2,1)}, u32[]{:S(2)}, u32[]{:S(2)}) collective-permute-start(bf16[4,48,768]{2,1,0:T(8,128)(2,1)S(1)} %pad_maximum_fusion.6), channel_id=1, source_target_pairs={{0,2},{1,3},{2,0},{3,1},{4,6},{5,7},{6,4},{7,5},{8,10},{9,11},{10,... | collective-permute-start | bytes 884744 | tf_op jit(solution)/shard_map/ppermute | solution.py:252
  92.7 19.3 %collective-permute-start.30 = (bf16[4,48,768]{2,1,0:T(8,128)(2,1)}, bf16[4,48,768]{2,1,0:T(8,128)(2,1)}, u32[]{:S(2)}, u32[]{:S(2)}) collective-permute-start(bf16[4,48,768]{2,1,0:T(8,128)(2,1)} %pad_maximum_fusion.7), channel_id=1, source_target_pairs={{0,16},{1,17},{2,18},{3,19},{4,20},{5,21},{6,22},{7,23},{8,24},{9,... | collective-permute-start | bytes 884744 | tf_op jit(solution)/shard_map/ppermute | solution.py:252
  111.3 6.0 %collective-permute-start.14 = (bf16[768,384]{1,0:T(8,128)(2,1)}, bf16[768,384]{1,0:T(8,128)(2,1)S(1)}, u32[]{:S(2)}, u32[]{:S(2)}) collective-permute-start(bf16[768,384]{1,0:T(8,128)(2,1)} %get-tuple-element.113.wout_mine), channel_id=1, source_target_pairs={{0,1},{1,0},{2,3},{3,2},{4,5},{5,4},{6,7},{7,6},{8,9},{9,8},{10,11... | collective-permute-start | bytes 1769480 | tf_op jit(solution)/shard_map/ppermute | solution.py:252
  111.5 5.8 %collective-permute-start.15 = (bf16[2,64,768]{2,1,0:T(8,128)(2,1)S(1)}, bf16[2,64,768]{2,1,0:T(8,128)(2,1)S(1)}, u32[]{:S(2)}, u32[]{:S(2)}) collective-permute-start(bf16[2,64,768]{2,1,0:T(8,128)(2,1)S(1)} %pad.18.cot_mine), channel_id=1, source_target_pairs={{0,1},{1,0},{2,3},{3,2},{4,5},{5,4},{6,7},{7,6},{8,9},{9,8},{10,11... | collective-permute-start | bytes 589832 | tf_op jit(solution)/shard_map/ppermute | solution.py:252
  112.0 5.3 %collective-permute-start.13 = (bf16[256,384]{1,0:T(8,128)(2,1)}, bf16[256,384]{1,0:T(8,128)(2,1)S(1)}, u32[]{:S(2)}, u32[]{:S(2)}) collective-permute-start(bf16[256,384]{1,0:T(8,128)(2,1)} %get-tuple-element.111.attn_mine), channel_id=1, source_target_pairs={{0,1},{1,0},{2,3},{3,2},{4,5},{5,4},{6,7},{7,6},{8,9},{9,8},{10,11... | collective-permute-start | bytes 589832 | tf_op jit(solution)/shard_map/ppermute | solution.py:252
  114.1 16.2 %collective-permute-start.32 = (bf16[8,48,768]{2,1,0:T(8,128)(2,1)S(1)}, bf16[8,48,768]{2,1,0:T(8,128)(2,1)S(1)}, u32[]{:S(2)}, u32[]{:S(2)}) collective-permute-start(bf16[8,48,768]{2,1,0:T(8,128)(2,1)S(1)} %constant_dynamic-update-slice_fusion.31.w2), channel_id=1, source_target_pairs={{0,2},{1,3},{2,0},{3,1},{4,6},{5,7},{6,4},{7,5},{8,10},{9,11},{10,... | collective-permute-start | bytes 1769480 | tf_op jit(solution)/shard_map/ppermute | solution.py:252
  116.0 16.0 %collective-permute-start.31 = (bf16[8,48,768]{2,1,0:T(8,128)(2,1)S(1)}, bf16[8,48,768]{2,1,0:T(8,128)(2,1)}, u32[]{:S(2)}, u32[]{:S(2)}) collective-permute-start(bf16[8,48,768]{2,1,0:T(8,128)(2,1)S(1)} %constant_dynamic-update-slice_fusion.29.w0), channel_id=1, source_target_pairs={{0,16},{1,17},{2,18},{3,19},{4,20},{5,21},{6,22},{7,23},{8,24},{9,... | collective-permute-start | bytes 1769480 | tf_op jit(solution)/shard_map/ppermute | solution.py:252
  128.2 15.9 %collective-permute-start.24 = (bf16[8,48,768]{2,1,0:T(8,128)(2,1)}, bf16[8,48,768]{2,1,0:T(8,128)(2,1)S(1)}, u32[]{:S(2)}, u32[]{:S(2)}) collective-permute-start(bf16[8,48,768]{2,1,0:T(8,128)(2,1)} %get-tuple-element.125), channel_id=1, source_target_pairs={{0,16},{1,17},{2,18},{3,19},{4,20},{5,21},{6,22},{7,23},{8,24},{9,... | collective-permute-start | bytes 1769480 | tf_op jit(solution)/shard_map/ppermute | solution.py:252
  129.1 15.0 %collective-permute-start.25 = (bf16[8,48,768]{2,1,0:T(8,128)(2,1)}, bf16[8,48,768]{2,1,0:T(8,128)(2,1)S(1)}, u32[]{:S(2)}, u32[]{:S(2)}) collective-permute-start(bf16[8,48,768]{2,1,0:T(8,128)(2,1)} %get-tuple-element.127), channel_id=1, source_target_pairs={{0,2},{1,3},{2,0},{3,1},{4,6},{5,7},{6,4},{7,5},{8,10},{9,11},{10,... | collective-permute-start | bytes 1769480 | tf_op jit(solution)/shard_map/ppermute | solution.py:252
  144.1 27.3 %collective-permute-start.36 = (bf16[8,48,768]{2,1,0:T(8,128)(2,1)}, bf16[8,48,768]{2,1,0:T(8,128)(2,1)S(1)}, u32[]{:S(2)}, u32[]{:S(2)}) collective-permute-start(bf16[8,48,768]{2,1,0:T(8,128)(2,1)} %get-tuple-element.162), channel_id=1, source_target_pairs={{0,16},{1,17},{2,18},{3,19},{4,20},{5,21},{6,22},{7,23},{8,24},{9,... | collective-permute-start | bytes 1769480 | tf_op jit(solution)/shard_map/ppermute | solution.py:252
  145.4 26.0 %collective-permute-start.37 = (bf16[8,48,768]{2,1,0:T(8,128)(2,1)}, bf16[8,48,768]{2,1,0:T(8,128)(2,1)S(1)}, u32[]{:S(2)}, u32[]{:S(2)}) collective-permute-start(bf16[8,48,768]{2,1,0:T(8,128)(2,1)} %get-tuple-element.164), channel_id=1, source_target_pairs={{0,2},{1,3},{2,0},{3,1},{4,6},{5,7},{6,4},{7,5},{8,10},{9,11},{10,... | collective-permute-start | bytes 1769480 | tf_op jit(solution)/shard_map/ppermute | solution.py:252
  146.9 4.5 %collective-permute-start.33 = (bf16[512,768]{1,0:T(8,128)(2,1)}, bf16[512,768]{1,0:T(8,128)(2,1)S(1)}, u32[]{:S(2)}, u32[]{:S(2)}) collective-permute-start(bf16[512,768]{1,0:T(8,128)(2,1)} %get-tuple-element.146.part_mine), channel_id=1, source_target_pairs={{0,1},{1,0},{2,3},{3,2},{4,5},{5,4},{6,7},{7,6},{8,9},{9,8},{10,11... | collective-permute-start | bytes 2359304 | tf_op jit(solution)/shard_map/ppermute | solution.py:252
  147.9 23.5 %collective-permute-start.35 = (bf16[4,48,768]{2,1,0:T(8,128)(2,1)S(1)}, bf16[4,48,768]{2,1,0:T(8,128)(2,1)}, u32[]{:S(2)}, u32[]{:S(2)}) collective-permute-start(bf16[4,48,768]{2,1,0:T(8,128)(2,1)S(1)} %add_convert_fusion.10), channel_id=1, source_target_pairs={{0,16},{1,17},{2,18},{3,19},{4,20},{5,21},{6,22},{7,23},{8,24},{9,... | collective-permute-start | bytes 884744 | tf_op jit(solution)/shard_map/ppermute | solution.py:252
  150.5 20.9 %collective-permute-start.34 = (bf16[4,48,768]{2,1,0:T(8,128)(2,1)}, bf16[4,48,768]{2,1,0:T(8,128)(2,1)}, u32[]{:S(2)}, u32[]{:S(2)}) collective-permute-start(bf16[4,48,768]{2,1,0:T(8,128)(2,1)} %add_convert_fusion.11), channel_id=1, source_target_pairs={{0,2},{1,3},{2,0},{3,1},{4,6},{5,7},{6,4},{7,5},{8,10},{9,11},{10,... | collective-permute-start | bytes 884744 | tf_op jit(solution)/shard_map/ppermute | solution.py:252
  152.3 19.3 %slice-start.2 = ((bf16[8,48,768]{2,1,0:T(8,128)(2,1)}), bf16[4,48,768]{2,1,0:T(8,128)(2,1)S(1)}, s32[]{:S(2)}) async-start(bf16[8,48,768]{2,1,0:T(8,128)(2,1)} %copy-done.11), calls=%async_computation.2 | async-start | bytes 589824 | tf_op jit(solution)/shard_map/slice | solution.py:341
  152.3 20.8 %slice-start.3 = ((bf16[8,48,768]{2,1,0:T(8,128)(2,1)}), bf16[4,48,768]{2,1,0:T(8,128)(2,1)S(1)}, s32[]{:S(2)}) async-start(bf16[8,48,768]{2,1,0:T(8,128)(2,1)} %copy-done.12), calls=%async_computation.3 | async-start | bytes 589824 | tf_op jit(solution)/shard_map/slice | solution.py:342
  171.5 23.3 %collective-permute-start.38 = (bf16[8,2,64,768]{3,2,1,0:T(8,128)(2,1)}, bf16[8,2,64,768]{3,2,1,0:T(8,128)(2,1)S(1)}, u32[]{:S(2)}, u32[]{:S(2)}) collective-permute-start(bf16[8,2,64,768]{3,2,1,0:T(8,128)(2,1)} %get-tuple-element.166), channel_id=1, source_target_pairs={{0,1},{1,0},{2,3},{3,2},{4,5},{5,4},{6,7},{7,6},{8,9},{9,8},{10,11... | collective-permute-start | bytes 4718600 | tf_op jit(solution)/shard_map/ppermute | solution.py:252
  174.9 7.7 %collective-permute-start.41 = (bf16[48,1536]{1,0:T(8,128)(2,1)S(1)}, bf16[48,1536]{1,0:T(8,128)(2,1)S(1)}, u32[]{:S(2)}, u32[]{:S(2)}) collective-permute-start(bf16[48,1536]{1,0:T(8,128)(2,1)S(1)} %get-tuple-element.253), channel_id=1, source_target_pairs={{0,12},{1,13},{2,14},{3,15},{4,8},{5,9},{6,10},{7,11},{8,4},{9,5},... | collective-permute-start | bytes 442376 | tf_op jit(solution)/shard_map/ppermute | solution.py:252
  178.1 16.6 %collective-permute-start.43 = (bf16[4,48,768]{2,1,0:T(8,128)(2,1)}, bf16[4,48,768]{2,1,0:T(8,128)(2,1)}, u32[]{:S(2)}, u32[]{:S(2)}) collective-permute-start(bf16[4,48,768]{2,1,0:T(8,128)(2,1)} %add_convert_fusion.6), channel_id=1, source_target_pairs={{0,16},{1,17},{2,18},{3,19},{4,20},{5,21},{6,22},{7,23},{8,24},{9,... | collective-permute-start | bytes 884744 | tf_op jit(solution)/shard_map/ppermute | solution.py:252
  179.5 15.3 %collective-permute-start.42 = (bf16[4,48,768]{2,1,0:T(8,128)(2,1)}, bf16[4,48,768]{2,1,0:T(8,128)(2,1)}, u32[]{:S(2)}, u32[]{:S(2)}) collective-permute-start(bf16[4,48,768]{2,1,0:T(8,128)(2,1)} %add_convert_fusion.7), channel_id=1, source_target_pairs={{0,2},{1,3},{2,0},{3,1},{4,6},{5,7},{6,4},{7,5},{8,10},{9,11},{10,... | collective-permute-start | bytes 884744 | tf_op jit(solution)/shard_map/ppermute | solution.py:252
  181.0 13.8 %collective-permute-start.39 = (bf16[48,1536]{1,0:T(8,128)(2,1)}, bf16[48,1536]{1,0:T(8,128)(2,1)}, u32[]{:S(2)}, u32[]{:S(2)}) collective-permute-start(bf16[48,1536]{1,0:T(8,128)(2,1)} %get-tuple-element.255), channel_id=1, source_target_pairs={{0,4},{1,5},{2,6},{3,7},{4,0},{5,1},{6,2},{7,3},{8,12},{9,13},{10,... | collective-permute-start | bytes 442376 | tf_op jit(solution)/shard_map/ppermute | solution.py:252
  182.6 12.1 %collective-permute-start.40 = (bf16[48,1536]{1,0:T(8,128)(2,1)S(1)}, bf16[48,1536]{1,0:T(8,128)(2,1)}, u32[]{:S(2)}, u32[]{:S(2)}) collective-permute-start(bf16[48,1536]{1,0:T(8,128)(2,1)S(1)} %get-tuple-element.256), channel_id=1, source_target_pairs={{0,8},{1,9},{2,10},{3,11},{4,12},{5,13},{6,14},{7,15},{8,0},{9,1},... | collective-permute-start | bytes 442376 | tf_op jit(solution)/shard_map/ppermute | solution.py:252
  195.0 25.0 %collective-permute-start.47 = (bf16[4,2,64,768]{3,2,1,0:T(8,128)(2,1)S(1)}, bf16[4,2,64,768]{3,2,1,0:T(8,128)(2,1)S(1)}, u32[]{:S(2)}, u32[]{:S(2)}) collective-permute-start(bf16[4,2,64,768]{3,2,1,0:T(8,128)(2,1)S(1)} %add_convert_fusion.1), channel_id=1, source_target_pairs={{0,2},{1,3},{2,0},{3,1},{4,6},{5,7},{6,4},{7,5},{8,10},{9,11},{10,... | collective-permute-start | bytes 2359304 | tf_op jit(solution)/shard_map/ppermute | solution.py:252
  195.9 24.2 %collective-permute-start.48 = (bf16[8,48,1152]{2,1,0:T(8,128)(2,1)S(1)}, bf16[8,48,1152]{2,1,0:T(8,128)(2,1)S(1)}, u32[]{:S(2)}, u32[]{:S(2)}) collective-permute-start(bf16[8,48,1152]{2,1,0:T(8,128)(2,1)S(1)} %copy-done.41), channel_id=1, source_target_pairs={{0,16},{1,17},{2,18},{3,19},{4,20},{5,21},{6,22},{7,23},{8,24},{9,... | collective-permute-start | bytes 2654216 | tf_op jit(solution)/shard_map/ppermute | solution.py:252
  198.6 8.7 %collective-permute-start.46 = (bf16[48,1536]{1,0:T(8,128)(2,1)S(1)}, bf16[48,1536]{1,0:T(8,128)(2,1)S(1)}, u32[]{:S(2)}, u32[]{:S(2)}) collective-permute-start(bf16[48,1536]{1,0:T(8,128)(2,1)S(1)} %get-tuple-element.249), channel_id=1, source_target_pairs={{0,12},{1,13},{2,14},{3,15},{4,8},{5,9},{6,10},{7,11},{8,4},{9,5},... | collective-permute-start | bytes 442376 | tf_op jit(solution)/shard_map/ppermute | solution.py:252
  199.8 7.5 %collective-permute-start.44 = (bf16[48,1536]{1,0:T(8,128)(2,1)S(1)}, bf16[48,1536]{1,0:T(8,128)(2,1)S(1)}, u32[]{:S(2)}, u32[]{:S(2)}) collective-permute-start(bf16[48,1536]{1,0:T(8,128)(2,1)S(1)} %get-tuple-element.251), channel_id=1, source_target_pairs={{0,4},{1,5},{2,6},{3,7},{4,0},{5,1},{6,2},{7,3},{8,12},{9,13},{10,... | collective-permute-start | bytes 442376 | tf_op jit(solution)/shard_map/ppermute | solution.py:252
  199.9 20.1 %collective-permute-start.49 = (bf16[8,48,384]{2,1,0:T(8,128)(2,1)S(1)}, bf16[8,48,384]{2,1,0:T(8,128)(2,1)S(1)}, u32[]{:S(2)}, u32[]{:S(2)}) collective-permute-start(bf16[8,48,384]{2,1,0:T(8,128)(2,1)S(1)} %copy-done.42), channel_id=1, source_target_pairs={{0,2},{1,3},{2,0},{3,1},{4,6},{5,7},{6,4},{7,5},{8,10},{9,11},{10,... | collective-permute-start | bytes 884744 | tf_op jit(solution)/shard_map/ppermute | solution.py:252
  207.3 6.0 %collective-permute-start.45 = (bf16[48,1536]{1,0:T(8,128)(2,1)S(1)}, bf16[48,1536]{1,0:T(8,128)(2,1)S(1)}, u32[]{:S(2)}, u32[]{:S(2)}) collective-permute-start(bf16[48,1536]{1,0:T(8,128)(2,1)S(1)} %get-tuple-element.252), channel_id=1, source_target_pairs={{0,8},{1,9},{2,10},{3,11},{4,12},{5,13},{6,14},{7,15},{8,0},{9,1},... | collective-permute-start | bytes 442376 | tf_op jit(solution)/shard_map/ppermute | solution.py:252
  222.3 5.5 %collective-permute-start.54 = (bf16[4,48,384]{2,1,0:T(8,128)(2,1)}, bf16[4,48,384]{2,1,0:T(8,128)(2,1)}, u32[]{:S(2)}, u32[]{:S(2)}) collective-permute-start(bf16[4,48,384]{2,1,0:T(8,128)(2,1)} %add_convert_fusion.13), channel_id=1, source_target_pairs={{0,16},{1,17},{2,18},{3,19},{4,20},{5,21},{6,22},{7,23},{8,24},{9,... | collective-permute-start | bytes 442376 | tf_op jit(solution)/shard_map/ppermute | solution.py:252
  222.7 37.0 %collective-permute-start.52 = (bf16[2,64,768]{2,1,0:T(8,128)(2,1)}, bf16[2,64,768]{2,1,0:T(8,128)(2,1)}, u32[]{:S(2)}, u32[]{:S(2)}) collective-permute-start(bf16[2,64,768]{2,1,0:T(8,128)(2,1)} %get-tuple-element.242), channel_id=1, source_target_pairs={{8,4},{9,5},{10,6},{11,7},{12,0},{13,1},{14,2},{15,3},{24,20},{25,... | collective-permute-start | bytes 589832 | tf_op jit(solution)/shard_map/ppermute | solution.py:252
  224.0 35.7 %collective-permute-start.51 = (bf16[2,64,768]{2,1,0:T(8,128)(2,1)}, bf16[2,64,768]{2,1,0:T(8,128)(2,1)}, u32[]{:S(2)}, u32[]{:S(2)}) collective-permute-start(bf16[2,64,768]{2,1,0:T(8,128)(2,1)} %get-tuple-element.243), channel_id=1, source_target_pairs={{8,0},{9,1},{10,2},{11,3},{12,4},{13,5},{14,6},{15,7},{24,16},{25,... | collective-permute-start | bytes 589832 | tf_op jit(solution)/shard_map/ppermute | solution.py:252
  225.5 1.4 collective-permute-start.59
  225.7 12.7 %collective-permute-start.53 = (bf16[4,48,1152]{2,1,0:T(8,128)(2,1)S(1)}, bf16[4,48,1152]{2,1,0:T(8,128)(2,1)}, u32[]{:S(2)}, u32[]{:S(2)}) collective-permute-start(bf16[4,48,1152]{2,1,0:T(8,128)(2,1)S(1)} %add_convert_fusion.3), channel_id=1, source_target_pairs={{0,2},{1,3},{2,0},{3,1},{4,6},{5,7},{6,4},{7,5},{8,10},{9,11},{10,... | collective-permute-start | bytes 1327112 | tf_op jit(solution)/shard_map/ppermute | solution.py:252
  239.6 8.2 %collective-permute-start.55 = (bf16[48,1536]{1,0:T(8,128)(2,1)S(1)}, bf16[48,1536]{1,0:T(8,128)(2,1)S(1)}, u32[]{:S(2)}, u32[]{:S(2)}) collective-permute-start(bf16[48,1536]{1,0:T(8,128)(2,1)S(1)} %get-tuple-element.246), channel_id=1, source_target_pairs={{0,4},{1,5},{2,6},{3,7},{4,0},{5,1},{6,2},{7,3},{8,12},{9,13},{10,... | collective-permute-start | bytes 442376 | tf_op jit(solution)/shard_map/ppermute | solution.py:252
  239.7 13.7 %collective-permute-start.57 = (bf16[48,1536]{1,0:T(8,128)(2,1)S(1)}, bf16[48,1536]{1,0:T(8,128)(2,1)S(1)}, u32[]{:S(2)}, u32[]{:S(2)}) collective-permute-start(bf16[48,1536]{1,0:T(8,128)(2,1)S(1)} %get-tuple-element.247), channel_id=1, source_target_pairs={{0,12},{1,13},{2,14},{3,15},{4,8},{5,9},{6,10},{7,11},{8,4},{9,5},... | collective-permute-start | bytes 442376 | tf_op jit(solution)/shard_map/ppermute | solution.py:252
  245.5 13.5 %collective-permute-start.56 = (bf16[48,1536]{1,0:T(8,128)(2,1)S(1)}, bf16[48,1536]{1,0:T(8,128)(2,1)S(1)}, u32[]{:S(2)}, u32[]{:S(2)}) collective-permute-start(bf16[48,1536]{1,0:T(8,128)(2,1)S(1)} %get-tuple-element.248), channel_id=1, source_target_pairs={{0,8},{1,9},{2,10},{3,11},{4,12},{5,13},{6,14},{7,15},{8,0},{9,1},... | collective-permute-start | bytes 442376 | tf_op jit(solution)/shard_map/ppermute | solution.py:252
  247.8 11.9 %collective-permute-start.50 = (bf16[2,64,768]{2,1,0:T(8,128)(2,1)S(1)}, bf16[2,64,768]{2,1,0:T(8,128)(2,1)S(1)}, u32[]{:S(2)}, u32[]{:S(2)}) collective-permute-start(bf16[2,64,768]{2,1,0:T(8,128)(2,1)S(1)} %copy-done.34), channel_id=1, source_target_pairs={{4,0},{5,1},{6,2},{7,3},{12,8},{13,9},{14,10},{15,11},{20,16},{21,... | collective-permute-start | bytes 589832 | tf_op jit(solution)/shard_map/ppermute | solution.py:252
  259.1 3.9 %collective-permute-start.58 = (f32[24,1536]{1,0:T(8,128)S(1)}, f32[24,1536]{1,0:T(8,128)S(1)}, u32[]{:S(2)}, u32[]{:S(2)}) collective-permute-start(f32[24,1536]{1,0:T(8,128)S(1)} %slice_select_fusion), channel_id=1, source_target_pairs={{0,1},{1,0},{2,3},{3,2},{4,5},{5,4},{6,7},{7,6},{8,9},{9,8},{10,11... | collective-permute-start | bytes 442376 | tf_op jit(solution)/shard_map/ppermute | solution.py:252
  (45 other events, 295.6 us)
